TPU v7x, 32 devices: a whole 2x2x4 slice. The times are simulated.
32 devices in a mesh: pipe: 4 (over y, x), expert: 8 (over z, core).
Axes of the slice: x: 2, y: 2, z: 4, core: 2. Of those that a mesh axis runs over, the one named last changes fastest.
Arguments:
- tokens_in: bfloat16 [2, 640, 2048], P(None, 'expert'), may hold values from -6 to 6
- out_grad: bfloat16 [2, 640, 2048], P(None, 'expert'), may hold values from -6 to 6
- routes: int32 [4, 2, 640, 1], P(None, None, 'expert'), may hold values from 0 to 7; in each aligned block of 80 rows (0 to 79, 80 to 159, ..., all dimensions but the last counted through in order) at most 15 rows name the same one
- router: bfloat16 [4, 2048, 8], P('pipe'), may hold values from -0.125 to 0.125
- norm_gain: bfloat16 [4, 2048], P('pipe'), may hold values from 0.5 to 1.5
- w_in: bfloat16 [4, 8, 2048, 1024], P('pipe', 'expert'), may hold values from -0.125 to 0.125
- w_out: bfloat16 [4, 8, 512, 2048], P('pipe', 'expert'), may hold values from -0.25 to 0.25
Outputs:
- grad_in: bfloat16 [4, 8, 2048, 1024], P('pipe', 'expert')
- grad_out: bfloat16 [4, 8, 512, 2048], P('pipe', 'expert')
Inputs may be any that keep to these rules, and one draw needn't show every extreme that they name: `routes`: in each aligned block of 80 rows (one device's tokens of one layer and microbatch) no expert is named by more than 15 tokens; a token's 1 ids differ.
All inputs are finite; a program needn't handle non-finite values.
Results may differ from a plain program's by a relative error of at most 0.029.
Values may be sent and summed in bfloat16 or wider, within the bound.
No kernel may reach another device: no remote copies, remote signals or barrier semaphores. Data moves between devices by JAX's collectives and lax.ppermute only.
A program may use at most 128 MiB of HBM per device.

v0:
```python
import functools

import jax
import jax.numpy as jnp
from jax import lax
from jax.experimental import pallas as pl
from jax.experimental.pallas import tpu as pltpu
from jax.sharding import PartitionSpec as P


epsilon = 1e-06


f32, bf16 = jnp.float32, jnp.bfloat16
VMEM = pl.BlockSpec(memory_space=pltpu.VMEM)
SMEM = pl.BlockSpec(memory_space=pltpu.SMEM)
ANY = pl.BlockSpec(memory_space=pl.ANY)
LAST = (((1,), (1,)), ((), ()))
FIRST = (((0,), (0,)), ((), ()))
LANES = 128
WIDEST = 8


def unpacked(ref, width):
    value = ref[...]
    size = value.shape[0]
    if value.shape[1] == width:
        return value
    real = size - 2
    spare = value[real:].astype(f32)
    blocks = [spare[:, i * LANES : (i + 1) * LANES] for i in range(real // 2)]
    tail = jnp.concatenate(blocks + [jnp.zeros((2, LANES), f32)], axis=0).astype(bf16)
    held = lax.broadcasted_iota(jnp.int32, value.shape, 0) < real
    return jnp.concatenate([jnp.where(held, value, jnp.zeros_like(value)), tail], axis=1)


def packed(value, short):
    if value.shape[1] == short:
        return value
    real = value.shape[0] - 2
    tail = value[:, short:].astype(f32)
    spare = jnp.concatenate([tail[2 * i : 2 * i + 2] for i in range(real // 2)], axis=1)
    last = value[-16:, :short].astype(f32)
    last = jnp.concatenate([last[:14], spare], axis=0).astype(bf16)
    return jnp.concatenate([value[:-16, :short], last], axis=0)


def joined_rows(refs, width):
    parts = [unpacked(ref, width) for ref in refs]
    return parts[0] if len(parts) == 1 else jnp.concatenate(parts, axis=0)


def split_rows(refs, value, keep=None, others=None):
    size, short = refs[0].shape
    for k, ref in enumerate(refs):
        block = packed(value[k * size : (k + 1) * size], short)
        if others is not None:
            block = jnp.where(keep, block, others[k][...])
        ref[...] = block


def normalize(hidden, gain):
    values = hidden.astype(f32)
    inverse = lax.rsqrt(jnp.mean(values * values, axis=-1, keepdims=True) + epsilon)
    scaled = values * inverse
    return (scaled * gain).astype(bf16), scaled, inverse


def gate_of(normed, column):
    return jax.nn.sigmoid(jnp.sum(normed.astype(f32) * column, axis=-1, keepdims=True))


def forward_kernel(count, chained, gain_ref, column_ref, in_ref, out_ref, *refs):
    arrived, refs = refs[:count], refs[count + chained :]
    sent, refs = refs[:count], refs[count:]
    hidden_ref, joined_ref, produced_ref = refs
    inner = out_ref.shape[0]
    hidden = joined_rows(arrived, in_ref.shape[0])
    normed, _, _ = normalize(hidden, gain_ref[...].astype(f32))
    share = gate_of(normed, column_ref[...]).astype(bf16).astype(f32)
    joined = jnp.dot(normed, in_ref[...], preferred_element_type=f32)
    gate_part = joined[:, :inner]
    activated = (gate_part * jax.nn.sigmoid(gate_part) * joined[:, inner:]).astype(bf16)
    produced = jnp.dot(activated, out_ref[...], preferred_element_type=f32).astype(bf16)
    output = (hidden.astype(f32) + share * produced.astype(f32)).astype(bf16)
    split_rows(sent, output)
    hidden_ref[...] = hidden
    joined_ref[...] = joined
    produced_ref[...] = produced


def backward_kernel(plan, place_ref, gain_ref, column_ref, in_ref, out_ref, *refs):
    count, layers, micros, sets, enters, first, chained, aliased, passes = plan
    last = layers - 1
    layer, step = place_ref[0], place_ref[2]
    refs = list(refs)
    take = lambda number: [refs.pop(0) for _ in range(number)]
    arrived = take(count)
    entered = take(count) if enters else None
    ahead = take(count) if first else None
    saved = [take(3) for _ in range(sets)]
    take(chained)
    if aliased:
        take(4)
    sent = take(count) if passes else None
    kept = take(4)
    stage = take(4)
    sems = refs.pop(0)
    width = out_ref.shape[0]
    upstream = joined_rows(arrived, width)
    if entered is not None:
        upstream = jnp.where(layer == last, joined_rows(entered, width), upstream)
    upstream_f = upstream.astype(f32)
    micro = step - (2 * last - layer)

    def pick(index):
        value = saved[0][index][...]
        for group in saved[1:]:
            value = jnp.where(micro == 1, group[index][...], value)
        return value

    hidden, joined, produced = pick(0), pick(1), pick(2)
    slot = jnp.where((micro >= 0) & (micro < micros), micro, micros)
    copies = [
        pltpu.make_async_copy(stage[i], kept[i].at[slot], sems.at[i]) for i in range(4)
    ]
    inner = out_ref.shape[1]
    gain, column = gain_ref[...].astype(f32), column_ref[...]
    normed, scaled, inverse = normalize(hidden, gain)
    gate = gate_of(normed, column)
    gate_part, up_part = joined[:, :inner], joined[:, inner:]
    sigmoid_gate = jax.nn.sigmoid(gate_part)
    silu_gate = gate_part * sigmoid_gate
    scaled_grad = (gate.astype(bf16).astype(f32) * upstream_f).astype(bf16)
    stage[0][...] = normed
    stage[2][...] = (silu_gate * up_part).astype(bf16)
    stage[3][...] = scaled_grad
    for i in (0, 2, 3):
        copies[i].start()
    act_grad = jnp.dot(scaled_grad, out_ref[...], preferred_element_type=f32)
    gate_grad = act_grad * up_part * sigmoid_gate * (1.0 + gate_part * (1.0 - sigmoid_gate))
    up_grad = act_grad * silu_gate
    joined_grad = jnp.concatenate([gate_grad, up_grad], axis=-1).astype(bf16)
    stage[1][...] = joined_grad
    copies[1].start()
    if passes:
        rows_grad = jnp.dot(joined_grad, in_ref[...], preferred_element_type=f32).astype(bf16)
        share_grad = jnp.sum(produced.astype(f32) * upstream_f, axis=-1, keepdims=True)
        logit_grad = share_grad.astype(bf16).astype(f32) * gate * (1.0 - gate)
        gained = (rows_grad.astype(f32) + logit_grad * column) * gain
        centred = gained - scaled * jnp.mean(gained * scaled, axis=-1, keepdims=True)
        passed = (upstream_f + inverse * centred).astype(bf16)
        split_rows(sent, passed, layer == last, ahead)
    for copy in copies:
        copy.wait()


def resort_kernel(plan, place_ref, order_ref, *refs):
    arrivals, count, width, entry, last = plan
    arrived = refs[:arrivals]
    rest = refs[arrivals:]
    sent = rest[-count:]
    value = jnp.dot(
        order_ref[0], joined_rows(arrived, width), preferred_element_type=f32
    ).astype(bf16)
    if entry:
        layer = place_ref[0]
        value = jnp.where((layer == 0) | (layer == last), rest[0][...], value)
    split_rows(sent, value)


def prepare_kernel(plan, place_ref, *refs):
    homes, layers, micros, ranks, room, size, count = plan
    routes, entering = refs[:homes], refs[homes : 2 * homes]
    sent = refs[2 * homes : 2 * homes + count]
    start_ref, order_ref = refs[2 * homes + count :]
    layer, rank = place_ref[0], place_ref[1]
    tokens = routes[0].shape[1]
    rows = size * count
    near = [jnp.maximum(layer - 1, 0), layer, jnp.minimum(layer + 1, layers - 1)]
    ids = [
        [[routes[j][pl.ds(at * micros + m, 1), :] for m in range(micros)] for at in near]
        for j in range(homes)
    ]
    experts = lax.broadcasted_iota(jnp.int32, (ranks, tokens), 0)
    before = (
        lax.broadcasted_iota(jnp.int32, (tokens, tokens), 0)
        < lax.broadcasted_iota(jnp.int32, (tokens, tokens), 1)
    ).astype(f32).astype(bf16)
    flat = [row for home in ids for at in home for row in at]
    marks = jnp.concatenate([(experts == row).astype(f32) for row in flat], axis=0)
    earlier = marks * jnp.dot(marks.astype(bf16), before, preferred_element_type=f32)
    within = [
        jnp.sum(earlier[i * ranks : (i + 1) * ranks], axis=0, keepdims=True).astype(jnp.int32)
        for i in range(len(flat))
    ]

    def one_hot(size, index):
        slots = lax.broadcasted_iota(jnp.int32, (size, tokens), 0)
        return (slots == index).astype(f32).astype(bf16)

    def places(j, at, m):
        row, depth = ids[j][at][m], within[(j * 3 + at) * micros + m]
        if homes == 1:
            index = row * room + depth
            return index, index
        offset = row ^ rank
        far, other = offset >> 1, offset & 1
        target = jnp.where(other == 0, far * size + j * room + depth, -1)
        side = other if j == 0 else 1 - other
        return target, other * rows + far * size + side * room + depth

    for m in range(micros):
        here = [one_hot(rows, places(j, 1, m)[0]) for j in range(homes)]
        for which, at in enumerate((0, 2)):
            total = 0.0
            for j in range(homes):
                there = one_hot(homes * rows, places(j, at, m)[1])
                total += lax.dot_general(here[j], there, LAST, preferred_element_type=f32)
            order_ref[which * micros + m] = total.astype(bf16)
        start = 0.0
        for j in range(homes):
            start += jnp.dot(here[j], entering[j][m], preferred_element_type=f32)
        if m == 0:
            split_rows(sent, start.astype(bf16))
        else:
            start_ref[m - 1] = start.astype(bf16)


def transpose_kernel(in_ref, out_ref, in_turned, out_turned):
    in_turned[...] = in_ref[...].T
    out_turned[...] = out_ref[...].T


def grads_kernel(parts, *refs):
    in_ref, out_ref = refs[4 * parts :]

    def gathered(which):
        groups = [refs[4 * part + which] for part in range(parts)]
        return jnp.concatenate([g[m] for g in groups for m in range(g.shape[0])], axis=0)

    in_ref[...] = lax.dot_general(
        gathered(0), gathered(1), FIRST, preferred_element_type=f32
    ).astype(bf16)
    out_ref[...] = lax.dot_general(
        gathered(2), gathered(3), FIRST, preferred_element_type=f32
    ).astype(bf16)


def shards(tokens_in, out_grad, routes, router, norm_gain, w_in, w_out):
    layers = lax.axis_size("pipe")
    ranks = lax.axis_size("expert")
    layer = lax.axis_index("pipe")
    rank = lax.axis_index("expert")
    micros, tokens, width = tokens_in.shape
    assert routes.shape[3] == 1 and router.shape[2] == ranks
    assert micros == 2 and layers > 2 and layers % 2 == 0
    capacity = max(2, tokens * 3 // (2 * ranks))
    paired = ranks <= WIDEST and ranks & (ranks - 1) == 0 and capacity >= 8
    count = ranks // 2 if paired else 1
    homes = 2 if paired else 1
    if paired:
        room = capacity
        size = -(-2 * room // 16) * 16
    else:
        room = -(-capacity // 4) * 4
        size = ranks * room
    rows = size * count
    tight = paired and size == 2 * room + 2 and width == LANES * (room + 1)
    short = width - LANES if tight else width
    parts = [[0, 3], [1, 2]] if count == 4 else [list(range(count))]
    last = layers - 1
    steps = 2 * last + micros
    own_in, own_out, gain_row = w_in[0, 0], w_out[0, 0], norm_gain
    double, inner = own_in.shape[1], own_out.shape[0]
    column = (
        lax.dynamic_index_in_dim(router[0], rank, 1, keepdims=False).astype(f32).reshape(1, width)
    )
    places = [
        jnp.stack([layer, rank, jnp.int32(step)]).astype(jnp.int32) for step in range(steps)
    ]
    piece = jax.ShapeDtypeStruct((size, short), bf16)
    params = pltpu.CompilerParams(vmem_limit_bytes=16 << 20)

    def permuted(block, offset, jump):
        route = []
        for p in range(layers):
            q = p if jump is None else jump(p)
            route += [(p * ranks + i, q * ranks + (i ^ offset)) for i in range(ranks)]
        return lax.ppermute(block, ("pipe", "expert"), route)

    def spread(pieces):
        return lax.all_to_all(
            pieces[0].reshape(ranks, room, width), "expert", split_axis=0, concat_axis=0, tiled=True
        ).reshape(rows, width)

    def to_experts(pieces):
        if not paired:
            return [spread(pieces)]
        arrived = [pieces[0]] + [None] * (count - 1)
        for k in sorted(range(1, count), key=lambda k: (k % 2, -k)):
            arrived[k] = permuted(pieces[k], 2 * k, None)
        return arrived

    def to_homes(pieces, jump):
        if not paired:
            return [lax.ppermute(spread(pieces), "pipe", [(p, jump(p)) for p in range(layers)])]
        arrived, swapped = [None] * count, [None] * count
        for part in parts:
            for k in reversed(part):
                arrived[k] = permuted(pieces[k], 2 * k, jump)
                swapped[k] = permuted(arrived[k], 1, None)
        return arrived + swapped

    entering = jnp.where(layer == 0, tokens_in, out_grad)
    ids = routes.reshape(layers * micros, tokens)
    both_ids, both_entering = [ids], [entering]
    if paired:
        both_ids.append(permuted(ids, 1, None))
        both_entering.append(permuted(entering, 1, None))
    *pieces, start, order = pl.pallas_call(
        functools.partial(prepare_kernel, (homes, layers, micros, ranks, room, size, count)),
        out_shape=[piece] * count
        + [
            jax.ShapeDtypeStruct((micros - 1, rows, width), bf16),
            jax.ShapeDtypeStruct((2 * micros, rows, homes * rows), bf16),
        ],
        in_specs=[SMEM] + [VMEM] * (2 * homes),
        out_specs=[VMEM] * (count + 2),
        compiler_params=params,
        name="prepare",
    )(places[0], *both_ids, *both_entering)

    def resort(step, arrived):
        def which(ref):
            forward_micro = ref[2] - ref[0]
            backward_micro = jnp.clip(forward_micro - 2 * (last - ref[0]), 0, micros - 1)
            is_forward = (forward_micro >= 0) & (forward_micro < micros)
            return jnp.where(is_forward, forward_micro, micros + backward_micro)

        entry = step < micros
        whole = lambda shape: pl.BlockSpec(shape, lambda i, ref: (0,) * len(shape))
        ins = list(arrived) + ([start[step - 1]] if entry else [])
        return pl.pallas_call(
            functools.partial(resort_kernel, (len(arrived), count, width, entry, last)),
            out_shape=[piece] * count,
            grid_spec=pltpu.PrefetchScalarGridSpec(
                num_scalar_prefetch=1,
                grid=(1,),
                in_specs=[
                    pl.BlockSpec((1, rows, homes * rows), lambda i, ref: (which(ref), 0, 0))
                ]
                + [whole(value.shape) for value in ins],
                out_specs=[whole((size, short))] * count,
            ),
            compiler_params=params,
            name="resort",
        )(places[step], order, *ins)

    def forward(arrived, earlier):
        many = len(arrived)
        out = pl.pallas_call(
            functools.partial(forward_kernel, many, len(earlier)),
            out_shape=[piece] * many
            + [
                jax.ShapeDtypeStruct((many * size, width), bf16),
                jax.ShapeDtypeStruct((many * size, double), f32),
                jax.ShapeDtypeStruct((many * size, width), bf16),
            ],
            in_specs=[VMEM] * (4 + many) + [ANY] * len(earlier),
            out_specs=[VMEM] * (many + 3),
            compiler_params=params,
            name="forward",
        )(gain_row, column, own_in, own_out, *arrived, *earlier)
        return out[:many], out[many:]

    kept_sizes = (width, double, inner, width)
    bands = 8
    turned_in, turned_out = pl.pallas_call(
        transpose_kernel,
        grid=(bands,),
        out_shape=[
            jax.ShapeDtypeStruct((double, width), bf16),
            jax.ShapeDtypeStruct((width, inner), bf16),
        ],
        in_specs=[
            pl.BlockSpec((width // bands, double), lambda i: (i, 0)),
            pl.BlockSpec((inner, width // bands), lambda i: (0, i)),
        ],
        out_specs=[
            pl.BlockSpec((double, width // bands), lambda i: (0, i)),
            pl.BlockSpec((width // bands, inner), lambda i: (i, 0)),
        ],
        compiler_params=params,
        name="turn",
    )(own_in, own_out)

    def backward(step, arrived, entered, ahead, saved, kept, earlier):
        passes = step + 1 < steps
        many = len(arrived)
        sources = [
            saved[step - 2 * (last - p)]
            for p in range(layers)
            if 0 <= step - (2 * last - p) < micros
        ]
        plan = (
            many,
            layers,
            micros,
            len(sources),
            entered is not None,
            step == last,
            len(earlier),
            kept is not None,
            passes,
        )
        operands = [places[step], gain_row, column, turned_in, turned_out, *arrived]
        if entered is not None:
            operands += entered
        if step == last:
            operands += ahead
        for group in sources:
            operands += group
        specs = [SMEM] + [VMEM] * (len(operands) - 1) + [ANY] * len(earlier)
        operands += earlier
        sent = many if passes else 0
        aliases = {}
        if kept is not None:
            aliases = {len(operands) + i: sent + i for i in range(4)}
            operands += kept
            specs += [ANY] * 4
        held = [(many * size, length) for length in kept_sizes]
        out = pl.pallas_call(
            functools.partial(backward_kernel, plan),
            out_shape=[piece] * sent
            + [jax.ShapeDtypeStruct((micros + 1, *shape), bf16) for shape in held],
            in_specs=specs,
            out_specs=[VMEM] * sent + [ANY] * 4,
            scratch_shapes=[pltpu.VMEM(shape, bf16) for shape in held]
            + [pltpu.SemaphoreType.DMA((4,))],
            input_output_aliases=aliases,
            compiler_params=params,
            name="backward",
        )(*operands)
        return out[:sent], out[sent:]

    arrivals = []
    forwards = [[] for _ in parts]
    kept = [None for _ in parts]
    for step in range(steps):
        arrived = to_experts(pieces)
        arrivals.append(arrived)
        pieces, earlier = [None] * count, []
        for index, part in enumerate(parts):
            here = [arrived[k] for k in part]
            passed = None
            if step < last + micros:
                passed, saved = forward(here, earlier)
                forwards[index].append(saved)
            if step >= last:
                entered = None
                if step < last + micros:
                    entered = [arrivals[step - last][k] for k in part]
                passed, kept[index] = backward(
                    step, here, entered, passed, forwards[index], kept[index], earlier
                )
            for k, value in zip(part, passed):
                pieces[k] = value
            earlier = passed[:1]
        if step + 1 == steps:
            break
        if step < last:
            jump = lambda p: (p + 1) % layers
        elif step == last:
            jump = lambda p: p ^ 1
        else:
            jump = lambda p: (p - 1) % layers
        pieces = resort(step + 1, to_homes(pieces, jump))

    cuts = 4
    specs = []
    for part in parts:
        depth = len(part) * size
        column_block = lambda length: pl.BlockSpec((micros, depth, length), lambda i: (0, 0, i))
        whole_block = lambda length: pl.BlockSpec((micros, depth, length), lambda i: (0, 0, 0))
        specs += [
            column_block(width // cuts),
            whole_block(double),
            column_block(inner // cuts),
            whole_block(width),
        ]
    grad_in, grad_out = pl.pallas_call(
        functools.partial(grads_kernel, len(parts)),
        grid=(cuts,),
        out_shape=[
            jax.ShapeDtypeStruct((width, double), bf16),
            jax.ShapeDtypeStruct((inner, width), bf16),
        ],
        in_specs=specs,
        out_specs=[
            pl.BlockSpec((width // cuts, double), lambda i: (i, 0)),
            pl.BlockSpec((inner // cuts, width), lambda i: (i, 0)),
        ],
        compiler_params=params,
        name="grads",
    )(*[buffer for group in kept for buffer in group])
    return grad_in[None, None], grad_out[None, None]


def solution(mesh):
    placed = (
        P(None, "expert", None),
        P(None, "expert", None),
        P(None, None, "expert", None),
        P("pipe", None, None),
        P("pipe", None),
        P("pipe", "expert", None, None),
        P("pipe", "expert", None, None),
    )
    return jax.shard_map(
        shards,
        mesh=mesh,
        in_specs=placed,
        out_specs=(P("pipe", "expert", None, None), P("pipe", "expert", None, None)),
        check_vma=False,
    )
```

profile of v0, /device:TPU:0, one launch (start us, length us, event | category | flops | bytes accessed | tf_op | source)
XLA Modules:
  0.0 266.3 jit_solution(3157246762129112154)
XLA Ops:
  6.5 5.0 %collective-permute-start.2 = (bf16[32,1920]{1,0:T(8,128)(2,1)S(1)}, bf16[32,1920]{1,0:T(8,128)(2,1)S(1)}, u32[]{:S(2)}, u32[]{:S(2)}) collective-permute-start(bf16[32,1920]{1,0:T(8,128)(2,1)S(1)} %get-tuple-element.146), channel_id=1, source_target_pairs={{0,6},{1,7},{2,4},{3,5},{4,2},{5,3},{6,0},{7,1},{8,14},{9,15},{10,... | collective-permute-start | bytes 368648 | tf_op jit(solution)/shard_map/ppermute | solution.py:290
  12.9 2.8 %collective-permute-done.2.refs_1_.refs_3_ = bf16[32,1920]{1,0:T(8,128)(2,1)S(1)} collective-permute-done((bf16[32,1920]{1,0:T(8,128)(2,1)S(1)}, bf16[32,1920]{1,0:T(8,128)(2,1)S(1)}, u32[]{:S(2)}, u32[]{:S(2)}) %collective-permute-start.2) | collective-permute-done | bytes 122912 | tf_op jit(solution)/shard_map/ppermute | solution.py:290
  15.8 2.2 copy-done
  20.2 1.8 collective-permute-start.3
  23.7 3.8 %collective-permute-start.6 = (bf16[32,1920]{1,0:T(8,128)(2,1)S(1)}, bf16[32,1920]{1,0:T(8,128)(2,1)S(1)}, u32[]{:S(2)}, u32[]{:S(2)}) collective-permute-start(bf16[32,1920]{1,0:T(8,128)(2,1)S(1)} %get-tuple-element.150), channel_id=1, source_target_pairs={{0,10},{1,11},{2,8},{3,9},{4,14},{5,15},{6,12},{7,13},{8,18},{9,19... | collective-permute-start | bytes 368648 | tf_op jit(solution)/shard_map/ppermute | solution.py:290
  27.5 2.0 collective-permute-start.7
  31.5 7.8 %collective-permute-done.7.refs_2_ = bf16[32,1920]{1,0:T(8,128)(2,1)S(1)} collective-permute-done((bf16[32,1920]{1,0:T(8,128)(2,1)S(1)}, bf16[32,1920]{1,0:T(8,128)(2,1)S(1)}, u32[]{:S(2)}, u32[]{:S(2)}) %collective-permute-start.7) | collective-permute-done | bytes 122912 | tf_op jit(solution)/shard_map/ppermute | solution.py:290
  41.6 1.8 collective-permute-start.13
  44.2 1.9 collective-permute-start.16
  46.1 3.7 %collective-permute-done.13.refs_1_.refs_3_ = bf16[32,1920]{1,0:T(8,128)(2,1)S(1)} collective-permute-done((bf16[32,1920]{1,0:T(8,128)(2,1)S(1)}, bf16[32,1920]{1,0:T(8,128)(2,1)S(1)}, u32[]{:S(2)}, u32[]{:S(2)}) %collective-permute-start.13) | collective-permute-done | bytes 122912 | tf_op jit(solution)/shard_map/ppermute | solution.py:290
  52.1 4.0 %collective-permute-done.16.refs_1_.refs_3_ = bf16[32,1920]{1,0:T(8,128)(2,1)S(1)} collective-permute-done((bf16[32,1920]{1,0:T(8,128)(2,1)S(1)}, bf16[32,1920]{1,0:T(8,128)(2,1)S(1)}, u32[]{:S(2)}, u32[]{:S(2)}) %collective-permute-start.16) | collective-permute-done | bytes 122912 | tf_op jit(solution)/shard_map/ppermute | solution.py:290
  57.7 3.8 %collective-permute-start.18 = (bf16[32,1920]{1,0:T(8,128)(2,1)S(1)}, bf16[32,1920]{1,0:T(8,128)(2,1)S(1)}, u32[]{:S(2)}, u32[]{:S(2)}) collective-permute-start(bf16[32,1920]{1,0:T(8,128)(2,1)S(1)} %get-tuple-element.160), channel_id=1, source_target_pairs={{0,12},{1,13},{2,14},{3,15},{4,8},{5,9},{6,10},{7,11},{8,20},{9,21... | collective-permute-start | bytes 368648 | tf_op jit(solution)/shard_map/ppermute | solution.py:290
  62.9 2.7 %collective-permute-done.17.refs_1_ = bf16[32,1920]{1,0:T(8,128)(2,1)S(1)} collective-permute-done((bf16[32,1920]{1,0:T(8,128)(2,1)S(1)}, bf16[32,1920]{1,0:T(8,128)(2,1)S(1)}, u32[]{:S(2)}, u32[]{:S(2)}) %collective-permute-start.17) | collective-permute-done | bytes 122912 | tf_op jit(solution)/shard_map/ppermute | solution.py:290
  65.6 5.8 %collective-permute-done.18.refs_2_ = bf16[32,1920]{1,0:T(8,128)(2,1)S(1)} collective-permute-done((bf16[32,1920]{1,0:T(8,128)(2,1)S(1)}, bf16[32,1920]{1,0:T(8,128)(2,1)S(1)}, u32[]{:S(2)}, u32[]{:S(2)}) %collective-permute-start.18) | collective-permute-done | bytes 122912 | tf_op jit(solution)/shard_map/ppermute | solution.py:290
  73.8 1.8 collective-permute-start.24
  76.5 1.7 collective-permute-start.27
  78.2 3.6 %collective-permute-done.24.refs_1_ = bf16[32,1920]{1,0:T(8,128)(2,1)S(1)} collective-permute-done((bf16[32,1920]{1,0:T(8,128)(2,1)S(1)}, bf16[32,1920]{1,0:T(8,128)(2,1)S(1)}, u32[]{:S(2)}, u32[]{:S(2)}) %collective-permute-start.24) | collective-permute-done | bytes 122912 | tf_op jit(solution)/shard_map/ppermute | solution.py:290
  84.1 4.3 %collective-permute-done.27.refs_1_ = bf16[32,1920]{1,0:T(8,128)(2,1)S(1)} collective-permute-done((bf16[32,1920]{1,0:T(8,128)(2,1)S(1)}, bf16[32,1920]{1,0:T(8,128)(2,1)S(1)}, u32[]{:S(2)}, u32[]{:S(2)}) %collective-permute-start.27) | collective-permute-done | bytes 122912 | tf_op jit(solution)/shard_map/ppermute | solution.py:290
  90.0 3.8 %collective-permute-start.29 = (bf16[32,1920]{1,0:T(8,128)(2,1)S(1)}, bf16[32,1920]{1,0:T(8,128)(2,1)S(1)}, u32[]{:S(2)}, u32[]{:S(2)}) collective-permute-start(bf16[32,1920]{1,0:T(8,128)(2,1)S(1)} %get-tuple-element.168), channel_id=1, source_target_pairs={{0,12},{1,13},{2,14},{3,15},{4,8},{5,9},{6,10},{7,11},{8,20},{9,21... | collective-permute-start | bytes 368648 | tf_op jit(solution)/shard_map/ppermute | solution.py:290
  95.3 2.4 collective-permute-done.28.refs_1_
  97.8 5.9 %collective-permute-done.29.refs_2_ = bf16[32,1920]{1,0:T(8,128)(2,1)S(1)} collective-permute-done((bf16[32,1920]{1,0:T(8,128)(2,1)S(1)}, bf16[32,1920]{1,0:T(8,128)(2,1)S(1)}, u32[]{:S(2)}, u32[]{:S(2)}) %collective-permute-start.29) | collective-permute-done | bytes 122912 | tf_op jit(solution)/shard_map/ppermute | solution.py:290
  106.0 1.7 collective-permute-start.35
  108.8 1.7 collective-permute-start.38
  110.5 2.9 %turn.1 = (bf16[1024,2048]{1,0:T(8,128)(2,1)S(1)}, bf16[2048,512]{1,0:T(8,128)(2,1)S(1)}) custom-call(bf16[2048,1024]{1,0:T(8,128)(2,1)S(1)} %bitcast.17, bf16[512,2048]{1,0:T(8,128)(2,1)S(1)} %bitcast.28), custom_call_target="tpu_custom_call" | custom-call | tf_op jit(solution)/shard_map/turn/pallas_call | solution.py:379
  115.6 2.9 %backward.10 = (bf16[32,1920]{1,0:T(8,128)(2,1)S(1)}, bf16[32,1920]{1,0:T(8,128)(2,1)S(1)}, bf16[3,64,2048]{2,1,0:T(8,128)(2,1)S(1)}, bf16[3,64,1024]{2,1,0:T(8,...) custom-call(s32[3]{0:T(128)S(1)} %get-tuple-element.285.place_ref, ...), custom_call_target="tpu_custom_call" | custom-call | tf_op jit(solution)/shard_map/backward/pallas_call | solution.py:433
  119.1 1.7 collective-permute-done.38.refs_1_
  122.3 2.9 %backward.11 = (bf16[32,1920]{1,0:T(8,128)(2,1)S(1)}, bf16[32,1920]{1,0:T(8,128)(2,1)S(1)}, bf16[3,64,2048]{2,1,0:T(8,128)(2,1)S(1)}, bf16[3,64,1024]{2,1,0:T(8,...) custom-call(s32[3]{0:T(128)S(1)} %get-tuple-element.285.place_ref, ...), custom_call_target="tpu_custom_call" | custom-call | tf_op jit(solution)/shard_map/backward/pallas_call | solution.py:433
  125.2 2.6 collective-permute-start.39
  128.4 1.9 collective-permute-start.41
  131.5 7.5 %collective-permute-done.40.refs_2_ = bf16[32,1920]{1,0:T(8,128)(2,1)S(1)} collective-permute-done((bf16[32,1920]{1,0:T(8,128)(2,1)S(1)}, bf16[32,1920]{1,0:T(8,128)(2,1)S(1)}, u32[]{:S(2)}, u32[]{:S(2)}) %collective-permute-start.40) | collective-permute-done | bytes 122912 | tf_op jit(solution)/shard_map/ppermute | solution.py:290
  141.4 1.6 collective-permute-start.46
  143.8 2.0 collective-permute-start.49
  145.8 3.7 %collective-permute-done.46.refs_1_ = bf16[32,1920]{1,0:T(8,128)(2,1)S(1)} collective-permute-done((bf16[32,1920]{1,0:T(8,128)(2,1)S(1)}, bf16[32,1920]{1,0:T(8,128)(2,1)S(1)}, u32[]{:S(2)}, u32[]{:S(2)}) %collective-permute-start.46) | collective-permute-done | bytes 122912 | tf_op jit(solution)/shard_map/ppermute | solution.py:290
  149.5 2.2 forward.18
  151.7 2.9 %backward.12 = (bf16[32,1920]{1,0:T(8,128)(2,1)S(1)}, bf16[32,1920]{1,0:T(8,128)(2,1)S(1)}, bf16[3,64,2048]{2,1,0:T(8,128)(2,1)S(1)}, bf16[3,64,1024]{2,1,0:T(8,...) custom-call(s32[3]{0:T(128)S(1)} %get-tuple-element.286.place_ref, ...), custom_call_target="tpu_custom_call", output_to_operand_aliasing={{2}: (15, {}), {3}: (16, {}), {4}: (17, {}), {5}: (18, {})} | custom-call | tf_op jit(solution)/shard_map/backward/pallas_call | solution.py:433
  155.9 2.2 forward.19
  158.0 2.9 %backward.13 = (bf16[32,1920]{1,0:T(8,128)(2,1)S(1)}, bf16[32,1920]{1,0:T(8,128)(2,1)S(1)}, bf16[3,64,2048]{2,1,0:T(8,128)(2,1)S(1)}, bf16[3,64,1024]{2,1,0:T(8,...) custom-call(s32[3]{0:T(128)S(1)} %get-tuple-element.286.place_ref, ...), custom_call_target="tpu_custom_call", output_to_operand_aliasing={{2}: (16, {}), {3}: (17, {}), {4}: (18, {}), {5}: (19, {})} | custom-call | tf_op jit(solution)/shard_map/backward/pallas_call | solution.py:433
  161.0 3.7 %collective-permute-start.50 = (bf16[32,1920]{1,0:T(8,128)(2,1)S(1)}, bf16[32,1920]{1,0:T(8,128)(2,1)S(1)}, u32[]{:S(2)}, u32[]{:S(2)}) collective-permute-start(bf16[32,1920]{1,0:T(8,128)(2,1)S(1)} %get-tuple-element.213), channel_id=1, source_target_pairs={{0,26},{1,27},{2,24},{3,25},{4,30},{5,31},{6,28},{7,29},{8,2},{9,3... | collective-permute-start | bytes 368648 | tf_op jit(solution)/shard_map/ppermute | solution.py:290
  165.6 2.3 collective-permute-start.52
  168.4 7.2 %collective-permute-done.51.refs_2_ = bf16[32,1920]{1,0:T(8,128)(2,1)S(1)} collective-permute-done((bf16[32,1920]{1,0:T(8,128)(2,1)S(1)}, bf16[32,1920]{1,0:T(8,128)(2,1)S(1)}, u32[]{:S(2)}, u32[]{:S(2)}) %collective-permute-start.51) | collective-permute-done | bytes 122912 | tf_op jit(solution)/shard_map/ppermute | solution.py:290
  178.0 2.1 collective-permute-start.57
  182.5 3.6 %collective-permute-done.57.refs_1_ = bf16[32,1920]{1,0:T(8,128)(2,1)S(1)} collective-permute-done((bf16[32,1920]{1,0:T(8,128)(2,1)S(1)}, bf16[32,1920]{1,0:T(8,128)(2,1)S(1)}, u32[]{:S(2)}, u32[]{:S(2)}) %collective-permute-start.57) | collective-permute-done | bytes 122912 | tf_op jit(solution)/shard_map/ppermute | solution.py:290
  186.1 2.9 %backward.14 = (bf16[32,1920]{1,0:T(8,128)(2,1)S(1)}, bf16[32,1920]{1,0:T(8,128)(2,1)S(1)}, bf16[3,64,2048]{2,1,0:T(8,128)(2,1)S(1)}, bf16[3,64,1024]{2,1,0:T(8,...) custom-call(s32[3]{0:T(128)S(1)} %get-tuple-element.287.place_ref, ...), custom_call_target="tpu_custom_call", output_to_operand_aliasing={{2}: (13, {}), {3}: (14, {}), {4}: (15, {}), {5}: (16, {})} | custom-call | tf_op jit(solution)/shard_map/backward/pallas_call | solution.py:433
  189.0 2.2 collective-permute-start.58
  192.5 2.9 %backward.15 = (bf16[32,1920]{1,0:T(8,128)(2,1)S(1)}, bf16[32,1920]{1,0:T(8,128)(2,1)S(1)}, bf16[3,64,2048]{2,1,0:T(8,128)(2,1)S(1)}, bf16[3,64,1024]{2,1,0:T(8,...) custom-call(s32[3]{0:T(128)S(1)} %get-tuple-element.287.place_ref, ...), custom_call_target="tpu_custom_call", output_to_operand_aliasing={{2}: (14, {}), {3}: (15, {}), {4}: (16, {}), {5}: (17, {})} | custom-call | tf_op jit(solution)/shard_map/backward/pallas_call | solution.py:433
  196.9 2.2 collective-permute-start.62
  199.2 3.1 %collective-permute-start.63 = (bf16[32,1920]{1,0:T(8,128)(2,1)S(1)}, bf16[32,1920]{1,0:T(8,128)(2,1)S(1)}, u32[]{:S(2)}, u32[]{:S(2)}) collective-permute-start(bf16[32,1920]{1,0:T(8,128)(2,1)S(1)} %get-tuple-element.237), channel_id=1, source_target_pairs={{0,30},{1,31},{2,28},{3,29},{4,26},{5,27},{6,24},{7,25},{8,6},{9,7... | collective-permute-start | bytes 368648 | tf_op jit(solution)/shard_map/ppermute | solution.py:290
  202.8 6.9 %collective-permute-done.62.refs_2_ = bf16[32,1920]{1,0:T(8,128)(2,1)S(1)} collective-permute-done((bf16[32,1920]{1,0:T(8,128)(2,1)S(1)}, bf16[32,1920]{1,0:T(8,128)(2,1)S(1)}, u32[]{:S(2)}, u32[]{:S(2)}) %collective-permute-start.62) | collective-permute-done | bytes 122912 | tf_op jit(solution)/shard_map/ppermute | solution.py:290
  212.1 1.8 collective-permute-start.68
  214.7 1.9 collective-permute-start.71
  216.6 3.7 %collective-permute-done.68.refs_1_ = bf16[32,1920]{1,0:T(8,128)(2,1)S(1)} collective-permute-done((bf16[32,1920]{1,0:T(8,128)(2,1)S(1)}, bf16[32,1920]{1,0:T(8,128)(2,1)S(1)}, u32[]{:S(2)}, u32[]{:S(2)}) %collective-permute-start.68) | collective-permute-done | bytes 122912 | tf_op jit(solution)/shard_map/ppermute | solution.py:290
  220.2 2.8 %backward.16 = (bf16[32,1920]{1,0:T(8,128)(2,1)S(1)}, bf16[32,1920]{1,0:T(8,128)(2,1)S(1)}, bf16[3,64,2048]{2,1,0:T(8,128)(2,1)S(1)}, bf16[3,64,1024]{2,1,0:T(8,...) custom-call(s32[3]{0:T(128)S(1)} %get-tuple-element.288.place_ref, ...), custom_call_target="tpu_custom_call", output_to_operand_aliasing={{2}: (13, {}), {3}: (14, {}), {4}: (15, {}), {5}: (16, {})} | custom-call | tf_op jit(solution)/shard_map/backward/pallas_call | solution.py:433
  223.1 2.0 collective-permute-start.69
  226.6 2.8 %backward.17 = (bf16[32,1920]{1,0:T(8,128)(2,1)S(1)}, bf16[32,1920]{1,0:T(8,128)(2,1)S(1)}, bf16[3,64,2048]{2,1,0:T(8,128)(2,1)S(1)}, bf16[3,64,1024]{2,1,0:T(8,...) custom-call(s32[3]{0:T(128)S(1)} %get-tuple-element.288.place_ref, ...), custom_call_target="tpu_custom_call", output_to_operand_aliasing={{2}: (14, {}), {3}: (15, {}), {4}: (16, {}), {5}: (17, {})} | custom-call | tf_op jit(solution)/shard_map/backward/pallas_call | solution.py:433
  230.8 2.6 collective-permute-start.73
  233.5 3.1 %collective-permute-start.74 = (bf16[32,1920]{1,0:T(8,128)(2,1)S(1)}, bf16[32,1920]{1,0:T(8,128)(2,1)S(1)}, u32[]{:S(2)}, u32[]{:S(2)}) collective-permute-start(bf16[32,1920]{1,0:T(8,128)(2,1)S(1)} %get-tuple-element.259), channel_id=1, source_target_pairs={{0,30},{1,31},{2,28},{3,29},{4,26},{5,27},{6,24},{7,25},{8,6},{9,7... | collective-permute-start | bytes 368648 | tf_op jit(solution)/shard_map/ppermute | solution.py:290
  237.1 6.6 %collective-permute-done.73.refs_2_ = bf16[32,1920]{1,0:T(8,128)(2,1)S(1)} collective-permute-done((bf16[32,1920]{1,0:T(8,128)(2,1)S(1)}, bf16[32,1920]{1,0:T(8,128)(2,1)S(1)}, u32[]{:S(2)}, u32[]{:S(2)}) %collective-permute-start.73) | collective-permute-done | bytes 122912 | tf_op jit(solution)/shard_map/ppermute | solution.py:290
  246.0 2.1 collective-permute-start.79
  248.9 1.6 collective-permute-start.81
  250.5 3.7 %collective-permute-done.79.refs_1_ = bf16[32,1920]{1,0:T(8,128)(2,1)S(1)} collective-permute-done((bf16[32,1920]{1,0:T(8,128)(2,1)S(1)}, bf16[32,1920]{1,0:T(8,128)(2,1)S(1)}, u32[]{:S(2)}, u32[]{:S(2)}) %collective-permute-start.79) | collective-permute-done | bytes 122912 | tf_op jit(solution)/shard_map/ppermute | solution.py:290
  254.1 1.8 backward.18
  257.0 3.5 %collective-permute-done.81.refs_1_ = bf16[32,1920]{1,0:T(8,128)(2,1)S(1)} collective-permute-done((bf16[32,1920]{1,0:T(8,128)(2,1)S(1)}, bf16[32,1920]{1,0:T(8,128)(2,1)S(1)}, u32[]{:S(2)}, u32[]{:S(2)}) %collective-permute-start.81) | collective-permute-done | bytes 122912 | tf_op jit(solution)/shard_map/ppermute | solution.py:290
  260.5 1.8 backward.19
  262.3 4.0 %grads.1 = (bf16[2048,1024]{1,0:T(8,128)(2,1)}, bf16[512,2048]{1,0:T(8,128)(2,1)}) custom-call(bf16[3,64,2048]{2,1,0:T(8,128)(2,1)S(1)} %get-tuple-element.266.refs_0_, bf16[3,64,1024]{2,1,0:T(8,128)(2,1)S(1)} %get-tuple-element.267.refs_1_, bf16[3,64,512]{2,1,0:T(8,128)(2,1)S(1)} %get-tuple-element.268.refs_2_, ...), custom_call_target="tpu_custom_call" | custom-call | tf_op jit(solution)/shard_map/grads/pallas_call | solution.py:492
  (146 shorter events, 64.6 us)
Async XLA Ops:
  6.5 9.2 %collective-permute-start.2 = (bf16[32,1920]{1,0:T(8,128)(2,1)S(1)}, bf16[32,1920]{1,0:T(8,128)(2,1)S(1)}, u32[]{:S(2)}, u32[]{:S(2)}) collective-permute-start(bf16[32,1920]{1,0:T(8,128)(2,1)S(1)} %get-tuple-element.146), channel_id=1, source_target_pairs={{0,6},{1,7},{2,4},{3,5},{4,2},{5,3},{6,0},{7,1},{8,14},{9,15},{10,... | collective-permute-start | bytes 368648 | tf_op jit(solution)/shard_map/ppermute | solution.py:290
  11.5 10.4 %collective-permute-start.4 = (bf16[32,1920]{1,0:T(8,128)(2,1)S(1)}, bf16[32,1920]{1,0:T(8,128)(2,1)S(1)}, u32[]{:S(2)}, u32[]{:S(2)}) collective-permute-start(bf16[32,1920]{1,0:T(8,128)(2,1)S(1)} %get-tuple-element.148), channel_id=1, source_target_pairs={{0,2},{1,3},{2,0},{3,1},{4,6},{5,7},{6,4},{7,5},{8,10},{9,11},{10,... | collective-permute-start | bytes 368648 | tf_op jit(solution)/shard_map/ppermute | solution.py:290
  11.5 10.7 %collective-permute-start.5 = (bf16[32,1920]{1,0:T(8,128)(2,1)S(1)}, bf16[32,1920]{1,0:T(8,128)(2,1)S(1)}, u32[]{:S(2)}, u32[]{:S(2)}) collective-permute-start(bf16[32,1920]{1,0:T(8,128)(2,1)S(1)} %get-tuple-element.149), channel_id=1, source_target_pairs={{0,4},{1,5},{2,6},{3,7},{4,0},{5,1},{6,2},{7,3},{8,12},{9,13},{10,... | collective-permute-start | bytes 368648 | tf_op jit(solution)/shard_map/ppermute | solution.py:290
  20.2 10.8 %collective-permute-start.3 = (bf16[32,1920]{1,0:T(8,128)(2,1)S(1)}, bf16[32,1920]{1,0:T(8,128)(2,1)S(1)}, u32[]{:S(2)}, u32[]{:S(2)}) collective-permute-start(bf16[32,1920]{1,0:T(8,128)(2,1)S(1)} %get-tuple-element.147.refs_2_), channel_id=1, source_target_pairs={{0,8},{1,9},{2,10},{3,11},{4,12},{5,13},{6,14},{7,15},{8,16},{9,17... | collective-permute-start | bytes 368648 | tf_op jit(solution)/shard_map/ppermute | solution.py:290
  23.7 7.3 %collective-permute-start.6 = (bf16[32,1920]{1,0:T(8,128)(2,1)S(1)}, bf16[32,1920]{1,0:T(8,128)(2,1)S(1)}, u32[]{:S(2)}, u32[]{:S(2)}) collective-permute-start(bf16[32,1920]{1,0:T(8,128)(2,1)S(1)} %get-tuple-element.150), channel_id=1, source_target_pairs={{0,10},{1,11},{2,8},{3,9},{4,14},{5,15},{6,12},{7,13},{8,18},{9,19... | collective-permute-start | bytes 368648 | tf_op jit(solution)/shard_map/ppermute | solution.py:290
  27.5 11.8 %collective-permute-start.7 = (bf16[32,1920]{1,0:T(8,128)(2,1)S(1)}, bf16[32,1920]{1,0:T(8,128)(2,1)S(1)}, u32[]{:S(2)}, u32[]{:S(2)}) collective-permute-start(bf16[32,1920]{1,0:T(8,128)(2,1)S(1)} %get-tuple-element.151), channel_id=1, source_target_pairs={{0,12},{1,13},{2,14},{3,15},{4,8},{5,9},{6,10},{7,11},{8,20},{9,21... | collective-permute-start | bytes 368648 | tf_op jit(solution)/shard_map/ppermute | solution.py:290
  29.5 9.7 %collective-permute-start.8 = (bf16[32,1920]{1,0:T(8,128)(2,1)S(1)}, bf16[32,1920]{1,0:T(8,128)(2,1)S(1)}, u32[]{:S(2)}, u32[]{:S(2)}) collective-permute-start(bf16[32,1920]{1,0:T(8,128)(2,1)S(1)} %get-tuple-element.152), channel_id=1, source_target_pairs={{0,14},{1,15},{2,12},{3,13},{4,10},{5,11},{6,8},{7,9},{8,22},{9,23... | collective-permute-start | bytes 368648 | tf_op jit(solution)/shard_map/ppermute | solution.py:290
  30.9 8.8 %collective-permute-start.9 = (bf16[32,1920]{1,0:T(8,128)(2,1)S(1)}, bf16[32,1920]{1,0:T(8,128)(2,1)S(1)}, u32[]{:S(2)}, u32[]{:S(2)}) collective-permute-start(bf16[32,1920]{1,0:T(8,128)(2,1)S(1)} %collective-permute-done.3.refs_0_), channel_id=1, source_target_pairs={{0,1},{1,0},{2,3},{3,2},{4,5},{5,4},{6,7},{7,6},{8,9},{9,8},{10,11... | collective-permute-start | bytes 368648 | tf_op jit(solution)/shard_map/ppermute | solution.py:290
  31.0 8.7 %collective-permute-start.10 = (bf16[32,1920]{1,0:T(8,128)(2,1)S(1)}, bf16[32,1920]{1,0:T(8,128)(2,1)S(1)}, u32[]{:S(2)}, u32[]{:S(2)}) collective-permute-start(bf16[32,1920]{1,0:T(8,128)(2,1)S(1)} %collective-permute-done.6.refs_1_), channel_id=1, source_target_pairs={{0,1},{1,0},{2,3},{3,2},{4,5},{5,4},{6,7},{7,6},{8,9},{9,8},{10,11... | collective-permute-start | bytes 368648 | tf_op jit(solution)/shard_map/ppermute | solution.py:290
  41.6 8.1 %collective-permute-start.13 = (bf16[32,1920]{1,0:T(8,128)(2,1)S(1)}, bf16[32,1920]{1,0:T(8,128)(2,1)S(1)}, u32[]{:S(2)}, u32[]{:S(2)}) collective-permute-start(bf16[32,1920]{1,0:T(8,128)(2,1)S(1)} %get-tuple-element.155), channel_id=1, source_target_pairs={{0,6},{1,7},{2,4},{3,5},{4,2},{5,3},{6,0},{7,1},{8,14},{9,15},{10,... | collective-permute-start | bytes 368648 | tf_op jit(solution)/shard_map/ppermute | solution.py:290
  43.4 8.7 %collective-permute-start.15 = (bf16[32,1920]{1,0:T(8,128)(2,1)S(1)}, bf16[32,1920]{1,0:T(8,128)(2,1)S(1)}, u32[]{:S(2)}, u32[]{:S(2)}) collective-permute-start(bf16[32,1920]{1,0:T(8,128)(2,1)S(1)} %get-tuple-element.157), channel_id=1, source_target_pairs={{0,2},{1,3},{2,0},{3,1},{4,6},{5,7},{6,4},{7,5},{8,10},{9,11},{10,... | collective-permute-start | bytes 368648 | tf_op jit(solution)/shard_map/ppermute | solution.py:290
  44.2 11.9 %collective-permute-start.16 = (bf16[32,1920]{1,0:T(8,128)(2,1)S(1)}, bf16[32,1920]{1,0:T(8,128)(2,1)S(1)}, u32[]{:S(2)}, u32[]{:S(2)}) collective-permute-start(bf16[32,1920]{1,0:T(8,128)(2,1)S(1)} %get-tuple-element.158), channel_id=1, source_target_pairs={{0,4},{1,5},{2,6},{3,7},{4,0},{5,1},{6,2},{7,3},{8,12},{9,13},{10,... | collective-permute-start | bytes 368648 | tf_op jit(solution)/shard_map/ppermute | solution.py:290
  51.2 11.7 %collective-permute-start.14 = (bf16[32,1920]{1,0:T(8,128)(2,1)S(1)}, bf16[32,1920]{1,0:T(8,128)(2,1)S(1)}, u32[]{:S(2)}, u32[]{:S(2)}) collective-permute-start(bf16[32,1920]{1,0:T(8,128)(2,1)S(1)} %get-tuple-element.156.refs_2_), channel_id=1, source_target_pairs={{0,8},{1,9},{2,10},{3,11},{4,12},{5,13},{6,14},{7,15},{8,16},{9,17... | collective-permute-start | bytes 368648 | tf_op jit(solution)/shard_map/ppermute | solution.py:290
  57.6 8.0 %collective-permute-start.17 = (bf16[32,1920]{1,0:T(8,128)(2,1)S(1)}, bf16[32,1920]{1,0:T(8,128)(2,1)S(1)}, u32[]{:S(2)}, u32[]{:S(2)}) collective-permute-start(bf16[32,1920]{1,0:T(8,128)(2,1)S(1)} %get-tuple-element.159), channel_id=1, source_target_pairs={{0,10},{1,11},{2,8},{3,9},{4,14},{5,15},{6,12},{7,13},{8,18},{9,19... | collective-permute-start | bytes 368648 | tf_op jit(solution)/shard_map/ppermute | solution.py:290
  57.7 13.7 %collective-permute-start.18 = (bf16[32,1920]{1,0:T(8,128)(2,1)S(1)}, bf16[32,1920]{1,0:T(8,128)(2,1)S(1)}, u32[]{:S(2)}, u32[]{:S(2)}) collective-permute-start(bf16[32,1920]{1,0:T(8,128)(2,1)S(1)} %get-tuple-element.160), channel_id=1, source_target_pairs={{0,12},{1,13},{2,14},{3,15},{4,8},{5,9},{6,10},{7,11},{8,20},{9,21... | collective-permute-start | bytes 368648 | tf_op jit(solution)/shard_map/ppermute | solution.py:290
  61.5 9.9 %collective-permute-start.19 = (bf16[32,1920]{1,0:T(8,128)(2,1)S(1)}, bf16[32,1920]{1,0:T(8,128)(2,1)S(1)}, u32[]{:S(2)}, u32[]{:S(2)}) collective-permute-start(bf16[32,1920]{1,0:T(8,128)(2,1)S(1)} %get-tuple-element.161), channel_id=1, source_target_pairs={{0,14},{1,15},{2,12},{3,13},{4,10},{5,11},{6,8},{7,9},{8,22},{9,23... | collective-permute-start | bytes 368648 | tf_op jit(solution)/shard_map/ppermute | solution.py:290
  62.9 9.0 %collective-permute-start.20 = (bf16[32,1920]{1,0:T(8,128)(2,1)S(1)}, bf16[32,1920]{1,0:T(8,128)(2,1)S(1)}, u32[]{:S(2)}, u32[]{:S(2)}) collective-permute-start(bf16[32,1920]{1,0:T(8,128)(2,1)S(1)} %collective-permute-done.14.refs_0_), channel_id=1, source_target_pairs={{0,1},{1,0},{2,3},{3,2},{4,5},{5,4},{6,7},{7,6},{8,9},{9,8},{10,11... | collective-permute-start | bytes 368648 | tf_op jit(solution)/shard_map/ppermute | solution.py:290
  73.8 8.1 %collective-permute-start.24 = (bf16[32,1920]{1,0:T(8,128)(2,1)S(1)}, bf16[32,1920]{1,0:T(8,128)(2,1)S(1)}, u32[]{:S(2)}, u32[]{:S(2)}) collective-permute-start(bf16[32,1920]{1,0:T(8,128)(2,1)S(1)} %get-tuple-element.163), channel_id=1, source_target_pairs={{0,6},{1,7},{2,4},{3,5},{4,2},{5,3},{6,0},{7,1},{8,14},{9,15},{10,... | collective-permute-start | bytes 368648 | tf_op jit(solution)/shard_map/ppermute | solution.py:290
  75.6 8.5 %collective-permute-start.26 = (bf16[32,1920]{1,0:T(8,128)(2,1)S(1)}, bf16[32,1920]{1,0:T(8,128)(2,1)S(1)}, u32[]{:S(2)}, u32[]{:S(2)}) collective-permute-start(bf16[32,1920]{1,0:T(8,128)(2,1)S(1)} %get-tuple-element.165), channel_id=1, source_target_pairs={{0,2},{1,3},{2,0},{3,1},{4,6},{5,7},{6,4},{7,5},{8,10},{9,11},{10,... | collective-permute-start | bytes 368648 | tf_op jit(solution)/shard_map/ppermute | solution.py:290
  76.5 11.9 %collective-permute-start.27 = (bf16[32,1920]{1,0:T(8,128)(2,1)S(1)}, bf16[32,1920]{1,0:T(8,128)(2,1)S(1)}, u32[]{:S(2)}, u32[]{:S(2)}) collective-permute-start(bf16[32,1920]{1,0:T(8,128)(2,1)S(1)} %get-tuple-element.166), channel_id=1, source_target_pairs={{0,4},{1,5},{2,6},{3,7},{4,0},{5,1},{6,2},{7,3},{8,12},{9,13},{10,... | collective-permute-start | bytes 368648 | tf_op jit(solution)/shard_map/ppermute | solution.py:290
  83.4 12.0 %collective-permute-start.25 = (bf16[32,1920]{1,0:T(8,128)(2,1)S(1)}, bf16[32,1920]{1,0:T(8,128)(2,1)S(1)}, u32[]{:S(2)}, u32[]{:S(2)}) collective-permute-start(bf16[32,1920]{1,0:T(8,128)(2,1)S(1)} %get-tuple-element.164.refs_2_), channel_id=1, source_target_pairs={{0,8},{1,9},{2,10},{3,11},{4,12},{5,13},{6,14},{7,15},{8,16},{9,17... | collective-permute-start | bytes 368648 | tf_op jit(solution)/shard_map/ppermute | solution.py:290
  89.9 7.8 %collective-permute-start.28 = (bf16[32,1920]{1,0:T(8,128)(2,1)S(1)}, bf16[32,1920]{1,0:T(8,128)(2,1)S(1)}, u32[]{:S(2)}, u32[]{:S(2)}) collective-permute-start(bf16[32,1920]{1,0:T(8,128)(2,1)S(1)} %get-tuple-element.167), channel_id=1, source_target_pairs={{0,10},{1,11},{2,8},{3,9},{4,14},{5,15},{6,12},{7,13},{8,18},{9,19... | collective-permute-start | bytes 368648 | tf_op jit(solution)/shard_map/ppermute | solution.py:290
  90.0 13.6 %collective-permute-start.29 = (bf16[32,1920]{1,0:T(8,128)(2,1)S(1)}, bf16[32,1920]{1,0:T(8,128)(2,1)S(1)}, u32[]{:S(2)}, u32[]{:S(2)}) collective-permute-start(bf16[32,1920]{1,0:T(8,128)(2,1)S(1)} %get-tuple-element.168), channel_id=1, source_target_pairs={{0,12},{1,13},{2,14},{3,15},{4,8},{5,9},{6,10},{7,11},{8,20},{9,21... | collective-permute-start | bytes 368648 | tf_op jit(solution)/shard_map/ppermute | solution.py:290
  93.8 9.9 %collective-permute-start.30 = (bf16[32,1920]{1,0:T(8,128)(2,1)S(1)}, bf16[32,1920]{1,0:T(8,128)(2,1)S(1)}, u32[]{:S(2)}, u32[]{:S(2)}) collective-permute-start(bf16[32,1920]{1,0:T(8,128)(2,1)S(1)} %get-tuple-element.169), channel_id=1, source_target_pairs={{0,14},{1,15},{2,12},{3,13},{4,10},{5,11},{6,8},{7,9},{8,22},{9,23... | collective-permute-start | bytes 368648 | tf_op jit(solution)/shard_map/ppermute | solution.py:290
  95.3 8.8 %collective-permute-start.31 = (bf16[32,1920]{1,0:T(8,128)(2,1)S(1)}, bf16[32,1920]{1,0:T(8,128)(2,1)S(1)}, u32[]{:S(2)}, u32[]{:S(2)}) collective-permute-start(bf16[32,1920]{1,0:T(8,128)(2,1)S(1)} %collective-permute-done.25.refs_0_), channel_id=1, source_target_pairs={{0,1},{1,0},{2,3},{3,2},{4,5},{5,4},{6,7},{7,6},{8,9},{9,8},{10,11... | collective-permute-start | bytes 368648 | tf_op jit(solution)/shard_map/ppermute | solution.py:290
  97.8 6.4 %collective-permute-start.32 = (bf16[32,1920]{1,0:T(8,128)(2,1)S(1)}, bf16[32,1920]{1,0:T(8,128)(2,1)S(1)}, u32[]{:S(2)}, u32[]{:S(2)}) collective-permute-start(bf16[32,1920]{1,0:T(8,128)(2,1)S(1)} %collective-permute-done.28.refs_1_), channel_id=1, source_target_pairs={{0,1},{1,0},{2,3},{3,2},{4,5},{5,4},{6,7},{7,6},{8,9},{9,8},{10,11... | collective-permute-start | bytes 368648 | tf_op jit(solution)/shard_map/ppermute | solution.py:290
  106.0 8.1 %collective-permute-start.35 = (bf16[32,1920]{1,0:T(8,128)(2,1)S(1)}, bf16[32,1920]{1,0:T(8,128)(2,1)S(1)}, u32[]{:S(2)}, u32[]{:S(2)}) collective-permute-start(bf16[32,1920]{1,0:T(8,128)(2,1)S(1)} %get-tuple-element.171), channel_id=1, source_target_pairs={{0,6},{1,7},{2,4},{3,5},{4,2},{5,3},{6,0},{7,1},{8,14},{9,15},{10,... | collective-permute-start | bytes 368648 | tf_op jit(solution)/shard_map/ppermute | solution.py:290
  107.8 11.3 %collective-permute-start.37 = (bf16[32,1920]{1,0:T(8,128)(2,1)S(1)}, bf16[32,1920]{1,0:T(8,128)(2,1)S(1)}, u32[]{:S(2)}, u32[]{:S(2)}) collective-permute-start(bf16[32,1920]{1,0:T(8,128)(2,1)S(1)} %get-tuple-element.178), channel_id=1, source_target_pairs={{0,2},{1,3},{2,0},{3,1},{4,6},{5,7},{6,4},{7,5},{8,10},{9,11},{10,... | collective-permute-start | bytes 368648 | tf_op jit(solution)/shard_map/ppermute | solution.py:290
  108.8 12.0 %collective-permute-start.38 = (bf16[32,1920]{1,0:T(8,128)(2,1)S(1)}, bf16[32,1920]{1,0:T(8,128)(2,1)S(1)}, u32[]{:S(2)}, u32[]{:S(2)}) collective-permute-start(bf16[32,1920]{1,0:T(8,128)(2,1)S(1)} %get-tuple-element.179), channel_id=1, source_target_pairs={{0,4},{1,5},{2,6},{3,7},{4,0},{5,1},{6,2},{7,3},{8,12},{9,13},{10,... | collective-permute-start | bytes 368648 | tf_op jit(solution)/shard_map/ppermute | solution.py:290
  118.5 11.7 %collective-permute-start.36 = (bf16[32,1920]{1,0:T(8,128)(2,1)S(1)}, bf16[32,1920]{1,0:T(8,128)(2,1)S(1)}, u32[]{:S(2)}, u32[]{:S(2)}) collective-permute-start(bf16[32,1920]{1,0:T(8,128)(2,1)S(1)} %get-tuple-element.177.refs_2_.refs_9_), channel_id=1, source_target_pairs={{0,8},{1,9},{2,10},{3,11},{4,12},{5,13},{6,14},{7,15},{8,0},{9,1},... | collective-permute-start | bytes 368648 | tf_op jit(solution)/shard_map/ppermute | solution.py:290
  127.8 11.2 %collective-permute-start.40 = (bf16[32,1920]{1,0:T(8,128)(2,1)S(1)}, bf16[32,1920]{1,0:T(8,128)(2,1)S(1)}, u32[]{:S(2)}, u32[]{:S(2)}) collective-permute-start(bf16[32,1920]{1,0:T(8,128)(2,1)S(1)} %get-tuple-element.186), channel_id=1, source_target_pairs={{0,12},{1,13},{2,14},{3,15},{4,8},{5,9},{6,10},{7,11},{8,4},{9,5},... | collective-permute-start | bytes 368648 | tf_op jit(solution)/shard_map/ppermute | solution.py:290
  128.4 10.7 %collective-permute-start.41 = (bf16[32,1920]{1,0:T(8,128)(2,1)S(1)}, bf16[32,1920]{1,0:T(8,128)(2,1)S(1)}, u32[]{:S(2)}, u32[]{:S(2)}) collective-permute-start(bf16[32,1920]{1,0:T(8,128)(2,1)S(1)} %get-tuple-element.187), channel_id=1, source_target_pairs={{0,14},{1,15},{2,12},{3,13},{4,10},{5,11},{6,8},{7,9},{8,6},{9,7},... | collective-permute-start | bytes 368648 | tf_op jit(solution)/shard_map/ppermute | solution.py:290
  130.2 9.3 %collective-permute-start.42 = (bf16[32,1920]{1,0:T(8,128)(2,1)S(1)}, bf16[32,1920]{1,0:T(8,128)(2,1)S(1)}, u32[]{:S(2)}, u32[]{:S(2)}) collective-permute-start(bf16[32,1920]{1,0:T(8,128)(2,1)S(1)} %collective-permute-done.36.refs_0_), channel_id=1, source_target_pairs={{0,1},{1,0},{2,3},{3,2},{4,5},{5,4},{6,7},{7,6},{8,9},{9,8},{10,11... | collective-permute-start | bytes 368648 | tf_op jit(solution)/shard_map/ppermute | solution.py:290
  131.5 8.1 %collective-permute-start.43 = (bf16[32,1920]{1,0:T(8,128)(2,1)S(1)}, bf16[32,1920]{1,0:T(8,128)(2,1)S(1)}, u32[]{:S(2)}, u32[]{:S(2)}) collective-permute-start(bf16[32,1920]{1,0:T(8,128)(2,1)S(1)} %collective-permute-done.39.refs_1_), channel_id=1, source_target_pairs={{0,1},{1,0},{2,3},{3,2},{4,5},{5,4},{6,7},{7,6},{8,9},{9,8},{10,11... | collective-permute-start | bytes 368648 | tf_op jit(solution)/shard_map/ppermute | solution.py:290
  141.4 8.1 %collective-permute-start.46 = (bf16[32,1920]{1,0:T(8,128)(2,1)S(1)}, bf16[32,1920]{1,0:T(8,128)(2,1)S(1)}, u32[]{:S(2)}, u32[]{:S(2)}) collective-permute-start(bf16[32,1920]{1,0:T(8,128)(2,1)S(1)} %get-tuple-element.189), channel_id=1, source_target_pairs={{0,6},{1,7},{2,4},{3,5},{4,2},{5,3},{6,0},{7,1},{8,14},{9,15},{10,... | collective-permute-start | bytes 368648 | tf_op jit(solution)/shard_map/ppermute | solution.py:290
  143.0 12.4 %collective-permute-start.48 = (bf16[32,1920]{1,0:T(8,128)(2,1)S(1)}, bf16[32,1920]{1,0:T(8,128)(2,1)S(1)}, u32[]{:S(2)}, u32[]{:S(2)}) collective-permute-start(bf16[32,1920]{1,0:T(8,128)(2,1)S(1)} %get-tuple-element.201), channel_id=1, source_target_pairs={{0,2},{1,3},{2,0},{3,1},{4,6},{5,7},{6,4},{7,5},{8,10},{9,11},{10,... | collective-permute-start | bytes 368648 | tf_op jit(solution)/shard_map/ppermute | solution.py:290
  143.8 12.1 %collective-permute-start.49 = (bf16[32,1920]{1,0:T(8,128)(2,1)S(1)}, bf16[32,1920]{1,0:T(8,128)(2,1)S(1)}, u32[]{:S(2)}, u32[]{:S(2)}) collective-permute-start(bf16[32,1920]{1,0:T(8,128)(2,1)S(1)} %get-tuple-element.202), channel_id=1, source_target_pairs={{0,4},{1,5},{2,6},{3,7},{4,0},{5,1},{6,2},{7,3},{8,12},{9,13},{10,... | collective-permute-start | bytes 368648 | tf_op jit(solution)/shard_map/ppermute | solution.py:290
  154.6 13.3 %collective-permute-start.47 = (bf16[32,1920]{1,0:T(8,128)(2,1)S(1)}, bf16[32,1920]{1,0:T(8,128)(2,1)S(1)}, u32[]{:S(2)}, u32[]{:S(2)}) collective-permute-start(bf16[32,1920]{1,0:T(8,128)(2,1)S(1)} %get-tuple-element.200.refs_2_.refs_10_), channel_id=1, source_target_pairs={{0,24},{1,25},{2,26},{3,27},{4,28},{5,29},{6,30},{7,31},{8,0},{9,1... | collective-permute-start | bytes 368648 | tf_op jit(solution)/shard_map/ppermute | solution.py:290
  161.0 7.0 %collective-permute-start.50 = (bf16[32,1920]{1,0:T(8,128)(2,1)S(1)}, bf16[32,1920]{1,0:T(8,128)(2,1)S(1)}, u32[]{:S(2)}, u32[]{:S(2)}) collective-permute-start(bf16[32,1920]{1,0:T(8,128)(2,1)S(1)} %get-tuple-element.213), channel_id=1, source_target_pairs={{0,26},{1,27},{2,24},{3,25},{4,30},{5,31},{6,28},{7,29},{8,2},{9,3... | collective-permute-start | bytes 368648 | tf_op jit(solution)/shard_map/ppermute | solution.py:290
  164.7 11.0 %collective-permute-start.51 = (bf16[32,1920]{1,0:T(8,128)(2,1)S(1)}, bf16[32,1920]{1,0:T(8,128)(2,1)S(1)}, u32[]{:S(2)}, u32[]{:S(2)}) collective-permute-start(bf16[32,1920]{1,0:T(8,128)(2,1)S(1)} %get-tuple-element.214), channel_id=1, source_target_pairs={{0,28},{1,29},{2,30},{3,31},{4,24},{5,25},{6,26},{7,27},{8,4},{9,5... | collective-permute-start | bytes 368648 | tf_op jit(solution)/shard_map/ppermute | solution.py:290
  165.6 10.1 %collective-permute-start.52 = (bf16[32,1920]{1,0:T(8,128)(2,1)S(1)}, bf16[32,1920]{1,0:T(8,128)(2,1)S(1)}, u32[]{:S(2)}, u32[]{:S(2)}) collective-permute-start(bf16[32,1920]{1,0:T(8,128)(2,1)S(1)} %get-tuple-element.215), channel_id=1, source_target_pairs={{0,30},{1,31},{2,28},{3,29},{4,26},{5,27},{6,24},{7,25},{8,6},{9,7... | collective-permute-start | bytes 368648 | tf_op jit(solution)/shard_map/ppermute | solution.py:290
  167.9 8.2 %collective-permute-start.53 = (bf16[32,1920]{1,0:T(8,128)(2,1)S(1)}, bf16[32,1920]{1,0:T(8,128)(2,1)S(1)}, u32[]{:S(2)}, u32[]{:S(2)}) collective-permute-start(bf16[32,1920]{1,0:T(8,128)(2,1)S(1)} %collective-permute-done.47.refs_0_), channel_id=1, source_target_pairs={{0,1},{1,0},{2,3},{3,2},{4,5},{5,4},{6,7},{7,6},{8,9},{9,8},{10,11... | collective-permute-start | bytes 368648 | tf_op jit(solution)/shard_map/ppermute | solution.py:290
  168.0 8.2 %collective-permute-start.54 = (bf16[32,1920]{1,0:T(8,128)(2,1)S(1)}, bf16[32,1920]{1,0:T(8,128)(2,1)S(1)}, u32[]{:S(2)}, u32[]{:S(2)}) collective-permute-start(bf16[32,1920]{1,0:T(8,128)(2,1)S(1)} %collective-permute-done.50.refs_1_), channel_id=1, source_target_pairs={{0,1},{1,0},{2,3},{3,2},{4,5},{5,4},{6,7},{7,6},{8,9},{9,8},{10,11... | collective-permute-start | bytes 368648 | tf_op jit(solution)/shard_map/ppermute | solution.py:290
  178.0 8.1 %collective-permute-start.57 = (bf16[32,1920]{1,0:T(8,128)(2,1)S(1)}, bf16[32,1920]{1,0:T(8,128)(2,1)S(1)}, u32[]{:S(2)}, u32[]{:S(2)}) collective-permute-start(bf16[32,1920]{1,0:T(8,128)(2,1)S(1)} %get-tuple-element.217), channel_id=1, source_target_pairs={{0,6},{1,7},{2,4},{3,5},{4,2},{5,3},{6,0},{7,1},{8,14},{9,15},{10,... | collective-permute-start | bytes 368648 | tf_op jit(solution)/shard_map/ppermute | solution.py:290
  180.1 11.1 %collective-permute-start.59 = (bf16[32,1920]{1,0:T(8,128)(2,1)S(1)}, bf16[32,1920]{1,0:T(8,128)(2,1)S(1)}, u32[]{:S(2)}, u32[]{:S(2)}) collective-permute-start(bf16[32,1920]{1,0:T(8,128)(2,1)S(1)} %get-tuple-element.226), channel_id=1, source_target_pairs={{0,2},{1,3},{2,0},{3,1},{4,6},{5,7},{6,4},{7,5},{8,10},{9,11},{10,... | collective-permute-start | bytes 368648 | tf_op jit(solution)/shard_map/ppermute | solution.py:290
  181.0 11.5 %collective-permute-start.60 = (bf16[32,1920]{1,0:T(8,128)(2,1)S(1)}, bf16[32,1920]{1,0:T(8,128)(2,1)S(1)}, u32[]{:S(2)}, u32[]{:S(2)}) collective-permute-start(bf16[32,1920]{1,0:T(8,128)(2,1)S(1)} %get-tuple-element.227), channel_id=1, source_target_pairs={{0,4},{1,5},{2,6},{3,7},{4,0},{5,1},{6,2},{7,3},{8,12},{9,13},{10,... | collective-permute-start | bytes 368648 | tf_op jit(solution)/shard_map/ppermute | solution.py:290
  189.0 13.3 %collective-permute-start.58 = (bf16[32,1920]{1,0:T(8,128)(2,1)S(1)}, bf16[32,1920]{1,0:T(8,128)(2,1)S(1)}, u32[]{:S(2)}, u32[]{:S(2)}) collective-permute-start(bf16[32,1920]{1,0:T(8,128)(2,1)S(1)} %get-tuple-element.225.refs_8_), channel_id=1, source_target_pairs={{0,24},{1,25},{2,26},{3,27},{4,28},{5,29},{6,30},{7,31},{8,0},{9,1... | collective-permute-start | bytes 368648 | tf_op jit(solution)/shard_map/ppermute | solution.py:290
  195.4 7.0 %collective-permute-start.61 = (bf16[32,1920]{1,0:T(8,128)(2,1)S(1)}, bf16[32,1920]{1,0:T(8,128)(2,1)S(1)}, u32[]{:S(2)}, u32[]{:S(2)}) collective-permute-start(bf16[32,1920]{1,0:T(8,128)(2,1)S(1)} %get-tuple-element.235), channel_id=1, source_target_pairs={{0,26},{1,27},{2,24},{3,25},{4,30},{5,31},{6,28},{7,29},{8,2},{9,3... | collective-permute-start | bytes 368648 | tf_op jit(solution)/shard_map/ppermute | solution.py:290
  196.9 12.8 %collective-permute-start.62 = (bf16[32,1920]{1,0:T(8,128)(2,1)S(1)}, bf16[32,1920]{1,0:T(8,128)(2,1)S(1)}, u32[]{:S(2)}, u32[]{:S(2)}) collective-permute-start(bf16[32,1920]{1,0:T(8,128)(2,1)S(1)} %get-tuple-element.236), channel_id=1, source_target_pairs={{0,28},{1,29},{2,30},{3,31},{4,24},{5,25},{6,26},{7,27},{8,4},{9,5... | collective-permute-start | bytes 368648 | tf_op jit(solution)/shard_map/ppermute | solution.py:290
  199.2 10.6 %collective-permute-start.63 = (bf16[32,1920]{1,0:T(8,128)(2,1)S(1)}, bf16[32,1920]{1,0:T(8,128)(2,1)S(1)}, u32[]{:S(2)}, u32[]{:S(2)}) collective-permute-start(bf16[32,1920]{1,0:T(8,128)(2,1)S(1)} %get-tuple-element.237), channel_id=1, source_target_pairs={{0,30},{1,31},{2,28},{3,29},{4,26},{5,27},{6,24},{7,25},{8,6},{9,7... | collective-permute-start | bytes 368648 | tf_op jit(solution)/shard_map/ppermute | solution.py:290
  202.3 7.9 %collective-permute-start.64 = (bf16[32,1920]{1,0:T(8,128)(2,1)S(1)}, bf16[32,1920]{1,0:T(8,128)(2,1)S(1)}, u32[]{:S(2)}, u32[]{:S(2)}) collective-permute-start(bf16[32,1920]{1,0:T(8,128)(2,1)S(1)} %collective-permute-done.58.refs_0_), channel_id=1, source_target_pairs={{0,1},{1,0},{2,3},{3,2},{4,5},{5,4},{6,7},{7,6},{8,9},{9,8},{10,11... | collective-permute-start | bytes 368648 | tf_op jit(solution)/shard_map/ppermute | solution.py:290
  202.3 7.9 %collective-permute-start.65 = (bf16[32,1920]{1,0:T(8,128)(2,1)S(1)}, bf16[32,1920]{1,0:T(8,128)(2,1)S(1)}, u32[]{:S(2)}, u32[]{:S(2)}) collective-permute-start(bf16[32,1920]{1,0:T(8,128)(2,1)S(1)} %collective-permute-done.61.refs_1_), channel_id=1, source_target_pairs={{0,1},{1,0},{2,3},{3,2},{4,5},{5,4},{6,7},{7,6},{8,9},{9,8},{10,11... | collective-permute-start | bytes 368648 | tf_op jit(solution)/shard_map/ppermute | solution.py:290
  212.1 8.1 %collective-permute-start.68 = (bf16[32,1920]{1,0:T(8,128)(2,1)S(1)}, bf16[32,1920]{1,0:T(8,128)(2,1)S(1)}, u32[]{:S(2)}, u32[]{:S(2)}) collective-permute-start(bf16[32,1920]{1,0:T(8,128)(2,1)S(1)} %get-tuple-element.239), channel_id=1, source_target_pairs={{0,6},{1,7},{2,4},{3,5},{4,2},{5,3},{6,0},{7,1},{8,14},{9,15},{10,... | collective-permute-start | bytes 368648 | tf_op jit(solution)/shard_map/ppermute | solution.py:290
  213.9 11.2 %collective-permute-start.70 = (bf16[32,1920]{1,0:T(8,128)(2,1)S(1)}, bf16[32,1920]{1,0:T(8,128)(2,1)S(1)}, u32[]{:S(2)}, u32[]{:S(2)}) collective-permute-start(bf16[32,1920]{1,0:T(8,128)(2,1)S(1)} %get-tuple-element.248), channel_id=1, source_target_pairs={{0,2},{1,3},{2,0},{3,1},{4,6},{5,7},{6,4},{7,5},{8,10},{9,11},{10,... | collective-permute-start | bytes 368648 | tf_op jit(solution)/shard_map/ppermute | solution.py:290
  214.7 11.9 %collective-permute-start.71 = (bf16[32,1920]{1,0:T(8,128)(2,1)S(1)}, bf16[32,1920]{1,0:T(8,128)(2,1)S(1)}, u32[]{:S(2)}, u32[]{:S(2)}) collective-permute-start(bf16[32,1920]{1,0:T(8,128)(2,1)S(1)} %get-tuple-element.249), channel_id=1, source_target_pairs={{0,4},{1,5},{2,6},{3,7},{4,0},{5,1},{6,2},{7,3},{8,12},{9,13},{10,... | collective-permute-start | bytes 368648 | tf_op jit(solution)/shard_map/ppermute | solution.py:290
  223.1 13.4 %collective-permute-start.69 = (bf16[32,1920]{1,0:T(8,128)(2,1)S(1)}, bf16[32,1920]{1,0:T(8,128)(2,1)S(1)}, u32[]{:S(2)}, u32[]{:S(2)}) collective-permute-start(bf16[32,1920]{1,0:T(8,128)(2,1)S(1)} %get-tuple-element.247.refs_8_), channel_id=1, source_target_pairs={{0,24},{1,25},{2,26},{3,27},{4,28},{5,29},{6,30},{7,31},{8,0},{9,1... | collective-permute-start | bytes 368648 | tf_op jit(solution)/shard_map/ppermute | solution.py:290
  229.5 7.1 %collective-permute-start.72 = (bf16[32,1920]{1,0:T(8,128)(2,1)S(1)}, bf16[32,1920]{1,0:T(8,128)(2,1)S(1)}, u32[]{:S(2)}, u32[]{:S(2)}) collective-permute-start(bf16[32,1920]{1,0:T(8,128)(2,1)S(1)} %get-tuple-element.257), channel_id=1, source_target_pairs={{0,26},{1,27},{2,24},{3,25},{4,30},{5,31},{6,28},{7,29},{8,2},{9,3... | collective-permute-start | bytes 368648 | tf_op jit(solution)/shard_map/ppermute | solution.py:290
  230.8 12.8 %collective-permute-start.73 = (bf16[32,1920]{1,0:T(8,128)(2,1)S(1)}, bf16[32,1920]{1,0:T(8,128)(2,1)S(1)}, u32[]{:S(2)}, u32[]{:S(2)}) collective-permute-start(bf16[32,1920]{1,0:T(8,128)(2,1)S(1)} %get-tuple-element.258), channel_id=1, source_target_pairs={{0,28},{1,29},{2,30},{3,31},{4,24},{5,25},{6,26},{7,27},{8,4},{9,5... | collective-permute-start | bytes 368648 | tf_op jit(solution)/shard_map/ppermute | solution.py:290
  233.5 10.2 %collective-permute-start.74 = (bf16[32,1920]{1,0:T(8,128)(2,1)S(1)}, bf16[32,1920]{1,0:T(8,128)(2,1)S(1)}, u32[]{:S(2)}, u32[]{:S(2)}) collective-permute-start(bf16[32,1920]{1,0:T(8,128)(2,1)S(1)} %get-tuple-element.259), channel_id=1, source_target_pairs={{0,30},{1,31},{2,28},{3,29},{4,26},{5,27},{6,24},{7,25},{8,6},{9,7... | collective-permute-start | bytes 368648 | tf_op jit(solution)/shard_map/ppermute | solution.py:290
  236.5 7.6 %collective-permute-start.75 = (bf16[32,1920]{1,0:T(8,128)(2,1)S(1)}, bf16[32,1920]{1,0:T(8,128)(2,1)S(1)}, u32[]{:S(2)}, u32[]{:S(2)}) collective-permute-start(bf16[32,1920]{1,0:T(8,128)(2,1)S(1)} %collective-permute-done.69.refs_0_), channel_id=1, source_target_pairs={{0,1},{1,0},{2,3},{3,2},{4,5},{5,4},{6,7},{7,6},{8,9},{9,8},{10,11... | collective-permute-start | bytes 368648 | tf_op jit(solution)/shard_map/ppermute | solution.py:290
  236.6 7.6 %collective-permute-start.76 = (bf16[32,1920]{1,0:T(8,128)(2,1)S(1)}, bf16[32,1920]{1,0:T(8,128)(2,1)S(1)}, u32[]{:S(2)}, u32[]{:S(2)}) collective-permute-start(bf16[32,1920]{1,0:T(8,128)(2,1)S(1)} %collective-permute-done.72.refs_1_), channel_id=1, source_target_pairs={{0,1},{1,0},{2,3},{3,2},{4,5},{5,4},{6,7},{7,6},{8,9},{9,8},{10,11... | collective-permute-start | bytes 368648 | tf_op jit(solution)/shard_map/ppermute | solution.py:290
  246.0 8.1 %collective-permute-start.79 = (bf16[32,1920]{1,0:T(8,128)(2,1)S(1)}, bf16[32,1920]{1,0:T(8,128)(2,1)S(1)}, u32[]{:S(2)}, u32[]{:S(2)}) collective-permute-start(bf16[32,1920]{1,0:T(8,128)(2,1)S(1)} %get-tuple-element.261), channel_id=1, source_target_pairs={{0,6},{1,7},{2,4},{3,5},{4,2},{5,3},{6,0},{7,1},{8,14},{9,15},{10,... | collective-permute-start | bytes 368648 | tf_op jit(solution)/shard_map/ppermute | solution.py:290
  248.1 8.9 %collective-permute-start.80 = (bf16[32,1920]{1,0:T(8,128)(2,1)S(1)}, bf16[32,1920]{1,0:T(8,128)(2,1)S(1)}, u32[]{:S(2)}, u32[]{:S(2)}) collective-permute-start(bf16[32,1920]{1,0:T(8,128)(2,1)S(1)} %get-tuple-element.270), channel_id=1, source_target_pairs={{0,2},{1,3},{2,0},{3,1},{4,6},{5,7},{6,4},{7,5},{8,10},{9,11},{10,... | collective-permute-start | bytes 368648 | tf_op jit(solution)/shard_map/ppermute | solution.py:290
  248.9 11.6 %collective-permute-start.81 = (bf16[32,1920]{1,0:T(8,128)(2,1)S(1)}, bf16[32,1920]{1,0:T(8,128)(2,1)S(1)}, u32[]{:S(2)}, u32[]{:S(2)}) collective-permute-start(bf16[32,1920]{1,0:T(8,128)(2,1)S(1)} %get-tuple-element.271), channel_id=1, source_target_pairs={{0,4},{1,5},{2,6},{3,7},{4,0},{5,1},{6,2},{7,3},{8,12},{9,13},{10,... | collective-permute-start | bytes 368648 | tf_op jit(solution)/shard_map/ppermute | solution.py:290
  (24 other events, 105.0 us)
where the time goes:
time: 267 us; the launch traced here: 266 us
  waiting for transfers between devices  107 us (40%)
  starting transfers between devices  95.3 us (36%)
  Pallas kernels  57.2 us (21%)
  local copies, waits for them, and re-layouts  3.59 us (1%)
    ppermute x82, waiting for transfers between devices, permuted(): return lax.ppermute(block, ('pipe', 'expert'), route)  107 us
    ppermute x82, starting transfers between devices, permuted(): return lax.ppermute(block, ('pipe', 'expert'), route)  95.3 us
    pallas_call x10, Pallas kernels, backward(): pl.pallas_call(functools.partial(backward_kernel, plan), out_shape=[piece...  26.5 us
    pallas_call x10, Pallas kernels, forward(): pl.pallas_call(functools.partial(forward_kernel, many, len(earlier)), out...  16.2 us
    pallas_call x7, Pallas kernels, resort(): pl.pallas_call(functools.partial(resort_kernel, (len(arrived), count, wid...  6.08 us
  transfers between devices with their start and end apart: 82, of which 45 were waited for; matrix products, arithmetic and copies ran while one was open for 0% of the time, Pallas kernels for 16%

commit v1 on v0

--- a/solution.py
+++ b/solution.py
@@ -73,11 +73,12 @@
 def forward_kernel(count, chained, gain_ref, column_ref, in_ref, out_ref, *refs):
     arrived, refs = refs[:count], refs[count + chained :]
     sent, refs = refs[:count], refs[count:]
-    hidden_ref, joined_ref, produced_ref = refs
+    hidden_ref, joined_ref, produced_ref, inverse_ref, gate_ref, normed_ref, activated_ref = refs
     inner = out_ref.shape[0]
     hidden = joined_rows(arrived, in_ref.shape[0])
-    normed, _, _ = normalize(hidden, gain_ref[...].astype(f32))
-    share = gate_of(normed, column_ref[...]).astype(bf16).astype(f32)
+    normed, _, inverse = normalize(hidden, gain_ref[...].astype(f32))
+    gate = gate_of(normed, column_ref[...])
+    share = gate.astype(bf16).astype(f32)
     joined = jnp.dot(normed, in_ref[...], preferred_element_type=f32)
     gate_part = joined[:, :inner]
     activated = (gate_part * jax.nn.sigmoid(gate_part) * joined[:, inner:]).astype(bf16)
@@ -87,10 +88,14 @@
     hidden_ref[...] = hidden
     joined_ref[...] = joined
     produced_ref[...] = produced
+    inverse_ref[...] = inverse
+    gate_ref[...] = gate
+    normed_ref[...] = normed
+    activated_ref[...] = activated
 
 
 def backward_kernel(plan, place_ref, gain_ref, column_ref, in_ref, out_ref, *refs):
-    count, layers, micros, sets, enters, first, chained, aliased, passes = plan
+    count, layers, _, sets, enters, first, chained, passes = plan
     last = layers - 1
     layer, step = place_ref[0], place_ref[2]
     refs = list(refs)
@@ -98,14 +103,10 @@
     arrived = take(count)
     entered = take(count) if enters else None
     ahead = take(count) if first else None
-    saved = [take(3) for _ in range(sets)]
+    saved = [take(5) for _ in range(sets)]
     take(chained)
-    if aliased:
-        take(4)
     sent = take(count) if passes else None
-    kept = take(4)
-    stage = take(4)
-    sems = refs.pop(0)
+    joined_grad_ref, scaled_grad_ref = refs
     width = out_ref.shape[0]
     upstream = joined_rows(arrived, width)
     if entered is not None:
@@ -119,40 +120,56 @@
             value = jnp.where(micro == 1, group[index][...], value)
         return value
 
-    hidden, joined, produced = pick(0), pick(1), pick(2)
-    slot = jnp.where((micro >= 0) & (micro < micros), micro, micros)
-    copies = [
-        pltpu.make_async_copy(stage[i], kept[i].at[slot], sems.at[i]) for i in range(4)
-    ]
+    joined, inverse, gate = pick(1), pick(3), pick(4)
     inner = out_ref.shape[1]
-    gain, column = gain_ref[...].astype(f32), column_ref[...]
-    normed, scaled, inverse = normalize(hidden, gain)
-    gate = gate_of(normed, column)
     gate_part, up_part = joined[:, :inner], joined[:, inner:]
     sigmoid_gate = jax.nn.sigmoid(gate_part)
     silu_gate = gate_part * sigmoid_gate
     scaled_grad = (gate.astype(bf16).astype(f32) * upstream_f).astype(bf16)
-    stage[0][...] = normed
-    stage[2][...] = (silu_gate * up_part).astype(bf16)
-    stage[3][...] = scaled_grad
-    for i in (0, 2, 3):
-        copies[i].start()
+    scaled_grad_ref[...] = scaled_grad
     act_grad = jnp.dot(scaled_grad, out_ref[...], preferred_element_type=f32)
     gate_grad = act_grad * up_part * sigmoid_gate * (1.0 + gate_part * (1.0 - sigmoid_gate))
     up_grad = act_grad * silu_gate
     joined_grad = jnp.concatenate([gate_grad, up_grad], axis=-1).astype(bf16)
-    stage[1][...] = joined_grad
-    copies[1].start()
+    joined_grad_ref[...] = joined_grad
     if passes:
         rows_grad = jnp.dot(joined_grad, in_ref[...], preferred_element_type=f32).astype(bf16)
-        share_grad = jnp.sum(produced.astype(f32) * upstream_f, axis=-1, keepdims=True)
+        share_grad = jnp.sum(pick(2).astype(f32) * upstream_f, axis=-1, keepdims=True)
         logit_grad = share_grad.astype(bf16).astype(f32) * gate * (1.0 - gate)
-        gained = (rows_grad.astype(f32) + logit_grad * column) * gain
+        gained = (rows_grad.astype(f32) + logit_grad * column_ref[...]) * gain_ref[...].astype(f32)
+        scaled = pick(0).astype(f32) * inverse
         centred = gained - scaled * jnp.mean(gained * scaled, axis=-1, keepdims=True)
         passed = (upstream_f + inverse * centred).astype(bf16)
         split_rows(sent, passed, layer == last, ahead)
-    for copy in copies:
-        copy.wait()
+
+
+def record_kernel(plan, place_ref, *refs):
+    layers, micros, sets, aliased = plan
+    refs = list(refs)
+    take = lambda number: [refs.pop(0) for _ in range(number)]
+    grads = take(2)
+    saved = [take(2) for _ in range(sets)]
+    take(4 * aliased)
+    kept = take(4)
+    sems = refs.pop(0)
+    micro = place_ref[2] - (2 * (layers - 1) - place_ref[0])
+    slot = jnp.where((micro >= 0) & (micro < micros), micro, micros)
+
+    def copy_all(chosen):
+        sources = (chosen[0], grads[0], chosen[1], grads[1])
+        copies = [
+            pltpu.make_async_copy(sources[i], kept[i].at[slot], sems.at[i]) for i in range(4)
+        ]
+        for copy in copies:
+            copy.start()
+        for copy in copies:
+            copy.wait()
+
+    if sets == 1:
+        copy_all(saved[0])
+    else:
+        pl.when(micro != 1)(lambda: copy_all(saved[0]))
+        pl.when(micro == 1)(lambda: copy_all(saved[1]))
 
 
 def resort_kernel(plan, place_ref, order_ref, *refs):
@@ -232,12 +249,21 @@
     out_turned[...] = out_ref[...].T
 
 
-def grads_kernel(parts, *refs):
-    in_ref, out_ref = refs[4 * parts :]
+def grads_kernel(parts, place_ref, *refs):
+    in_ref, out_ref = refs[8 * parts :]
+    first = place_ref[0] == 0
 
     def gathered(which):
-        groups = [refs[4 * part + which] for part in range(parts)]
-        return jnp.concatenate([g[m] for g in groups for m in range(g.shape[0])], axis=0)
+        blocks = []
+        for part in range(parts):
+            ref = refs[8 * part + which]
+            micros = ref.shape[0]
+            for m in range(micros):
+                block = ref[m]
+                if m == micros - 1:
+                    block = jnp.where(first, refs[8 * part + which + 4][...], block)
+                blocks.append(block)
+        return jnp.concatenate(blocks, axis=0)
 
     in_ref[...] = lax.dot_general(
         gathered(0), gathered(1), FIRST, preferred_element_type=f32
@@ -359,22 +385,59 @@
 
     def forward(arrived, earlier):
         many = len(arrived)
+        form = lambda length, dtype: jax.ShapeDtypeStruct((many * size, length), dtype)
         out = pl.pallas_call(
             functools.partial(forward_kernel, many, len(earlier)),
             out_shape=[piece] * many
             + [
-                jax.ShapeDtypeStruct((many * size, width), bf16),
-                jax.ShapeDtypeStruct((many * size, double), f32),
-                jax.ShapeDtypeStruct((many * size, width), bf16),
+                form(width, bf16),
+                form(double, f32),
+                form(width, bf16),
+                form(1, f32),
+                form(1, f32),
+                form(width, bf16),
+                form(inner, bf16),
             ],
             in_specs=[VMEM] * (4 + many) + [ANY] * len(earlier),
-            out_specs=[VMEM] * (many + 3),
+            out_specs=[VMEM] * (many + 7),
             compiler_params=params,
             name="forward",
         )(gain_row, column, own_in, own_out, *arrived, *earlier)
         return out[:many], out[many:]
 
-    kept_sizes = (width, double, inner, width)
+    def record(step, grads, saved, kept):
+        sources = sources_of(step, saved)
+        operands = [places[step], *grads]
+        for group in sources:
+            operands += group[5:]
+        specs = [SMEM] + [ANY] * (len(operands) - 1)
+        aliases = {}
+        if kept is not None:
+            aliases = {len(operands) + i: i for i in range(4)}
+            operands += kept
+            specs += [ANY] * 4
+        depth = grads[0].shape[0]
+        return pl.pallas_call(
+            functools.partial(record_kernel, (layers, micros, len(sources), kept is not None)),
+            out_shape=[
+                jax.ShapeDtypeStruct((micros + 1, depth, length), bf16)
+                for length in (width, double, inner, width)
+            ],
+            in_specs=specs,
+            out_specs=[ANY] * 4,
+            scratch_shapes=[pltpu.SemaphoreType.DMA((4,))],
+            input_output_aliases=aliases,
+            compiler_params=params,
+            name="record",
+        )(*operands)
+
+    def sources_of(step, saved):
+        return [
+            saved[step - 2 * (last - p)]
+            for p in range(layers)
+            if 0 <= step - (2 * last - p) < micros
+        ]
+
     bands = 8
     turned_in, turned_out = pl.pallas_call(
         transpose_kernel,
@@ -395,14 +458,10 @@
         name="turn",
     )(own_in, own_out)
 
-    def backward(step, arrived, entered, ahead, saved, kept, earlier):
+    def backward(step, arrived, entered, ahead, saved, earlier):
         passes = step + 1 < steps
         many = len(arrived)
-        sources = [
-            saved[step - 2 * (last - p)]
-            for p in range(layers)
-            if 0 <= step - (2 * last - p) < micros
-        ]
+        sources = sources_of(step, saved)
         plan = (
             many,
             layers,
@@ -411,7 +470,6 @@
             entered is not None,
             step == last,
             len(earlier),
-            kept is not None,
             passes,
         )
         operands = [places[step], gain_row, column, turned_in, turned_out, *arrived]
@@ -420,25 +478,18 @@
         if step == last:
             operands += ahead
         for group in sources:
-            operands += group
+            operands += group[:5]
         specs = [SMEM] + [VMEM] * (len(operands) - 1) + [ANY] * len(earlier)
         operands += earlier
         sent = many if passes else 0
-        aliases = {}
-        if kept is not None:
-            aliases = {len(operands) + i: sent + i for i in range(4)}
-            operands += kept
-            specs += [ANY] * 4
-        held = [(many * size, length) for length in kept_sizes]
         out = pl.pallas_call(
             functools.partial(backward_kernel, plan),
             out_shape=[piece] * sent
-            + [jax.ShapeDtypeStruct((micros + 1, *shape), bf16) for shape in held],
+            + [
+                jax.ShapeDtypeStruct((many * size, length), bf16) for length in (double, width)
+            ],
             in_specs=specs,
-            out_specs=[VMEM] * sent + [ANY] * 4,
-            scratch_shapes=[pltpu.VMEM(shape, bf16) for shape in held]
-            + [pltpu.SemaphoreType.DMA((4,))],
-            input_output_aliases=aliases,
+            out_specs=[VMEM] * (sent + 2),
             compiler_params=params,
             name="backward",
         )(*operands)
@@ -447,6 +498,7 @@
     arrivals = []
     forwards = [[] for _ in parts]
     kept = [None for _ in parts]
+    grads = [None for _ in parts]
     for step in range(steps):
         arrived = to_experts(pieces)
         arrivals.append(arrived)
@@ -461,9 +513,13 @@
                 entered = None
                 if step < last + micros:
                     entered = [arrivals[step - last][k] for k in part]
-                passed, kept[index] = backward(
-                    step, here, entered, passed, forwards[index], kept[index], earlier
+                passed, grads[index] = backward(
+                    step, here, entered, passed, forwards[index], earlier
                 )
+                if step + 1 < steps:
+                    kept[index] = record(
+                        step, grads[index], forwards[index], kept[index]
+                    )
             for k, value in zip(part, passed):
                 pieces[k] = value
             earlier = passed[:1]
@@ -488,7 +544,15 @@
             whole_block(double),
             column_block(inner // cuts),
             whole_block(width),
+            pl.BlockSpec((depth, width // cuts), lambda i: (0, i)),
+            pl.BlockSpec((depth, double), lambda i: (0, 0)),
+            pl.BlockSpec((depth, inner // cuts), lambda i: (0, i)),
+            pl.BlockSpec((depth, width), lambda i: (0, 0)),
         ]
+    final = []
+    for group, pair, saved in zip(kept, grads, forwards):
+        normed, activated = saved[steps - 1 - 2 * last][5:]
+        final += [*group, normed, pair[0], activated, pair[1]]
     grad_in, grad_out = pl.pallas_call(
         functools.partial(grads_kernel, len(parts)),
         grid=(cuts,),
@@ -496,14 +560,14 @@
             jax.ShapeDtypeStruct((width, double), bf16),
             jax.ShapeDtypeStruct((inner, width), bf16),
         ],
-        in_specs=specs,
+        in_specs=[SMEM] + specs,
         out_specs=[
             pl.BlockSpec((width // cuts, double), lambda i: (i, 0)),
             pl.BlockSpec((inner // cuts, width), lambda i: (i, 0)),
         ],
         compiler_params=params,
         name="grads",
-    )(*[buffer for group in kept for buffer in group])
+    )(places[0], *final)
     return grad_in[None, None], grad_out[None, None]
 
 

time: 267 us -> 263 us (0.985)
    pallas_call x0 -> x8, Pallas kernels: none -> 7.1 us  [record(): pl.pallas_call(functools.partial(record_kernel, (layers, micros, len(sour...]
    pallas_call x10, Pallas kernels: 26.5 us -> 19.6 us  [backward(): pl.pallas_call(functools.partial(backward_kernel, plan), out_shape=[piece...]
  transfers between devices with their start and end apart: 82 -> 82, of which waited for: 45 -> 57; matrix products, arithmetic and copies ran while one was open for 0% -> 0% of each run, Pallas kernels for 16% -> 11%
where the time goes in v1:
time: 263 us
  waiting for transfers between devices  105 us (40%)
  starting transfers between devices  93.4 us (36%)
  Pallas kernels  58.2 us (22%)
  local copies, waits for them, and re-layouts  3.59 us (1%)
    ppermute x82, waiting for transfers between devices, permuted(): return lax.ppermute(block, ('pipe', 'expert'), route)  105 us
    ppermute x82, starting transfers between devices, permuted(): return lax.ppermute(block, ('pipe', 'expert'), route)  93.4 us
    pallas_call x10, Pallas kernels, backward(): pl.pallas_call(functools.partial(backward_kernel, plan), out_shape=[piece...  19.6 us
    pallas_call x10, Pallas kernels, forward(): pl.pallas_call(functools.partial(forward_kernel, many, len(earlier)), out...  16.4 us
    pallas_call x8, Pallas kernels, record(): pl.pallas_call(functools.partial(record_kernel, (layers, micros, len(sour...  7.1 us
    pallas_call x7, Pallas kernels, resort(): pl.pallas_call(functools.partial(resort_kernel, (len(arrived), count, wid...  6.08 us
  transfers between devices with their start and end apart: 82, of which 57 were waited for; matrix products, arithmetic and copies ran while one was open for 0% of the time, Pallas kernels for 11%

profile of v1, /device:TPU:0, one launch (start us, length us, event | category | flops | bytes accessed | tf_op | source)
XLA Modules:
  0.0 263.0 jit_solution(14684858624892505480)
XLA Ops:
  5.0 1.5 prepare.1
  6.5 5.0 %collective-permute-start.2 = (bf16[32,1920]{1,0:T(8,128)(2,1)S(1)}, bf16[32,1920]{1,0:T(8,128)(2,1)S(1)}, u32[]{:S(2)}, u32[]{:S(2)}) collective-permute-start(bf16[32,1920]{1,0:T(8,128)(2,1)S(1)} %get-tuple-element.198), channel_id=1, source_target_pairs={{0,6},{1,7},{2,4},{3,5},{4,2},{5,3},{6,0},{7,1},{8,14},{9,15},{10,... | collective-permute-start | bytes 368648 | tf_op jit(solution)/shard_map/ppermute | solution.py:316
  12.9 2.8 %collective-permute-done.2.refs_1_.refs_3_ = bf16[32,1920]{1,0:T(8,128)(2,1)S(1)} collective-permute-done((bf16[32,1920]{1,0:T(8,128)(2,1)S(1)}, bf16[32,1920]{1,0:T(8,128)(2,1)S(1)}, u32[]{:S(2)}, u32[]{:S(2)}) %collective-permute-start.2) | collective-permute-done | bytes 122912 | tf_op jit(solution)/shard_map/ppermute | solution.py:316
  15.8 2.2 copy-done
  20.2 2.0 collective-permute-done.5.refs_1_.refs_3_
  23.7 2.3 collective-permute-start.6
  26.0 2.7 %collective-permute-start.7 = (bf16[32,1920]{1,0:T(8,128)(2,1)S(1)}, bf16[32,1920]{1,0:T(8,128)(2,1)S(1)}, u32[]{:S(2)}, u32[]{:S(2)}) collective-permute-start(bf16[32,1920]{1,0:T(8,128)(2,1)S(1)} %get-tuple-element.203), channel_id=1, source_target_pairs={{0,12},{1,13},{2,14},{3,15},{4,8},{5,9},{6,10},{7,11},{8,20},{9,21... | collective-permute-start | bytes 368648 | tf_op jit(solution)/shard_map/ppermute | solution.py:316
  31.5 7.8 %collective-permute-done.7.refs_2_ = bf16[32,1920]{1,0:T(8,128)(2,1)S(1)} collective-permute-done((bf16[32,1920]{1,0:T(8,128)(2,1)S(1)}, bf16[32,1920]{1,0:T(8,128)(2,1)S(1)}, u32[]{:S(2)}, u32[]{:S(2)}) %collective-permute-start.7) | collective-permute-done | bytes 122912 | tf_op jit(solution)/shard_map/ppermute | solution.py:316
  43.9 2.6 collective-permute-start.16
  46.4 3.7 %collective-permute-done.13.refs_1_.refs_3_ = bf16[32,1920]{1,0:T(8,128)(2,1)S(1)} collective-permute-done((bf16[32,1920]{1,0:T(8,128)(2,1)S(1)}, bf16[32,1920]{1,0:T(8,128)(2,1)S(1)}, u32[]{:S(2)}, u32[]{:S(2)}) %collective-permute-start.13) | collective-permute-done | bytes 122912 | tf_op jit(solution)/shard_map/ppermute | solution.py:316
  51.8 4.4 %collective-permute-done.16.refs_1_.refs_3_ = bf16[32,1920]{1,0:T(8,128)(2,1)S(1)} collective-permute-done((bf16[32,1920]{1,0:T(8,128)(2,1)S(1)}, bf16[32,1920]{1,0:T(8,128)(2,1)S(1)}, u32[]{:S(2)}, u32[]{:S(2)}) %collective-permute-start.16) | collective-permute-done | bytes 122912 | tf_op jit(solution)/shard_map/ppermute | solution.py:316
  57.7 3.8 %collective-permute-start.18 = (bf16[32,1920]{1,0:T(8,128)(2,1)S(1)}, bf16[32,1920]{1,0:T(8,128)(2,1)S(1)}, u32[]{:S(2)}, u32[]{:S(2)}) collective-permute-start(bf16[32,1920]{1,0:T(8,128)(2,1)S(1)} %get-tuple-element.212), channel_id=1, source_target_pairs={{0,12},{1,13},{2,14},{3,15},{4,8},{5,9},{6,10},{7,11},{8,20},{9,21... | collective-permute-start | bytes 368648 | tf_op jit(solution)/shard_map/ppermute | solution.py:316
  61.5 3.9 %collective-permute-start.19 = (bf16[32,1920]{1,0:T(8,128)(2,1)S(1)}, bf16[32,1920]{1,0:T(8,128)(2,1)S(1)}, u32[]{:S(2)}, u32[]{:S(2)}) collective-permute-start(bf16[32,1920]{1,0:T(8,128)(2,1)S(1)} %get-tuple-element.213), channel_id=1, source_target_pairs={{0,14},{1,15},{2,12},{3,13},{4,10},{5,11},{6,8},{7,9},{8,22},{9,23... | collective-permute-start | bytes 368648 | tf_op jit(solution)/shard_map/ppermute | solution.py:316
  65.8 5.8 %collective-permute-done.18.refs_2_ = bf16[32,1920]{1,0:T(8,128)(2,1)S(1)} collective-permute-done((bf16[32,1920]{1,0:T(8,128)(2,1)S(1)}, bf16[32,1920]{1,0:T(8,128)(2,1)S(1)}, u32[]{:S(2)}, u32[]{:S(2)}) %collective-permute-start.18) | collective-permute-done | bytes 122912 | tf_op jit(solution)/shard_map/ppermute | solution.py:316
  76.3 2.5 collective-permute-start.27
  78.8 3.7 %collective-permute-done.24.refs_1_ = bf16[32,1920]{1,0:T(8,128)(2,1)S(1)} collective-permute-done((bf16[32,1920]{1,0:T(8,128)(2,1)S(1)}, bf16[32,1920]{1,0:T(8,128)(2,1)S(1)}, u32[]{:S(2)}, u32[]{:S(2)}) %collective-permute-start.24) | collective-permute-done | bytes 122912 | tf_op jit(solution)/shard_map/ppermute | solution.py:316
  84.6 3.8 %collective-permute-done.27.refs_1_ = bf16[32,1920]{1,0:T(8,128)(2,1)S(1)} collective-permute-done((bf16[32,1920]{1,0:T(8,128)(2,1)S(1)}, bf16[32,1920]{1,0:T(8,128)(2,1)S(1)}, u32[]{:S(2)}, u32[]{:S(2)}) %collective-permute-start.27) | collective-permute-done | bytes 122912 | tf_op jit(solution)/shard_map/ppermute | solution.py:316
  90.1 3.8 %collective-permute-start.29 = (bf16[32,1920]{1,0:T(8,128)(2,1)S(1)}, bf16[32,1920]{1,0:T(8,128)(2,1)S(1)}, u32[]{:S(2)}, u32[]{:S(2)}) collective-permute-start(bf16[32,1920]{1,0:T(8,128)(2,1)S(1)} %get-tuple-element.220), channel_id=1, source_target_pairs={{0,12},{1,13},{2,14},{3,15},{4,8},{5,9},{6,10},{7,11},{8,20},{9,21... | collective-permute-start | bytes 368648 | tf_op jit(solution)/shard_map/ppermute | solution.py:316
  94.2 3.5 %collective-permute-start.30 = (bf16[32,1920]{1,0:T(8,128)(2,1)S(1)}, bf16[32,1920]{1,0:T(8,128)(2,1)S(1)}, u32[]{:S(2)}, u32[]{:S(2)}) collective-permute-start(bf16[32,1920]{1,0:T(8,128)(2,1)S(1)} %get-tuple-element.221), channel_id=1, source_target_pairs={{0,14},{1,15},{2,12},{3,13},{4,10},{5,11},{6,8},{7,9},{8,22},{9,23... | collective-permute-start | bytes 368648 | tf_op jit(solution)/shard_map/ppermute | solution.py:316
  98.1 5.8 %collective-permute-done.29.refs_2_ = bf16[32,1920]{1,0:T(8,128)(2,1)S(1)} collective-permute-done((bf16[32,1920]{1,0:T(8,128)(2,1)S(1)}, bf16[32,1920]{1,0:T(8,128)(2,1)S(1)}, u32[]{:S(2)}, u32[]{:S(2)}) %collective-permute-start.29) | collective-permute-done | bytes 122912 | tf_op jit(solution)/shard_map/ppermute | solution.py:316
  106.6 1.6 collective-permute-start.35
  109.0 2.1 collective-permute-start.38
  111.1 2.9 %turn.1 = (bf16[1024,2048]{1,0:T(8,128)(2,1)S(1)}, bf16[2048,512]{1,0:T(8,128)(2,1)S(1)}) custom-call(bf16[2048,1024]{1,0:T(8,128)(2,1)S(1)} %bitcast.17, bf16[512,2048]{1,0:T(8,128)(2,1)S(1)} %bitcast.28), custom_call_target="tpu_custom_call" | custom-call | tf_op jit(solution)/shard_map/turn/pallas_call | solution.py:442
  116.3 2.2 backward.10
  118.5 2.3 collective-permute-done.38.refs_1_
  122.3 2.2 backward.11
  125.2 2.7 %collective-permute-start.40 = (bf16[32,1920]{1,0:T(8,128)(2,1)S(1)}, bf16[32,1920]{1,0:T(8,128)(2,1)S(1)}, u32[]{:S(2)}, u32[]{:S(2)}) collective-permute-start(bf16[32,1920]{1,0:T(8,128)(2,1)S(1)} %get-tuple-element.242), channel_id=1, source_target_pairs={{0,12},{1,13},{2,14},{3,15},{4,8},{5,9},{6,10},{7,11},{8,4},{9,5},... | collective-permute-start | bytes 368648 | tf_op jit(solution)/shard_map/ppermute | solution.py:316
  128.7 2.7 %collective-permute-start.41 = (bf16[32,1920]{1,0:T(8,128)(2,1)S(1)}, bf16[32,1920]{1,0:T(8,128)(2,1)S(1)}, u32[]{:S(2)}, u32[]{:S(2)}) collective-permute-start(bf16[32,1920]{1,0:T(8,128)(2,1)S(1)} %get-tuple-element.243), channel_id=1, source_target_pairs={{0,14},{1,15},{2,12},{3,13},{4,10},{5,11},{6,8},{7,9},{8,6},{9,7},... | collective-permute-start | bytes 368648 | tf_op jit(solution)/shard_map/ppermute | solution.py:316
  131.7 6.0 %collective-permute-done.40.refs_2_ = bf16[32,1920]{1,0:T(8,128)(2,1)S(1)} collective-permute-done((bf16[32,1920]{1,0:T(8,128)(2,1)S(1)}, bf16[32,1920]{1,0:T(8,128)(2,1)S(1)}, u32[]{:S(2)}, u32[]{:S(2)}) %collective-permute-start.40) | collective-permute-done | bytes 122912 | tf_op jit(solution)/shard_map/ppermute | solution.py:316
  140.5 2.3 collective-permute-start.46
  143.3 1.6 collective-permute-start.49
  145.0 3.6 %collective-permute-done.46.refs_1_ = bf16[32,1920]{1,0:T(8,128)(2,1)S(1)} collective-permute-done((bf16[32,1920]{1,0:T(8,128)(2,1)S(1)}, bf16[32,1920]{1,0:T(8,128)(2,1)S(1)}, u32[]{:S(2)}, u32[]{:S(2)}) %collective-permute-start.46) | collective-permute-done | bytes 122912 | tf_op jit(solution)/shard_map/ppermute | solution.py:316
  148.6 2.2 forward.18
  150.8 2.2 backward.12
  153.0 1.6 collective-permute-done.49.refs_1_
  154.6 2.2 forward.19
  156.8 2.2 backward.13
  159.0 2.2 collective-permute-start.50
  161.2 1.5 collective-permute-start.51
  162.7 1.8 collective-permute-start.47
  164.6 2.2 collective-permute-start.52
  166.7 6.6 %collective-permute-done.51.refs_2_ = bf16[32,1920]{1,0:T(8,128)(2,1)S(1)} collective-permute-done((bf16[32,1920]{1,0:T(8,128)(2,1)S(1)}, bf16[32,1920]{1,0:T(8,128)(2,1)S(1)}, u32[]{:S(2)}, u32[]{:S(2)}) %collective-permute-start.51) | collective-permute-done | bytes 122912 | tf_op jit(solution)/shard_map/ppermute | solution.py:316
  176.0 2.3 collective-permute-start.57
  178.8 1.7 collective-permute-start.60
  180.5 3.6 %collective-permute-done.57.refs_1_ = bf16[32,1920]{1,0:T(8,128)(2,1)S(1)} collective-permute-done((bf16[32,1920]{1,0:T(8,128)(2,1)S(1)}, bf16[32,1920]{1,0:T(8,128)(2,1)S(1)}, u32[]{:S(2)}, u32[]{:S(2)}) %collective-permute-start.57) | collective-permute-done | bytes 122912 | tf_op jit(solution)/shard_map/ppermute | solution.py:316
  184.1 2.2 backward.14
  187.2 3.0 %collective-permute-done.60.refs_1_ = bf16[32,1920]{1,0:T(8,128)(2,1)S(1)} collective-permute-done((bf16[32,1920]{1,0:T(8,128)(2,1)S(1)}, bf16[32,1920]{1,0:T(8,128)(2,1)S(1)}, u32[]{:S(2)}, u32[]{:S(2)}) %collective-permute-start.60) | collective-permute-done | bytes 122912 | tf_op jit(solution)/shard_map/ppermute | solution.py:316
  190.2 2.2 backward.15
  193.4 2.7 %collective-permute-start.62 = (bf16[32,1920]{1,0:T(8,128)(2,1)S(1)}, bf16[32,1920]{1,0:T(8,128)(2,1)S(1)}, u32[]{:S(2)}, u32[]{:S(2)}) collective-permute-start(bf16[32,1920]{1,0:T(8,128)(2,1)S(1)} %get-tuple-element.288), channel_id=1, source_target_pairs={{0,28},{1,29},{2,30},{3,31},{4,24},{5,25},{6,26},{7,27},{8,4},{9,5... | collective-permute-start | bytes 368648 | tf_op jit(solution)/shard_map/ppermute | solution.py:316
  196.1 2.8 %collective-permute-start.58 = (bf16[32,1920]{1,0:T(8,128)(2,1)S(1)}, bf16[32,1920]{1,0:T(8,128)(2,1)S(1)}, u32[]{:S(2)}, u32[]{:S(2)}) collective-permute-start(bf16[32,1920]{1,0:T(8,128)(2,1)S(1)} %get-tuple-element.279.refs_12_), channel_id=1, source_target_pairs={{0,24},{1,25},{2,26},{3,27},{4,28},{5,29},{6,30},{7,31},{8,0},{9,1... | collective-permute-start | bytes 368648 | tf_op jit(solution)/shard_map/ppermute | solution.py:316
  200.1 4.8 %collective-permute-done.62.refs_2_ = bf16[32,1920]{1,0:T(8,128)(2,1)S(1)} collective-permute-done((bf16[32,1920]{1,0:T(8,128)(2,1)S(1)}, bf16[32,1920]{1,0:T(8,128)(2,1)S(1)}, u32[]{:S(2)}, u32[]{:S(2)}) %collective-permute-start.62) | collective-permute-done | bytes 122912 | tf_op jit(solution)/shard_map/ppermute | solution.py:316
  208.8 2.4 collective-permute-start.68
  211.8 1.5 collective-permute-start.71
  213.3 3.6 %collective-permute-done.68.refs_1_ = bf16[32,1920]{1,0:T(8,128)(2,1)S(1)} collective-permute-done((bf16[32,1920]{1,0:T(8,128)(2,1)S(1)}, bf16[32,1920]{1,0:T(8,128)(2,1)S(1)}, u32[]{:S(2)}, u32[]{:S(2)}) %collective-permute-start.68) | collective-permute-done | bytes 122912 | tf_op jit(solution)/shard_map/ppermute | solution.py:316
  216.9 2.2 backward.16
  219.2 4.3 %collective-permute-done.71.refs_1_ = bf16[32,1920]{1,0:T(8,128)(2,1)S(1)} collective-permute-done((bf16[32,1920]{1,0:T(8,128)(2,1)S(1)}, bf16[32,1920]{1,0:T(8,128)(2,1)S(1)}, u32[]{:S(2)}, u32[]{:S(2)}) %collective-permute-start.71) | collective-permute-done | bytes 122912 | tf_op jit(solution)/shard_map/ppermute | solution.py:316
  223.6 2.2 backward.17
  226.6 3.3 %collective-permute-start.73 = (bf16[32,1920]{1,0:T(8,128)(2,1)S(1)}, bf16[32,1920]{1,0:T(8,128)(2,1)S(1)}, u32[]{:S(2)}, u32[]{:S(2)}) collective-permute-start(bf16[32,1920]{1,0:T(8,128)(2,1)S(1)} %get-tuple-element.340), channel_id=1, source_target_pairs={{0,28},{1,29},{2,30},{3,31},{4,24},{5,25},{6,26},{7,27},{8,4},{9,5... | collective-permute-start | bytes 368648 | tf_op jit(solution)/shard_map/ppermute | solution.py:316
  229.8 2.1 collective-permute-start.69
  233.4 4.7 %collective-permute-done.73.refs_2_ = bf16[32,1920]{1,0:T(8,128)(2,1)S(1)} collective-permute-done((bf16[32,1920]{1,0:T(8,128)(2,1)S(1)}, bf16[32,1920]{1,0:T(8,128)(2,1)S(1)}, u32[]{:S(2)}, u32[]{:S(2)}) %collective-permute-start.73) | collective-permute-done | bytes 122912 | tf_op jit(solution)/shard_map/ppermute | solution.py:316
  241.8 2.2 collective-permute-start.80
  244.8 1.6 collective-permute-start.79
  253.6 2.6 collective-permute-done.81.refs_1_
  258.4 4.6 %grads.1 = (bf16[2048,1024]{1,0:T(8,128)(2,1)}, bf16[512,2048]{1,0:T(8,128)(2,1)}) custom-call(s32[3]{0:T(128)S(1)} %get-tuple-element.394.place_ref, bf16[3,64,2048]{2,1,0:T(8,128)(2,1)S(1)} %get-tuple-element.327.refs_0_, bf16[3,64,1024]{2,1,0:T(8,128)(2,1)S(1)} %get-tuple-element.328.refs_1_, bf16[3,64,512]{2,1,0:T(8,128)(2,1)S(1)} %get-tuple-element.329.refs_2_, ...), custom_call_target="tpu_custom_call" | custom-call | tf_op jit(solution)/shard_map/grads/pallas_call | solution.py:556
  (154 shorter events, 68.8 us)
Async XLA Ops:
  2.0 2.3 collective-permute-start.1
  2.5 1.7 collective-permute-start
  6.5 9.2 %collective-permute-start.2 = (bf16[32,1920]{1,0:T(8,128)(2,1)S(1)}, bf16[32,1920]{1,0:T(8,128)(2,1)S(1)}, u32[]{:S(2)}, u32[]{:S(2)}) collective-permute-start(bf16[32,1920]{1,0:T(8,128)(2,1)S(1)} %get-tuple-element.198), channel_id=1, source_target_pairs={{0,6},{1,7},{2,4},{3,5},{4,2},{5,3},{6,0},{7,1},{8,14},{9,15},{10,... | collective-permute-start | bytes 368648 | tf_op jit(solution)/shard_map/ppermute | solution.py:316
  11.5 8.6 %collective-permute-start.4 = (bf16[32,1920]{1,0:T(8,128)(2,1)S(1)}, bf16[32,1920]{1,0:T(8,128)(2,1)S(1)}, u32[]{:S(2)}, u32[]{:S(2)}) collective-permute-start(bf16[32,1920]{1,0:T(8,128)(2,1)S(1)} %get-tuple-element.200), channel_id=1, source_target_pairs={{0,2},{1,3},{2,0},{3,1},{4,6},{5,7},{6,4},{7,5},{8,10},{9,11},{10,... | collective-permute-start | bytes 368648 | tf_op jit(solution)/shard_map/ppermute | solution.py:316
  11.5 10.7 %collective-permute-start.5 = (bf16[32,1920]{1,0:T(8,128)(2,1)S(1)}, bf16[32,1920]{1,0:T(8,128)(2,1)S(1)}, u32[]{:S(2)}, u32[]{:S(2)}) collective-permute-start(bf16[32,1920]{1,0:T(8,128)(2,1)S(1)} %get-tuple-element.201), channel_id=1, source_target_pairs={{0,4},{1,5},{2,6},{3,7},{4,0},{5,1},{6,2},{7,3},{8,12},{9,13},{10,... | collective-permute-start | bytes 368648 | tf_op jit(solution)/shard_map/ppermute | solution.py:316
  23.7 7.8 %collective-permute-start.6 = (bf16[32,1920]{1,0:T(8,128)(2,1)S(1)}, bf16[32,1920]{1,0:T(8,128)(2,1)S(1)}, u32[]{:S(2)}, u32[]{:S(2)}) collective-permute-start(bf16[32,1920]{1,0:T(8,128)(2,1)S(1)} %get-tuple-element.202), channel_id=1, source_target_pairs={{0,10},{1,11},{2,8},{3,9},{4,14},{5,15},{6,12},{7,13},{8,18},{9,19... | collective-permute-start | bytes 368648 | tf_op jit(solution)/shard_map/ppermute | solution.py:316
  26.0 13.3 %collective-permute-start.7 = (bf16[32,1920]{1,0:T(8,128)(2,1)S(1)}, bf16[32,1920]{1,0:T(8,128)(2,1)S(1)}, u32[]{:S(2)}, u32[]{:S(2)}) collective-permute-start(bf16[32,1920]{1,0:T(8,128)(2,1)S(1)} %get-tuple-element.203), channel_id=1, source_target_pairs={{0,12},{1,13},{2,14},{3,15},{4,8},{5,9},{6,10},{7,11},{8,20},{9,21... | collective-permute-start | bytes 368648 | tf_op jit(solution)/shard_map/ppermute | solution.py:316
  28.7 10.6 %collective-permute-start.3 = (bf16[32,1920]{1,0:T(8,128)(2,1)S(1)}, bf16[32,1920]{1,0:T(8,128)(2,1)S(1)}, u32[]{:S(2)}, u32[]{:S(2)}) collective-permute-start(bf16[32,1920]{1,0:T(8,128)(2,1)S(1)} %get-tuple-element.199.refs_2_), channel_id=1, source_target_pairs={{0,8},{1,9},{2,10},{3,11},{4,12},{5,13},{6,14},{7,15},{8,16},{9,17... | collective-permute-start | bytes 368648 | tf_op jit(solution)/shard_map/ppermute | solution.py:316
  30.2 9.6 %collective-permute-start.8 = (bf16[32,1920]{1,0:T(8,128)(2,1)S(1)}, bf16[32,1920]{1,0:T(8,128)(2,1)S(1)}, u32[]{:S(2)}, u32[]{:S(2)}) collective-permute-start(bf16[32,1920]{1,0:T(8,128)(2,1)S(1)} %get-tuple-element.204), channel_id=1, source_target_pairs={{0,14},{1,15},{2,12},{3,13},{4,10},{5,11},{6,8},{7,9},{8,22},{9,23... | collective-permute-start | bytes 368648 | tf_op jit(solution)/shard_map/ppermute | solution.py:316
  31.5 8.4 %collective-permute-start.10 = (bf16[32,1920]{1,0:T(8,128)(2,1)S(1)}, bf16[32,1920]{1,0:T(8,128)(2,1)S(1)}, u32[]{:S(2)}, u32[]{:S(2)}) collective-permute-start(bf16[32,1920]{1,0:T(8,128)(2,1)S(1)} %collective-permute-done.6.refs_1_), channel_id=1, source_target_pairs={{0,1},{1,0},{2,3},{3,2},{4,5},{5,4},{6,7},{7,6},{8,9},{9,8},{10,11... | collective-permute-start | bytes 368648 | tf_op jit(solution)/shard_map/ppermute | solution.py:316
  39.3 1.5 collective-permute-start.9
  42.0 8.1 %collective-permute-start.13 = (bf16[32,1920]{1,0:T(8,128)(2,1)S(1)}, bf16[32,1920]{1,0:T(8,128)(2,1)S(1)}, u32[]{:S(2)}, u32[]{:S(2)}) collective-permute-start(bf16[32,1920]{1,0:T(8,128)(2,1)S(1)} %get-tuple-element.207), channel_id=1, source_target_pairs={{0,6},{1,7},{2,4},{3,5},{4,2},{5,3},{6,0},{7,1},{8,14},{9,15},{10,... | collective-permute-start | bytes 368648 | tf_op jit(solution)/shard_map/ppermute | solution.py:316
  43.2 8.6 %collective-permute-start.15 = (bf16[32,1920]{1,0:T(8,128)(2,1)S(1)}, bf16[32,1920]{1,0:T(8,128)(2,1)S(1)}, u32[]{:S(2)}, u32[]{:S(2)}) collective-permute-start(bf16[32,1920]{1,0:T(8,128)(2,1)S(1)} %get-tuple-element.209), channel_id=1, source_target_pairs={{0,2},{1,3},{2,0},{3,1},{4,6},{5,7},{6,4},{7,5},{8,10},{9,11},{10,... | collective-permute-start | bytes 368648 | tf_op jit(solution)/shard_map/ppermute | solution.py:316
  43.9 12.3 %collective-permute-start.16 = (bf16[32,1920]{1,0:T(8,128)(2,1)S(1)}, bf16[32,1920]{1,0:T(8,128)(2,1)S(1)}, u32[]{:S(2)}, u32[]{:S(2)}) collective-permute-start(bf16[32,1920]{1,0:T(8,128)(2,1)S(1)} %get-tuple-element.210), channel_id=1, source_target_pairs={{0,4},{1,5},{2,6},{3,7},{4,0},{5,1},{6,2},{7,3},{8,12},{9,13},{10,... | collective-permute-start | bytes 368648 | tf_op jit(solution)/shard_map/ppermute | solution.py:316
  57.7 8.1 %collective-permute-start.17 = (bf16[32,1920]{1,0:T(8,128)(2,1)S(1)}, bf16[32,1920]{1,0:T(8,128)(2,1)S(1)}, u32[]{:S(2)}, u32[]{:S(2)}) collective-permute-start(bf16[32,1920]{1,0:T(8,128)(2,1)S(1)} %get-tuple-element.211), channel_id=1, source_target_pairs={{0,10},{1,11},{2,8},{3,9},{4,14},{5,15},{6,12},{7,13},{8,18},{9,19... | collective-permute-start | bytes 368648 | tf_op jit(solution)/shard_map/ppermute | solution.py:316
  57.7 13.9 %collective-permute-start.18 = (bf16[32,1920]{1,0:T(8,128)(2,1)S(1)}, bf16[32,1920]{1,0:T(8,128)(2,1)S(1)}, u32[]{:S(2)}, u32[]{:S(2)}) collective-permute-start(bf16[32,1920]{1,0:T(8,128)(2,1)S(1)} %get-tuple-element.212), channel_id=1, source_target_pairs={{0,12},{1,13},{2,14},{3,15},{4,8},{5,9},{6,10},{7,11},{8,20},{9,21... | collective-permute-start | bytes 368648 | tf_op jit(solution)/shard_map/ppermute | solution.py:316
  61.5 10.4 %collective-permute-start.14 = (bf16[32,1920]{1,0:T(8,128)(2,1)S(1)}, bf16[32,1920]{1,0:T(8,128)(2,1)S(1)}, u32[]{:S(2)}, u32[]{:S(2)}) collective-permute-start(bf16[32,1920]{1,0:T(8,128)(2,1)S(1)} %get-tuple-element.208.refs_2_), channel_id=1, source_target_pairs={{0,8},{1,9},{2,10},{3,11},{4,12},{5,13},{6,14},{7,15},{8,16},{9,17... | collective-permute-start | bytes 368648 | tf_op jit(solution)/shard_map/ppermute | solution.py:316
  61.5 10.6 %collective-permute-start.19 = (bf16[32,1920]{1,0:T(8,128)(2,1)S(1)}, bf16[32,1920]{1,0:T(8,128)(2,1)S(1)}, u32[]{:S(2)}, u32[]{:S(2)}) collective-permute-start(bf16[32,1920]{1,0:T(8,128)(2,1)S(1)} %get-tuple-element.213), channel_id=1, source_target_pairs={{0,14},{1,15},{2,12},{3,13},{4,10},{5,11},{6,8},{7,9},{8,22},{9,23... | collective-permute-start | bytes 368648 | tf_op jit(solution)/shard_map/ppermute | solution.py:316
  65.8 6.7 %collective-permute-start.21 = (bf16[32,1920]{1,0:T(8,128)(2,1)S(1)}, bf16[32,1920]{1,0:T(8,128)(2,1)S(1)}, u32[]{:S(2)}, u32[]{:S(2)}) collective-permute-start(bf16[32,1920]{1,0:T(8,128)(2,1)S(1)} %collective-permute-done.17.refs_1_), channel_id=1, source_target_pairs={{0,1},{1,0},{2,3},{3,2},{4,5},{5,4},{6,7},{7,6},{8,9},{9,8},{10,11... | collective-permute-start | bytes 368648 | tf_op jit(solution)/shard_map/ppermute | solution.py:316
  74.3 8.1 %collective-permute-start.24 = (bf16[32,1920]{1,0:T(8,128)(2,1)S(1)}, bf16[32,1920]{1,0:T(8,128)(2,1)S(1)}, u32[]{:S(2)}, u32[]{:S(2)}) collective-permute-start(bf16[32,1920]{1,0:T(8,128)(2,1)S(1)} %get-tuple-element.215), channel_id=1, source_target_pairs={{0,6},{1,7},{2,4},{3,5},{4,2},{5,3},{6,0},{7,1},{8,14},{9,15},{10,... | collective-permute-start | bytes 368648 | tf_op jit(solution)/shard_map/ppermute | solution.py:316
  75.7 8.9 %collective-permute-start.26 = (bf16[32,1920]{1,0:T(8,128)(2,1)S(1)}, bf16[32,1920]{1,0:T(8,128)(2,1)S(1)}, u32[]{:S(2)}, u32[]{:S(2)}) collective-permute-start(bf16[32,1920]{1,0:T(8,128)(2,1)S(1)} %get-tuple-element.217), channel_id=1, source_target_pairs={{0,2},{1,3},{2,0},{3,1},{4,6},{5,7},{6,4},{7,5},{8,10},{9,11},{10,... | collective-permute-start | bytes 368648 | tf_op jit(solution)/shard_map/ppermute | solution.py:316
  76.3 12.2 %collective-permute-start.27 = (bf16[32,1920]{1,0:T(8,128)(2,1)S(1)}, bf16[32,1920]{1,0:T(8,128)(2,1)S(1)}, u32[]{:S(2)}, u32[]{:S(2)}) collective-permute-start(bf16[32,1920]{1,0:T(8,128)(2,1)S(1)} %get-tuple-element.218), channel_id=1, source_target_pairs={{0,4},{1,5},{2,6},{3,7},{4,0},{5,1},{6,2},{7,3},{8,12},{9,13},{10,... | collective-permute-start | bytes 368648 | tf_op jit(solution)/shard_map/ppermute | solution.py:316
  90.0 8.1 %collective-permute-start.28 = (bf16[32,1920]{1,0:T(8,128)(2,1)S(1)}, bf16[32,1920]{1,0:T(8,128)(2,1)S(1)}, u32[]{:S(2)}, u32[]{:S(2)}) collective-permute-start(bf16[32,1920]{1,0:T(8,128)(2,1)S(1)} %get-tuple-element.219), channel_id=1, source_target_pairs={{0,10},{1,11},{2,8},{3,9},{4,14},{5,15},{6,12},{7,13},{8,18},{9,19... | collective-permute-start | bytes 368648 | tf_op jit(solution)/shard_map/ppermute | solution.py:316
  90.1 13.8 %collective-permute-start.29 = (bf16[32,1920]{1,0:T(8,128)(2,1)S(1)}, bf16[32,1920]{1,0:T(8,128)(2,1)S(1)}, u32[]{:S(2)}, u32[]{:S(2)}) collective-permute-start(bf16[32,1920]{1,0:T(8,128)(2,1)S(1)} %get-tuple-element.220), channel_id=1, source_target_pairs={{0,12},{1,13},{2,14},{3,15},{4,8},{5,9},{6,10},{7,11},{8,20},{9,21... | collective-permute-start | bytes 368648 | tf_op jit(solution)/shard_map/ppermute | solution.py:316
  93.8 10.4 %collective-permute-start.25 = (bf16[32,1920]{1,0:T(8,128)(2,1)S(1)}, bf16[32,1920]{1,0:T(8,128)(2,1)S(1)}, u32[]{:S(2)}, u32[]{:S(2)}) collective-permute-start(bf16[32,1920]{1,0:T(8,128)(2,1)S(1)} %get-tuple-element.216.refs_2_), channel_id=1, source_target_pairs={{0,8},{1,9},{2,10},{3,11},{4,12},{5,13},{6,14},{7,15},{8,16},{9,17... | collective-permute-start | bytes 368648 | tf_op jit(solution)/shard_map/ppermute | solution.py:316
  94.2 10.2 %collective-permute-start.30 = (bf16[32,1920]{1,0:T(8,128)(2,1)S(1)}, bf16[32,1920]{1,0:T(8,128)(2,1)S(1)}, u32[]{:S(2)}, u32[]{:S(2)}) collective-permute-start(bf16[32,1920]{1,0:T(8,128)(2,1)S(1)} %get-tuple-element.221), channel_id=1, source_target_pairs={{0,14},{1,15},{2,12},{3,13},{4,10},{5,11},{6,8},{7,9},{8,22},{9,23... | collective-permute-start | bytes 368648 | tf_op jit(solution)/shard_map/ppermute | solution.py:316
  98.1 6.7 %collective-permute-start.32 = (bf16[32,1920]{1,0:T(8,128)(2,1)S(1)}, bf16[32,1920]{1,0:T(8,128)(2,1)S(1)}, u32[]{:S(2)}, u32[]{:S(2)}) collective-permute-start(bf16[32,1920]{1,0:T(8,128)(2,1)S(1)} %collective-permute-done.28.refs_1_), channel_id=1, source_target_pairs={{0,1},{1,0},{2,3},{3,2},{4,5},{5,4},{6,7},{7,6},{8,9},{9,8},{10,11... | collective-permute-start | bytes 368648 | tf_op jit(solution)/shard_map/ppermute | solution.py:316
  106.6 8.1 %collective-permute-start.35 = (bf16[32,1920]{1,0:T(8,128)(2,1)S(1)}, bf16[32,1920]{1,0:T(8,128)(2,1)S(1)}, u32[]{:S(2)}, u32[]{:S(2)}) collective-permute-start(bf16[32,1920]{1,0:T(8,128)(2,1)S(1)} %get-tuple-element.223), channel_id=1, source_target_pairs={{0,6},{1,7},{2,4},{3,5},{4,2},{5,3},{6,0},{7,1},{8,14},{9,15},{10,... | collective-permute-start | bytes 368648 | tf_op jit(solution)/shard_map/ppermute | solution.py:316
  108.3 10.2 %collective-permute-start.37 = (bf16[32,1920]{1,0:T(8,128)(2,1)S(1)}, bf16[32,1920]{1,0:T(8,128)(2,1)S(1)}, u32[]{:S(2)}, u32[]{:S(2)}) collective-permute-start(bf16[32,1920]{1,0:T(8,128)(2,1)S(1)} %get-tuple-element.232), channel_id=1, source_target_pairs={{0,2},{1,3},{2,0},{3,1},{4,6},{5,7},{6,4},{7,5},{8,10},{9,11},{10,... | collective-permute-start | bytes 368648 | tf_op jit(solution)/shard_map/ppermute | solution.py:316
  109.0 11.8 %collective-permute-start.38 = (bf16[32,1920]{1,0:T(8,128)(2,1)S(1)}, bf16[32,1920]{1,0:T(8,128)(2,1)S(1)}, u32[]{:S(2)}, u32[]{:S(2)}) collective-permute-start(bf16[32,1920]{1,0:T(8,128)(2,1)S(1)} %get-tuple-element.233), channel_id=1, source_target_pairs={{0,4},{1,5},{2,6},{3,7},{4,0},{5,1},{6,2},{7,3},{8,12},{9,13},{10,... | collective-permute-start | bytes 368648 | tf_op jit(solution)/shard_map/ppermute | solution.py:316
  124.5 7.2 %collective-permute-start.39 = (bf16[32,1920]{1,0:T(8,128)(2,1)S(1)}, bf16[32,1920]{1,0:T(8,128)(2,1)S(1)}, u32[]{:S(2)}, u32[]{:S(2)}) collective-permute-start(bf16[32,1920]{1,0:T(8,128)(2,1)S(1)} %get-tuple-element.241), channel_id=1, source_target_pairs={{0,10},{1,11},{2,8},{3,9},{4,14},{5,15},{6,12},{7,13},{8,2},{9,3},... | collective-permute-start | bytes 368648 | tf_op jit(solution)/shard_map/ppermute | solution.py:316
  125.2 12.6 %collective-permute-start.40 = (bf16[32,1920]{1,0:T(8,128)(2,1)S(1)}, bf16[32,1920]{1,0:T(8,128)(2,1)S(1)}, u32[]{:S(2)}, u32[]{:S(2)}) collective-permute-start(bf16[32,1920]{1,0:T(8,128)(2,1)S(1)} %get-tuple-element.242), channel_id=1, source_target_pairs={{0,12},{1,13},{2,14},{3,15},{4,8},{5,9},{6,10},{7,11},{8,4},{9,5},... | collective-permute-start | bytes 368648 | tf_op jit(solution)/shard_map/ppermute | solution.py:316
  127.8 10.1 %collective-permute-start.36 = (bf16[32,1920]{1,0:T(8,128)(2,1)S(1)}, bf16[32,1920]{1,0:T(8,128)(2,1)S(1)}, u32[]{:S(2)}, u32[]{:S(2)}) collective-permute-start(bf16[32,1920]{1,0:T(8,128)(2,1)S(1)} %get-tuple-element.231.refs_2_.refs_11_), channel_id=1, source_target_pairs={{0,8},{1,9},{2,10},{3,11},{4,12},{5,13},{6,14},{7,15},{8,0},{9,1},... | collective-permute-start | bytes 368648 | tf_op jit(solution)/shard_map/ppermute | solution.py:316
  128.7 9.6 %collective-permute-start.41 = (bf16[32,1920]{1,0:T(8,128)(2,1)S(1)}, bf16[32,1920]{1,0:T(8,128)(2,1)S(1)}, u32[]{:S(2)}, u32[]{:S(2)}) collective-permute-start(bf16[32,1920]{1,0:T(8,128)(2,1)S(1)} %get-tuple-element.243), channel_id=1, source_target_pairs={{0,14},{1,15},{2,12},{3,13},{4,10},{5,11},{6,8},{7,9},{8,6},{9,7},... | collective-permute-start | bytes 368648 | tf_op jit(solution)/shard_map/ppermute | solution.py:316
  131.7 6.7 %collective-permute-start.43 = (bf16[32,1920]{1,0:T(8,128)(2,1)S(1)}, bf16[32,1920]{1,0:T(8,128)(2,1)S(1)}, u32[]{:S(2)}, u32[]{:S(2)}) collective-permute-start(bf16[32,1920]{1,0:T(8,128)(2,1)S(1)} %collective-permute-done.39.refs_1_), channel_id=1, source_target_pairs={{0,1},{1,0},{2,3},{3,2},{4,5},{5,4},{6,7},{7,6},{8,9},{9,8},{10,11... | collective-permute-start | bytes 368648 | tf_op jit(solution)/shard_map/ppermute | solution.py:316
  140.5 8.1 %collective-permute-start.46 = (bf16[32,1920]{1,0:T(8,128)(2,1)S(1)}, bf16[32,1920]{1,0:T(8,128)(2,1)S(1)}, u32[]{:S(2)}, u32[]{:S(2)}) collective-permute-start(bf16[32,1920]{1,0:T(8,128)(2,1)S(1)} %get-tuple-element.245), channel_id=1, source_target_pairs={{0,6},{1,7},{2,4},{3,5},{4,2},{5,3},{6,0},{7,1},{8,14},{9,15},{10,... | collective-permute-start | bytes 368648 | tf_op jit(solution)/shard_map/ppermute | solution.py:316
  142.8 10.2 %collective-permute-start.48 = (bf16[32,1920]{1,0:T(8,128)(2,1)S(1)}, bf16[32,1920]{1,0:T(8,128)(2,1)S(1)}, u32[]{:S(2)}, u32[]{:S(2)}) collective-permute-start(bf16[32,1920]{1,0:T(8,128)(2,1)S(1)} %get-tuple-element.257), channel_id=1, source_target_pairs={{0,2},{1,3},{2,0},{3,1},{4,6},{5,7},{6,4},{7,5},{8,10},{9,11},{10,... | collective-permute-start | bytes 368648 | tf_op jit(solution)/shard_map/ppermute | solution.py:316
  143.3 11.3 %collective-permute-start.49 = (bf16[32,1920]{1,0:T(8,128)(2,1)S(1)}, bf16[32,1920]{1,0:T(8,128)(2,1)S(1)}, u32[]{:S(2)}, u32[]{:S(2)}) collective-permute-start(bf16[32,1920]{1,0:T(8,128)(2,1)S(1)} %get-tuple-element.258), channel_id=1, source_target_pairs={{0,4},{1,5},{2,6},{3,7},{4,0},{5,1},{6,2},{7,3},{8,12},{9,13},{10,... | collective-permute-start | bytes 368648 | tf_op jit(solution)/shard_map/ppermute | solution.py:316
  159.0 7.7 %collective-permute-start.50 = (bf16[32,1920]{1,0:T(8,128)(2,1)S(1)}, bf16[32,1920]{1,0:T(8,128)(2,1)S(1)}, u32[]{:S(2)}, u32[]{:S(2)}) collective-permute-start(bf16[32,1920]{1,0:T(8,128)(2,1)S(1)} %get-tuple-element.269), channel_id=1, source_target_pairs={{0,26},{1,27},{2,24},{3,25},{4,30},{5,31},{6,28},{7,29},{8,2},{9,3... | collective-permute-start | bytes 368648 | tf_op jit(solution)/shard_map/ppermute | solution.py:316
  161.2 12.1 %collective-permute-start.51 = (bf16[32,1920]{1,0:T(8,128)(2,1)S(1)}, bf16[32,1920]{1,0:T(8,128)(2,1)S(1)}, u32[]{:S(2)}, u32[]{:S(2)}) collective-permute-start(bf16[32,1920]{1,0:T(8,128)(2,1)S(1)} %get-tuple-element.270), channel_id=1, source_target_pairs={{0,28},{1,29},{2,30},{3,31},{4,24},{5,25},{6,26},{7,27},{8,4},{9,5... | collective-permute-start | bytes 368648 | tf_op jit(solution)/shard_map/ppermute | solution.py:316
  162.7 10.6 %collective-permute-start.47 = (bf16[32,1920]{1,0:T(8,128)(2,1)S(1)}, bf16[32,1920]{1,0:T(8,128)(2,1)S(1)}, u32[]{:S(2)}, u32[]{:S(2)}) collective-permute-start(bf16[32,1920]{1,0:T(8,128)(2,1)S(1)} %get-tuple-element.256.refs_2_.refs_14_), channel_id=1, source_target_pairs={{0,24},{1,25},{2,26},{3,27},{4,28},{5,29},{6,30},{7,31},{8,0},{9,1... | collective-permute-start | bytes 368648 | tf_op jit(solution)/shard_map/ppermute | solution.py:316
  164.6 9.3 %collective-permute-start.52 = (bf16[32,1920]{1,0:T(8,128)(2,1)S(1)}, bf16[32,1920]{1,0:T(8,128)(2,1)S(1)}, u32[]{:S(2)}, u32[]{:S(2)}) collective-permute-start(bf16[32,1920]{1,0:T(8,128)(2,1)S(1)} %get-tuple-element.271), channel_id=1, source_target_pairs={{0,30},{1,31},{2,28},{3,29},{4,26},{5,27},{6,24},{7,25},{8,6},{9,7... | collective-permute-start | bytes 368648 | tf_op jit(solution)/shard_map/ppermute | solution.py:316
  166.7 7.2 %collective-permute-start.54 = (bf16[32,1920]{1,0:T(8,128)(2,1)S(1)}, bf16[32,1920]{1,0:T(8,128)(2,1)S(1)}, u32[]{:S(2)}, u32[]{:S(2)}) collective-permute-start(bf16[32,1920]{1,0:T(8,128)(2,1)S(1)} %collective-permute-done.50.refs_1_), channel_id=1, source_target_pairs={{0,1},{1,0},{2,3},{3,2},{4,5},{5,4},{6,7},{7,6},{8,9},{9,8},{10,11... | collective-permute-start | bytes 368648 | tf_op jit(solution)/shard_map/ppermute | solution.py:316
  173.3 1.5 collective-permute-start.53
  176.0 8.1 %collective-permute-start.57 = (bf16[32,1920]{1,0:T(8,128)(2,1)S(1)}, bf16[32,1920]{1,0:T(8,128)(2,1)S(1)}, u32[]{:S(2)}, u32[]{:S(2)}) collective-permute-start(bf16[32,1920]{1,0:T(8,128)(2,1)S(1)} %get-tuple-element.273), channel_id=1, source_target_pairs={{0,6},{1,7},{2,4},{3,5},{4,2},{5,3},{6,0},{7,1},{8,14},{9,15},{10,... | collective-permute-start | bytes 368648 | tf_op jit(solution)/shard_map/ppermute | solution.py:316
  178.4 8.8 %collective-permute-start.59 = (bf16[32,1920]{1,0:T(8,128)(2,1)S(1)}, bf16[32,1920]{1,0:T(8,128)(2,1)S(1)}, u32[]{:S(2)}, u32[]{:S(2)}) collective-permute-start(bf16[32,1920]{1,0:T(8,128)(2,1)S(1)} %get-tuple-element.280), channel_id=1, source_target_pairs={{0,2},{1,3},{2,0},{3,1},{4,6},{5,7},{6,4},{7,5},{8,10},{9,11},{10,... | collective-permute-start | bytes 368648 | tf_op jit(solution)/shard_map/ppermute | solution.py:316
  178.8 11.3 %collective-permute-start.60 = (bf16[32,1920]{1,0:T(8,128)(2,1)S(1)}, bf16[32,1920]{1,0:T(8,128)(2,1)S(1)}, u32[]{:S(2)}, u32[]{:S(2)}) collective-permute-start(bf16[32,1920]{1,0:T(8,128)(2,1)S(1)} %get-tuple-element.281), channel_id=1, source_target_pairs={{0,4},{1,5},{2,6},{3,7},{4,0},{5,1},{6,2},{7,3},{8,12},{9,13},{10,... | collective-permute-start | bytes 368648 | tf_op jit(solution)/shard_map/ppermute | solution.py:316
  192.3 7.7 %collective-permute-start.61 = (bf16[32,1920]{1,0:T(8,128)(2,1)S(1)}, bf16[32,1920]{1,0:T(8,128)(2,1)S(1)}, u32[]{:S(2)}, u32[]{:S(2)}) collective-permute-start(bf16[32,1920]{1,0:T(8,128)(2,1)S(1)} %get-tuple-element.287), channel_id=1, source_target_pairs={{0,26},{1,27},{2,24},{3,25},{4,30},{5,31},{6,28},{7,29},{8,2},{9,3... | collective-permute-start | bytes 368648 | tf_op jit(solution)/shard_map/ppermute | solution.py:316
  193.4 11.4 %collective-permute-start.62 = (bf16[32,1920]{1,0:T(8,128)(2,1)S(1)}, bf16[32,1920]{1,0:T(8,128)(2,1)S(1)}, u32[]{:S(2)}, u32[]{:S(2)}) collective-permute-start(bf16[32,1920]{1,0:T(8,128)(2,1)S(1)} %get-tuple-element.288), channel_id=1, source_target_pairs={{0,28},{1,29},{2,30},{3,31},{4,24},{5,25},{6,26},{7,27},{8,4},{9,5... | collective-permute-start | bytes 368648 | tf_op jit(solution)/shard_map/ppermute | solution.py:316
  196.1 9.6 %collective-permute-start.58 = (bf16[32,1920]{1,0:T(8,128)(2,1)S(1)}, bf16[32,1920]{1,0:T(8,128)(2,1)S(1)}, u32[]{:S(2)}, u32[]{:S(2)}) collective-permute-start(bf16[32,1920]{1,0:T(8,128)(2,1)S(1)} %get-tuple-element.279.refs_12_), channel_id=1, source_target_pairs={{0,24},{1,25},{2,26},{3,27},{4,28},{5,29},{6,30},{7,31},{8,0},{9,1... | collective-permute-start | bytes 368648 | tf_op jit(solution)/shard_map/ppermute | solution.py:316
  199.0 7.7 %collective-permute-start.63 = (bf16[32,1920]{1,0:T(8,128)(2,1)S(1)}, bf16[32,1920]{1,0:T(8,128)(2,1)S(1)}, u32[]{:S(2)}, u32[]{:S(2)}) collective-permute-start(bf16[32,1920]{1,0:T(8,128)(2,1)S(1)} %get-tuple-element.289), channel_id=1, source_target_pairs={{0,30},{1,31},{2,28},{3,29},{4,26},{5,27},{6,24},{7,25},{8,6},{9,7... | collective-permute-start | bytes 368648 | tf_op jit(solution)/shard_map/ppermute | solution.py:316
  200.1 6.6 %collective-permute-start.65 = (bf16[32,1920]{1,0:T(8,128)(2,1)S(1)}, bf16[32,1920]{1,0:T(8,128)(2,1)S(1)}, u32[]{:S(2)}, u32[]{:S(2)}) collective-permute-start(bf16[32,1920]{1,0:T(8,128)(2,1)S(1)} %collective-permute-done.61.refs_1_), channel_id=1, source_target_pairs={{0,1},{1,0},{2,3},{3,2},{4,5},{5,4},{6,7},{7,6},{8,9},{9,8},{10,11... | collective-permute-start | bytes 368648 | tf_op jit(solution)/shard_map/ppermute | solution.py:316
  204.9 1.8 collective-permute-start.66
  208.8 8.1 %collective-permute-start.68 = (bf16[32,1920]{1,0:T(8,128)(2,1)S(1)}, bf16[32,1920]{1,0:T(8,128)(2,1)S(1)}, u32[]{:S(2)}, u32[]{:S(2)}) collective-permute-start(bf16[32,1920]{1,0:T(8,128)(2,1)S(1)} %get-tuple-element.291), channel_id=1, source_target_pairs={{0,6},{1,7},{2,4},{3,5},{4,2},{5,3},{6,0},{7,1},{8,14},{9,15},{10,... | collective-permute-start | bytes 368648 | tf_op jit(solution)/shard_map/ppermute | solution.py:316
  211.3 8.0 %collective-permute-start.70 = (bf16[32,1920]{1,0:T(8,128)(2,1)S(1)}, bf16[32,1920]{1,0:T(8,128)(2,1)S(1)}, u32[]{:S(2)}, u32[]{:S(2)}) collective-permute-start(bf16[32,1920]{1,0:T(8,128)(2,1)S(1)} %get-tuple-element.332), channel_id=1, source_target_pairs={{0,2},{1,3},{2,0},{3,1},{4,6},{5,7},{6,4},{7,5},{8,10},{9,11},{10,... | collective-permute-start | bytes 368648 | tf_op jit(solution)/shard_map/ppermute | solution.py:316
  211.8 11.8 %collective-permute-start.71 = (bf16[32,1920]{1,0:T(8,128)(2,1)S(1)}, bf16[32,1920]{1,0:T(8,128)(2,1)S(1)}, u32[]{:S(2)}, u32[]{:S(2)}) collective-permute-start(bf16[32,1920]{1,0:T(8,128)(2,1)S(1)} %get-tuple-element.333), channel_id=1, source_target_pairs={{0,4},{1,5},{2,6},{3,7},{4,0},{5,1},{6,2},{7,3},{8,12},{9,13},{10,... | collective-permute-start | bytes 368648 | tf_op jit(solution)/shard_map/ppermute | solution.py:316
  225.7 7.7 %collective-permute-start.72 = (bf16[32,1920]{1,0:T(8,128)(2,1)S(1)}, bf16[32,1920]{1,0:T(8,128)(2,1)S(1)}, u32[]{:S(2)}, u32[]{:S(2)}) collective-permute-start(bf16[32,1920]{1,0:T(8,128)(2,1)S(1)} %get-tuple-element.339), channel_id=1, source_target_pairs={{0,26},{1,27},{2,24},{3,25},{4,30},{5,31},{6,28},{7,29},{8,2},{9,3... | collective-permute-start | bytes 368648 | tf_op jit(solution)/shard_map/ppermute | solution.py:316
  226.6 11.6 %collective-permute-start.73 = (bf16[32,1920]{1,0:T(8,128)(2,1)S(1)}, bf16[32,1920]{1,0:T(8,128)(2,1)S(1)}, u32[]{:S(2)}, u32[]{:S(2)}) collective-permute-start(bf16[32,1920]{1,0:T(8,128)(2,1)S(1)} %get-tuple-element.340), channel_id=1, source_target_pairs={{0,28},{1,29},{2,30},{3,31},{4,24},{5,25},{6,26},{7,27},{8,4},{9,5... | collective-permute-start | bytes 368648 | tf_op jit(solution)/shard_map/ppermute | solution.py:316
  229.8 8.9 %collective-permute-start.69 = (bf16[32,1920]{1,0:T(8,128)(2,1)S(1)}, bf16[32,1920]{1,0:T(8,128)(2,1)S(1)}, u32[]{:S(2)}, u32[]{:S(2)}) collective-permute-start(bf16[32,1920]{1,0:T(8,128)(2,1)S(1)} %get-tuple-element.331.refs_12_), channel_id=1, source_target_pairs={{0,24},{1,25},{2,26},{3,27},{4,28},{5,29},{6,30},{7,31},{8,0},{9,1... | collective-permute-start | bytes 368648 | tf_op jit(solution)/shard_map/ppermute | solution.py:316
  231.9 7.7 %collective-permute-start.74 = (bf16[32,1920]{1,0:T(8,128)(2,1)S(1)}, bf16[32,1920]{1,0:T(8,128)(2,1)S(1)}, u32[]{:S(2)}, u32[]{:S(2)}) collective-permute-start(bf16[32,1920]{1,0:T(8,128)(2,1)S(1)} %get-tuple-element.341), channel_id=1, source_target_pairs={{0,30},{1,31},{2,28},{3,29},{4,26},{5,27},{6,24},{7,25},{8,6},{9,7... | collective-permute-start | bytes 368648 | tf_op jit(solution)/shard_map/ppermute | solution.py:316
  233.4 6.2 %collective-permute-start.76 = (bf16[32,1920]{1,0:T(8,128)(2,1)S(1)}, bf16[32,1920]{1,0:T(8,128)(2,1)S(1)}, u32[]{:S(2)}, u32[]{:S(2)}) collective-permute-start(bf16[32,1920]{1,0:T(8,128)(2,1)S(1)} %collective-permute-done.72.refs_1_), channel_id=1, source_target_pairs={{0,1},{1,0},{2,3},{3,2},{4,5},{5,4},{6,7},{7,6},{8,9},{9,8},{10,11... | collective-permute-start | bytes 368648 | tf_op jit(solution)/shard_map/ppermute | solution.py:316
  241.8 11.8 %collective-permute-start.80 = (bf16[32,1920]{1,0:T(8,128)(2,1)S(1)}, bf16[32,1920]{1,0:T(8,128)(2,1)S(1)}, u32[]{:S(2)}, u32[]{:S(2)}) collective-permute-start(bf16[32,1920]{1,0:T(8,128)(2,1)S(1)} %get-tuple-element.380), channel_id=1, source_target_pairs={{0,2},{1,3},{2,0},{3,1},{4,6},{5,7},{6,4},{7,5},{8,10},{9,11},{10,... | collective-permute-start | bytes 368648 | tf_op jit(solution)/shard_map/ppermute | solution.py:316
  244.0 12.2 %collective-permute-start.81 = (bf16[32,1920]{1,0:T(8,128)(2,1)S(1)}, bf16[32,1920]{1,0:T(8,128)(2,1)S(1)}, u32[]{:S(2)}, u32[]{:S(2)}) collective-permute-start(bf16[32,1920]{1,0:T(8,128)(2,1)S(1)} %get-tuple-element.381), channel_id=1, source_target_pairs={{0,4},{1,5},{2,6},{3,7},{4,0},{5,1},{6,2},{7,3},{8,12},{9,13},{10,... | collective-permute-start | bytes 368648 | tf_op jit(solution)/shard_map/ppermute | solution.py:316
  244.8 12.5 %collective-permute-start.79 = (bf16[32,1920]{1,0:T(8,128)(2,1)S(1)}, bf16[32,1920]{1,0:T(8,128)(2,1)S(1)}, u32[]{:S(2)}, u32[]{:S(2)}) collective-permute-start(bf16[32,1920]{1,0:T(8,128)(2,1)S(1)} %get-tuple-element.343), channel_id=1, source_target_pairs={{0,6},{1,7},{2,4},{3,5},{4,2},{5,3},{6,0},{7,1},{8,14},{9,15},{10,... | collective-permute-start | bytes 368648 | tf_op jit(solution)/shard_map/ppermute | solution.py:316
  (24 other events, 91.1 us)

commit v2 on v1

--- a/solution.py
+++ b/solution.py
@@ -242,6 +242,17 @@
             split_rows(sent, start.astype(bf16))
         else:
             start_ref[m - 1] = start.astype(bf16)
+
+
+def fetch_kernel(in_ref, out_ref, in_near, out_near, sems):
+    copies = [
+        pltpu.make_async_copy(in_ref, in_near, sems.at[0]),
+        pltpu.make_async_copy(out_ref, out_near, sems.at[1]),
+    ]
+    for copy in copies:
+        copy.start()
+    for copy in copies:
+        copy.wait()
 
 
 def transpose_kernel(in_ref, out_ref, in_turned, out_turned):
@@ -382,6 +393,19 @@
             compiler_params=params,
             name="resort",
         )(places[step], order, *ins)
+
+    own_in, own_out = pl.pallas_call(
+        fetch_kernel,
+        out_shape=[
+            jax.ShapeDtypeStruct(own_in.shape, bf16),
+            jax.ShapeDtypeStruct(own_out.shape, bf16),
+        ],
+        in_specs=[ANY] * 2,
+        out_specs=[VMEM] * 2,
+        scratch_shapes=[pltpu.SemaphoreType.DMA((2,))],
+        compiler_params=params,
+        name="fetch",
+    )(own_in, own_out)
 
     def forward(arrived, earlier):
         many = len(arrived)

time: 263 us -> 239 us (0.909)
  waiting for transfers between devices: 105 us -> 73.5 us
  starting transfers between devices: 93.4 us -> 99.8 us
    ppermute x82, waiting for transfers between devices: 105 us -> 73.5 us  [permuted(): return lax.ppermute(block, ('pipe', 'expert'), route)]
    ppermute x82, starting transfers between devices: 93.4 us -> 99.8 us  [permuted(): return lax.ppermute(block, ('pipe', 'expert'), route)]
  transfers between devices with their start and end apart: 82 -> 82, of which waited for: 57 -> 32; matrix products, arithmetic and copies ran while one was open for 0% -> 0% of each run, Pallas kernels for 11% -> 19%
where the time goes in v2:
time: 239 us
  starting transfers between devices  99.8 us (42%)
  waiting for transfers between devices  73.5 us (31%)
  Pallas kernels  58.7 us (25%)
  local copies, waits for them, and re-layouts  3.8 us (2%)
    ppermute x82, starting transfers between devices, permuted(): return lax.ppermute(block, ('pipe', 'expert'), route)  99.8 us
    ppermute x82, waiting for transfers between devices, permuted(): return lax.ppermute(block, ('pipe', 'expert'), route)  73.5 us
    pallas_call x10, Pallas kernels, backward(): pl.pallas_call(functools.partial(backward_kernel, plan), out_shape=[piece...  19.6 us
    pallas_call x10, Pallas kernels, forward(): pl.pallas_call(functools.partial(forward_kernel, many, len(earlier)), out...  16.4 us
    pallas_call x8, Pallas kernels, record(): pl.pallas_call(functools.partial(record_kernel, (layers, micros, len(sour...  7.1 us
    pallas_call x7, Pallas kernels, resort(): pl.pallas_call(functools.partial(resort_kernel, (len(arrived), count, wid...  6.06 us
  transfers between devices with their start and end apart: 82, of which 32 were waited for; matrix products, arithmetic and copies ran while one was open for 0% of the time, Pallas kernels for 19%

profile of v2, /device:TPU:0, one launch (start us, length us, event | category | flops | bytes accessed | tf_op | source)
XLA Modules:
  0.0 239.0 jit_solution(5634073963199507549)
XLA Ops:
  2.6 2.2 copy-done
  4.8 1.6 copy-done.2
  6.9 1.6 prepare.1
  8.4 5.1 %collective-permute-start.2 = (bf16[32,1920]{1,0:T(8,128)(2,1)S(1)}, bf16[32,1920]{1,0:T(8,128)(2,1)S(1)}, u32[]{:S(2)}, u32[]{:S(2)}) collective-permute-start(bf16[32,1920]{1,0:T(8,128)(2,1)S(1)} %get-tuple-element.202), channel_id=1, source_target_pairs={{0,6},{1,7},{2,4},{3,5},{4,2},{5,3},{6,0},{7,1},{8,14},{9,15},{10,... | collective-permute-start | bytes 368648 | tf_op jit(solution)/shard_map/ppermute | solution.py:327
  14.9 2.8 %collective-permute-done.2.refs_1_.refs_3_ = bf16[32,1920]{1,0:T(8,128)(2,1)S(1)} collective-permute-done((bf16[32,1920]{1,0:T(8,128)(2,1)S(1)}, bf16[32,1920]{1,0:T(8,128)(2,1)S(1)}, u32[]{:S(2)}, u32[]{:S(2)}) %collective-permute-start.2) | collective-permute-done | bytes 122912 | tf_op jit(solution)/shard_map/ppermute | solution.py:327
  19.3 4.8 %collective-permute-start.8 = (bf16[32,1920]{1,0:T(8,128)(2,1)S(1)}, bf16[32,1920]{1,0:T(8,128)(2,1)S(1)}, u32[]{:S(2)}, u32[]{:S(2)}) collective-permute-start(bf16[32,1920]{1,0:T(8,128)(2,1)S(1)} %get-tuple-element.208), channel_id=1, source_target_pairs={{0,14},{1,15},{2,12},{3,13},{4,10},{5,11},{6,8},{7,9},{8,22},{9,23... | collective-permute-start | bytes 368648 | tf_op jit(solution)/shard_map/ppermute | solution.py:327
  25.6 2.1 collective-permute-done.5.refs_1_.refs_3_
  29.2 3.3 %collective-permute-start.7 = (bf16[32,1920]{1,0:T(8,128)(2,1)S(1)}, bf16[32,1920]{1,0:T(8,128)(2,1)S(1)}, u32[]{:S(2)}, u32[]{:S(2)}) collective-permute-start(bf16[32,1920]{1,0:T(8,128)(2,1)S(1)} %get-tuple-element.207), channel_id=1, source_target_pairs={{0,12},{1,13},{2,14},{3,15},{4,8},{5,9},{6,10},{7,11},{8,20},{9,21... | collective-permute-start | bytes 368648 | tf_op jit(solution)/shard_map/ppermute | solution.py:327
  33.1 4.2 %collective-permute-done.6.refs_1_ = bf16[32,1920]{1,0:T(8,128)(2,1)S(1)} collective-permute-done((bf16[32,1920]{1,0:T(8,128)(2,1)S(1)}, bf16[32,1920]{1,0:T(8,128)(2,1)S(1)}, u32[]{:S(2)}, u32[]{:S(2)}) %collective-permute-start.6) | collective-permute-done | bytes 122912 | tf_op jit(solution)/shard_map/ppermute | solution.py:327
  39.6 1.9 collective-permute-start.13
  42.1 1.9 collective-permute-start.16
  44.1 3.7 %collective-permute-done.13.refs_1_.refs_3_ = bf16[32,1920]{1,0:T(8,128)(2,1)S(1)} collective-permute-done((bf16[32,1920]{1,0:T(8,128)(2,1)S(1)}, bf16[32,1920]{1,0:T(8,128)(2,1)S(1)}, u32[]{:S(2)}, u32[]{:S(2)}) %collective-permute-start.13) | collective-permute-done | bytes 122912 | tf_op jit(solution)/shard_map/ppermute | solution.py:327
  50.7 2.0 collective-permute-start.14
  52.7 5.0 %collective-permute-done.16.refs_1_.refs_3_ = bf16[32,1920]{1,0:T(8,128)(2,1)S(1)} collective-permute-done((bf16[32,1920]{1,0:T(8,128)(2,1)S(1)}, bf16[32,1920]{1,0:T(8,128)(2,1)S(1)}, u32[]{:S(2)}, u32[]{:S(2)}) %collective-permute-start.16) | collective-permute-done | bytes 122912 | tf_op jit(solution)/shard_map/ppermute | solution.py:327
  59.2 2.2 collective-permute-start.18
  62.0 4.8 %collective-permute-done.17.refs_1_ = bf16[32,1920]{1,0:T(8,128)(2,1)S(1)} collective-permute-done((bf16[32,1920]{1,0:T(8,128)(2,1)S(1)}, bf16[32,1920]{1,0:T(8,128)(2,1)S(1)}, u32[]{:S(2)}, u32[]{:S(2)}) %collective-permute-start.17) | collective-permute-done | bytes 122912 | tf_op jit(solution)/shard_map/ppermute | solution.py:327
  66.7 2.6 %collective-permute-done.18.refs_2_ = bf16[32,1920]{1,0:T(8,128)(2,1)S(1)} collective-permute-done((bf16[32,1920]{1,0:T(8,128)(2,1)S(1)}, bf16[32,1920]{1,0:T(8,128)(2,1)S(1)}, u32[]{:S(2)}, u32[]{:S(2)}) %collective-permute-start.18) | collective-permute-done | bytes 122912 | tf_op jit(solution)/shard_map/ppermute | solution.py:327
  72.8 3.1 %collective-permute-start.27 = (bf16[32,1920]{1,0:T(8,128)(2,1)S(1)}, bf16[32,1920]{1,0:T(8,128)(2,1)S(1)}, u32[]{:S(2)}, u32[]{:S(2)}) collective-permute-start(bf16[32,1920]{1,0:T(8,128)(2,1)S(1)} %get-tuple-element.222), channel_id=1, source_target_pairs={{0,4},{1,5},{2,6},{3,7},{4,0},{5,1},{6,2},{7,3},{8,12},{9,13},{10,... | collective-permute-start | bytes 368648 | tf_op jit(solution)/shard_map/ppermute | solution.py:327
  76.0 3.7 %collective-permute-done.24.refs_1_ = bf16[32,1920]{1,0:T(8,128)(2,1)S(1)} collective-permute-done((bf16[32,1920]{1,0:T(8,128)(2,1)S(1)}, bf16[32,1920]{1,0:T(8,128)(2,1)S(1)}, u32[]{:S(2)}, u32[]{:S(2)}) %collective-permute-start.24) | collective-permute-done | bytes 122912 | tf_op jit(solution)/shard_map/ppermute | solution.py:327
  81.1 1.8 collective-permute-start.30
  83.0 1.6 collective-permute-start.25
  86.2 4.4 %collective-permute-start.29 = (bf16[32,1920]{1,0:T(8,128)(2,1)S(1)}, bf16[32,1920]{1,0:T(8,128)(2,1)S(1)}, u32[]{:S(2)}, u32[]{:S(2)}) collective-permute-start(bf16[32,1920]{1,0:T(8,128)(2,1)S(1)} %get-tuple-element.224), channel_id=1, source_target_pairs={{0,12},{1,13},{2,14},{3,15},{4,8},{5,9},{6,10},{7,11},{8,20},{9,21... | collective-permute-start | bytes 368648 | tf_op jit(solution)/shard_map/ppermute | solution.py:327
  90.6 3.9 %collective-permute-done.25.refs_0_ = bf16[32,1920]{1,0:T(8,128)(2,1)S(1)} collective-permute-done((bf16[32,1920]{1,0:T(8,128)(2,1)S(1)}, bf16[32,1920]{1,0:T(8,128)(2,1)S(1)}, u32[]{:S(2)}, u32[]{:S(2)}) %collective-permute-start.25) | collective-permute-done | bytes 122912 | tf_op jit(solution)/shard_map/ppermute | solution.py:327
  98.6 1.8 collective-permute-start.35
  100.4 2.7 %collective-permute-start.38 = (bf16[32,1920]{1,0:T(8,128)(2,1)S(1)}, bf16[32,1920]{1,0:T(8,128)(2,1)S(1)}, u32[]{:S(2)}, u32[]{:S(2)}) collective-permute-start(bf16[32,1920]{1,0:T(8,128)(2,1)S(1)} %get-tuple-element.237), channel_id=1, source_target_pairs={{0,4},{1,5},{2,6},{3,7},{4,0},{5,1},{6,2},{7,3},{8,12},{9,13},{10,... | collective-permute-start | bytes 368648 | tf_op jit(solution)/shard_map/ppermute | solution.py:327
  103.1 2.9 %turn.1 = (bf16[1024,2048]{1,0:T(8,128)(2,1)S(1)}, bf16[2048,512]{1,0:T(8,128)(2,1)S(1)}) custom-call(bf16[2048,1024]{1,0:T(8,128)(2,1)S(1)} %get-tuple-element.196.in_ref, bf16[512,2048]{1,0:T(8,128)(2,1)S(1)} %get-tuple-element.197.out_ref), custom_call_target="tpu_custom_call" | custom-call | tf_op jit(solution)/shard_map/turn/pallas_call | solution.py:466
  108.2 2.2 backward.10
  110.4 1.5 collective-permute-start.41
  112.0 1.7 collective-permute-start.36
  115.2 2.2 backward.11
  118.1 3.0 %collective-permute-start.40 = (bf16[32,1920]{1,0:T(8,128)(2,1)S(1)}, bf16[32,1920]{1,0:T(8,128)(2,1)S(1)}, u32[]{:S(2)}, u32[]{:S(2)}) collective-permute-start(bf16[32,1920]{1,0:T(8,128)(2,1)S(1)} %get-tuple-element.246), channel_id=1, source_target_pairs={{0,12},{1,13},{2,14},{3,15},{4,8},{5,9},{6,10},{7,11},{8,4},{9,5},... | collective-permute-start | bytes 368648 | tf_op jit(solution)/shard_map/ppermute | solution.py:327
  121.6 1.9 collective-permute-done.39.refs_1_
  123.5 2.6 %collective-permute-done.40.refs_2_ = bf16[32,1920]{1,0:T(8,128)(2,1)S(1)} collective-permute-done((bf16[32,1920]{1,0:T(8,128)(2,1)S(1)}, bf16[32,1920]{1,0:T(8,128)(2,1)S(1)}, u32[]{:S(2)}, u32[]{:S(2)}) %collective-permute-start.40) | collective-permute-done | bytes 122912 | tf_op jit(solution)/shard_map/ppermute | solution.py:327
  130.1 2.6 %collective-permute-start.49 = (bf16[32,1920]{1,0:T(8,128)(2,1)S(1)}, bf16[32,1920]{1,0:T(8,128)(2,1)S(1)}, u32[]{:S(2)}, u32[]{:S(2)}) collective-permute-start(bf16[32,1920]{1,0:T(8,128)(2,1)S(1)} %get-tuple-element.262), channel_id=1, source_target_pairs={{0,4},{1,5},{2,6},{3,7},{4,0},{5,1},{6,2},{7,3},{8,12},{9,13},{10,... | collective-permute-start | bytes 368648 | tf_op jit(solution)/shard_map/ppermute | solution.py:327
  132.7 3.6 %collective-permute-done.46.refs_1_ = bf16[32,1920]{1,0:T(8,128)(2,1)S(1)} collective-permute-done((bf16[32,1920]{1,0:T(8,128)(2,1)S(1)}, bf16[32,1920]{1,0:T(8,128)(2,1)S(1)}, u32[]{:S(2)}, u32[]{:S(2)}) %collective-permute-start.46) | collective-permute-done | bytes 122912 | tf_op jit(solution)/shard_map/ppermute | solution.py:327
  136.4 2.2 forward.18
  138.6 2.2 backward.12
  140.8 4.1 %collective-permute-start.52 = (bf16[32,1920]{1,0:T(8,128)(2,1)S(1)}, bf16[32,1920]{1,0:T(8,128)(2,1)S(1)}, u32[]{:S(2)}, u32[]{:S(2)}) collective-permute-start(bf16[32,1920]{1,0:T(8,128)(2,1)S(1)} %get-tuple-element.275), channel_id=1, source_target_pairs={{0,30},{1,31},{2,28},{3,29},{4,26},{5,27},{6,24},{7,25},{8,6},{9,7... | collective-permute-start | bytes 368648 | tf_op jit(solution)/shard_map/ppermute | solution.py:327
  144.9 2.2 forward.19
  147.0 2.2 backward.13
  151.4 1.6 collective-permute-start.47
  152.9 3.0 %collective-permute-done.50.refs_1_ = bf16[32,1920]{1,0:T(8,128)(2,1)S(1)} collective-permute-done((bf16[32,1920]{1,0:T(8,128)(2,1)S(1)}, bf16[32,1920]{1,0:T(8,128)(2,1)S(1)}, u32[]{:S(2)}, u32[]{:S(2)}) %collective-permute-start.50) | collective-permute-done | bytes 122912 | tf_op jit(solution)/shard_map/ppermute | solution.py:327
  155.9 2.5 %collective-permute-done.51.refs_2_ = bf16[32,1920]{1,0:T(8,128)(2,1)S(1)} collective-permute-done((bf16[32,1920]{1,0:T(8,128)(2,1)S(1)}, bf16[32,1920]{1,0:T(8,128)(2,1)S(1)}, u32[]{:S(2)}, u32[]{:S(2)}) %collective-permute-start.51) | collective-permute-done | bytes 122912 | tf_op jit(solution)/shard_map/ppermute | solution.py:327
  158.4 1.6 collective-permute-done.47.refs_0_
  163.5 3.2 %collective-permute-start.60 = (bf16[32,1920]{1,0:T(8,128)(2,1)S(1)}, bf16[32,1920]{1,0:T(8,128)(2,1)S(1)}, u32[]{:S(2)}, u32[]{:S(2)}) collective-permute-start(bf16[32,1920]{1,0:T(8,128)(2,1)S(1)} %get-tuple-element.285), channel_id=1, source_target_pairs={{0,4},{1,5},{2,6},{3,7},{4,0},{5,1},{6,2},{7,3},{8,12},{9,13},{10,... | collective-permute-start | bytes 368648 | tf_op jit(solution)/shard_map/ppermute | solution.py:327
  166.7 3.7 %collective-permute-done.57.refs_1_ = bf16[32,1920]{1,0:T(8,128)(2,1)S(1)} collective-permute-done((bf16[32,1920]{1,0:T(8,128)(2,1)S(1)}, bf16[32,1920]{1,0:T(8,128)(2,1)S(1)}, u32[]{:S(2)}, u32[]{:S(2)}) %collective-permute-start.57) | collective-permute-done | bytes 122912 | tf_op jit(solution)/shard_map/ppermute | solution.py:327
  170.4 2.2 backward.14
  172.5 2.3 collective-permute-start.63
  175.4 2.2 backward.15
  177.5 2.6 %collective-permute-start.61 = (bf16[32,1920]{1,0:T(8,128)(2,1)S(1)}, bf16[32,1920]{1,0:T(8,128)(2,1)S(1)}, u32[]{:S(2)}, u32[]{:S(2)}) collective-permute-start(bf16[32,1920]{1,0:T(8,128)(2,1)S(1)} %get-tuple-element.291), channel_id=1, source_target_pairs={{0,26},{1,27},{2,24},{3,25},{4,30},{5,31},{6,28},{7,29},{8,2},{9,3... | collective-permute-start | bytes 368648 | tf_op jit(solution)/shard_map/ppermute | solution.py:327
  180.1 2.3 collective-permute-start.62
  182.5 2.7 %collective-permute-done.58.refs_0_ = bf16[32,1920]{1,0:T(8,128)(2,1)S(1)} collective-permute-done((bf16[32,1920]{1,0:T(8,128)(2,1)S(1)}, bf16[32,1920]{1,0:T(8,128)(2,1)S(1)}, u32[]{:S(2)}, u32[]{:S(2)}) %collective-permute-start.58) | collective-permute-done | bytes 122912 | tf_op jit(solution)/shard_map/ppermute | solution.py:327
  189.0 4.1 %collective-permute-start.68 = (bf16[32,1920]{1,0:T(8,128)(2,1)S(1)}, bf16[32,1920]{1,0:T(8,128)(2,1)S(1)}, u32[]{:S(2)}, u32[]{:S(2)}) collective-permute-start(bf16[32,1920]{1,0:T(8,128)(2,1)S(1)} %get-tuple-element.295), channel_id=1, source_target_pairs={{0,6},{1,7},{2,4},{3,5},{4,2},{5,3},{6,0},{7,1},{8,14},{9,15},{10,... | collective-permute-start | bytes 368648 | tf_op jit(solution)/shard_map/ppermute | solution.py:327
  195.1 1.7 collective-permute-done.68.refs_1_
  196.9 2.2 backward.16
  199.1 6.9 %collective-permute-start.74 = (bf16[32,1920]{1,0:T(8,128)(2,1)S(1)}, bf16[32,1920]{1,0:T(8,128)(2,1)S(1)}, u32[]{:S(2)}, u32[]{:S(2)}) collective-permute-start(bf16[32,1920]{1,0:T(8,128)(2,1)S(1)} %get-tuple-element.345), channel_id=1, source_target_pairs={{0,30},{1,31},{2,28},{3,29},{4,26},{5,27},{6,24},{7,25},{8,6},{9,7... | collective-permute-start | bytes 368648 | tf_op jit(solution)/shard_map/ppermute | solution.py:327
  206.3 2.2 backward.17
  208.4 1.8 collective-permute-start.72
  210.3 2.7 %collective-permute-start.73 = (bf16[32,1920]{1,0:T(8,128)(2,1)S(1)}, bf16[32,1920]{1,0:T(8,128)(2,1)S(1)}, u32[]{:S(2)}, u32[]{:S(2)}) collective-permute-start(bf16[32,1920]{1,0:T(8,128)(2,1)S(1)} %get-tuple-element.344), channel_id=1, source_target_pairs={{0,28},{1,29},{2,30},{3,31},{4,24},{5,25},{6,26},{7,27},{8,4},{9,5... | collective-permute-start | bytes 368648 | tf_op jit(solution)/shard_map/ppermute | solution.py:327
  213.4 2.0 collective-permute-done.72.refs_1_
  215.4 2.9 %collective-permute-done.73.refs_2_ = bf16[32,1920]{1,0:T(8,128)(2,1)S(1)} collective-permute-done((bf16[32,1920]{1,0:T(8,128)(2,1)S(1)}, bf16[32,1920]{1,0:T(8,128)(2,1)S(1)}, u32[]{:S(2)}, u32[]{:S(2)}) %collective-permute-start.73) | collective-permute-done | bytes 122912 | tf_op jit(solution)/shard_map/ppermute | solution.py:327
  220.5 1.8 collective-permute-start.79
  222.3 2.7 %collective-permute-start.81 = (bf16[32,1920]{1,0:T(8,128)(2,1)S(1)}, bf16[32,1920]{1,0:T(8,128)(2,1)S(1)}, u32[]{:S(2)}, u32[]{:S(2)}) collective-permute-start(bf16[32,1920]{1,0:T(8,128)(2,1)S(1)} %get-tuple-element.385), channel_id=1, source_target_pairs={{0,4},{1,5},{2,6},{3,7},{4,0},{5,1},{6,2},{7,3},{8,12},{9,13},{10,... | collective-permute-start | bytes 368648 | tf_op jit(solution)/shard_map/ppermute | solution.py:327
  234.4 4.6 %grads.1 = (bf16[2048,1024]{1,0:T(8,128)(2,1)}, bf16[512,2048]{1,0:T(8,128)(2,1)}) custom-call(s32[3]{0:T(128)S(1)} %get-tuple-element.398.place_ref, bf16[3,64,2048]{2,1,0:T(8,128)(2,1)S(1)} %get-tuple-element.331.refs_0_, bf16[3,64,1024]{2,1,0:T(8,128)(2,1)S(1)} %get-tuple-element.332.refs_1_, bf16[3,64,512]{2,1,0:T(8,128)(2,1)S(1)} %get-tuple-element.333.refs_2_, ...), custom_call_target="tpu_custom_call" | custom-call | tf_op jit(solution)/shard_map/grads/pallas_call | solution.py:580
  (151 shorter events, 60.9 us)
Async XLA Ops:
  1.8 5.0 %collective-permute-start.1 = (bf16[2,80,2048]{2,1,0:T(8,128)(2,1)S(1)}, bf16[2,80,2048]{2,1,0:T(8,128)(2,1)S(1)}, u32[]{:S(2)}, u32[]{:S(2)}) collective-permute-start(bf16[2,80,2048]{2,1,0:T(8,128)(2,1)S(1)} %broadcast_select_fusion.refs_2_), channel_id=1, source_target_pairs={{0,1},{1,0},{2,3},{3,2},{4,5},{5,4},{6,7},{7,6},{8,9},{9,8},{10,11... | collective-permute-start | bytes 1966088 | tf_op jit(solution)/shard_map/ppermute | solution.py:327
  2.4 4.5 %collective-permute-start = (s32[8,80]{1,0:T(8,128)}, s32[8,80]{1,0:T(8,128)S(1)}, u32[]{:S(2)}, u32[]{:S(2)}) collective-permute-start(s32[8,80]{1,0:T(8,128)} %bitcast.14), channel_id=1, source_target_pairs={{0,1},{1,0},{2,3},{3,2},{4,5},{5,4},{6,7},{7,6},{8,9},{9,8},{10,11... | collective-permute-start | bytes 7688 | tf_op jit(solution)/shard_map/ppermute | solution.py:327
  8.4 9.3 %collective-permute-start.2 = (bf16[32,1920]{1,0:T(8,128)(2,1)S(1)}, bf16[32,1920]{1,0:T(8,128)(2,1)S(1)}, u32[]{:S(2)}, u32[]{:S(2)}) collective-permute-start(bf16[32,1920]{1,0:T(8,128)(2,1)S(1)} %get-tuple-element.202), channel_id=1, source_target_pairs={{0,6},{1,7},{2,4},{3,5},{4,2},{5,3},{6,0},{7,1},{8,14},{9,15},{10,... | collective-permute-start | bytes 368648 | tf_op jit(solution)/shard_map/ppermute | solution.py:327
  13.5 12.0 %collective-permute-start.4 = (bf16[32,1920]{1,0:T(8,128)(2,1)S(1)}, bf16[32,1920]{1,0:T(8,128)(2,1)S(1)}, u32[]{:S(2)}, u32[]{:S(2)}) collective-permute-start(bf16[32,1920]{1,0:T(8,128)(2,1)S(1)} %get-tuple-element.204), channel_id=1, source_target_pairs={{0,2},{1,3},{2,0},{3,1},{4,6},{5,7},{6,4},{7,5},{8,10},{9,11},{10,... | collective-permute-start | bytes 368648 | tf_op jit(solution)/shard_map/ppermute | solution.py:327
  13.5 14.1 %collective-permute-start.5 = (bf16[32,1920]{1,0:T(8,128)(2,1)S(1)}, bf16[32,1920]{1,0:T(8,128)(2,1)S(1)}, u32[]{:S(2)}, u32[]{:S(2)}) collective-permute-start(bf16[32,1920]{1,0:T(8,128)(2,1)S(1)} %get-tuple-element.205), channel_id=1, source_target_pairs={{0,4},{1,5},{2,6},{3,7},{4,0},{5,1},{6,2},{7,3},{8,12},{9,13},{10,... | collective-permute-start | bytes 368648 | tf_op jit(solution)/shard_map/ppermute | solution.py:327
  19.3 13.3 %collective-permute-start.8 = (bf16[32,1920]{1,0:T(8,128)(2,1)S(1)}, bf16[32,1920]{1,0:T(8,128)(2,1)S(1)}, u32[]{:S(2)}, u32[]{:S(2)}) collective-permute-start(bf16[32,1920]{1,0:T(8,128)(2,1)S(1)} %get-tuple-element.208), channel_id=1, source_target_pairs={{0,14},{1,15},{2,12},{3,13},{4,10},{5,11},{6,8},{7,9},{8,22},{9,23... | collective-permute-start | bytes 368648 | tf_op jit(solution)/shard_map/ppermute | solution.py:327
  24.1 8.5 %collective-permute-start.3 = (bf16[32,1920]{1,0:T(8,128)(2,1)S(1)}, bf16[32,1920]{1,0:T(8,128)(2,1)S(1)}, u32[]{:S(2)}, u32[]{:S(2)}) collective-permute-start(bf16[32,1920]{1,0:T(8,128)(2,1)S(1)} %get-tuple-element.203.refs_2_), channel_id=1, source_target_pairs={{0,8},{1,9},{2,10},{3,11},{4,12},{5,13},{6,14},{7,15},{8,16},{9,17... | collective-permute-start | bytes 368648 | tf_op jit(solution)/shard_map/ppermute | solution.py:327
  29.2 8.0 %collective-permute-start.6 = (bf16[32,1920]{1,0:T(8,128)(2,1)S(1)}, bf16[32,1920]{1,0:T(8,128)(2,1)S(1)}, u32[]{:S(2)}, u32[]{:S(2)}) collective-permute-start(bf16[32,1920]{1,0:T(8,128)(2,1)S(1)} %get-tuple-element.206), channel_id=1, source_target_pairs={{0,10},{1,11},{2,8},{3,9},{4,14},{5,15},{6,12},{7,13},{8,18},{9,19... | collective-permute-start | bytes 368648 | tf_op jit(solution)/shard_map/ppermute | solution.py:327
  29.2 8.0 %collective-permute-start.7 = (bf16[32,1920]{1,0:T(8,128)(2,1)S(1)}, bf16[32,1920]{1,0:T(8,128)(2,1)S(1)}, u32[]{:S(2)}, u32[]{:S(2)}) collective-permute-start(bf16[32,1920]{1,0:T(8,128)(2,1)S(1)} %get-tuple-element.207), channel_id=1, source_target_pairs={{0,12},{1,13},{2,14},{3,15},{4,8},{5,9},{6,10},{7,11},{8,20},{9,21... | collective-permute-start | bytes 368648 | tf_op jit(solution)/shard_map/ppermute | solution.py:327
  32.5 5.2 %collective-permute-start.12 = (bf16[32,1920]{1,0:T(8,128)(2,1)S(1)}, bf16[32,1920]{1,0:T(8,128)(2,1)S(1)}, u32[]{:S(2)}, u32[]{:S(2)}) collective-permute-start(bf16[32,1920]{1,0:T(8,128)(2,1)S(1)} %collective-permute-done.8.refs_3_), channel_id=1, source_target_pairs={{0,1},{1,0},{2,3},{3,2},{4,5},{5,4},{6,7},{7,6},{8,9},{9,8},{10,11... | collective-permute-start | bytes 368648 | tf_op jit(solution)/shard_map/ppermute | solution.py:327
  32.5 5.2 %collective-permute-start.9 = (bf16[32,1920]{1,0:T(8,128)(2,1)S(1)}, bf16[32,1920]{1,0:T(8,128)(2,1)S(1)}, u32[]{:S(2)}, u32[]{:S(2)}) collective-permute-start(bf16[32,1920]{1,0:T(8,128)(2,1)S(1)} %collective-permute-done.3.refs_0_), channel_id=1, source_target_pairs={{0,1},{1,0},{2,3},{3,2},{4,5},{5,4},{6,7},{7,6},{8,9},{9,8},{10,11... | collective-permute-start | bytes 368648 | tf_op jit(solution)/shard_map/ppermute | solution.py:327
  39.6 8.1 %collective-permute-start.13 = (bf16[32,1920]{1,0:T(8,128)(2,1)S(1)}, bf16[32,1920]{1,0:T(8,128)(2,1)S(1)}, u32[]{:S(2)}, u32[]{:S(2)}) collective-permute-start(bf16[32,1920]{1,0:T(8,128)(2,1)S(1)} %get-tuple-element.211), channel_id=1, source_target_pairs={{0,6},{1,7},{2,4},{3,5},{4,2},{5,3},{6,0},{7,1},{8,14},{9,15},{10,... | collective-permute-start | bytes 368648 | tf_op jit(solution)/shard_map/ppermute | solution.py:327
  41.5 11.2 %collective-permute-start.15 = (bf16[32,1920]{1,0:T(8,128)(2,1)S(1)}, bf16[32,1920]{1,0:T(8,128)(2,1)S(1)}, u32[]{:S(2)}, u32[]{:S(2)}) collective-permute-start(bf16[32,1920]{1,0:T(8,128)(2,1)S(1)} %get-tuple-element.213), channel_id=1, source_target_pairs={{0,2},{1,3},{2,0},{3,1},{4,6},{5,7},{6,4},{7,5},{8,10},{9,11},{10,... | collective-permute-start | bytes 368648 | tf_op jit(solution)/shard_map/ppermute | solution.py:327
  42.1 15.6 %collective-permute-start.16 = (bf16[32,1920]{1,0:T(8,128)(2,1)S(1)}, bf16[32,1920]{1,0:T(8,128)(2,1)S(1)}, u32[]{:S(2)}, u32[]{:S(2)}) collective-permute-start(bf16[32,1920]{1,0:T(8,128)(2,1)S(1)} %get-tuple-element.214), channel_id=1, source_target_pairs={{0,4},{1,5},{2,6},{3,7},{4,0},{5,1},{6,2},{7,3},{8,12},{9,13},{10,... | collective-permute-start | bytes 368648 | tf_op jit(solution)/shard_map/ppermute | solution.py:327
  49.2 12.2 %collective-permute-start.19 = (bf16[32,1920]{1,0:T(8,128)(2,1)S(1)}, bf16[32,1920]{1,0:T(8,128)(2,1)S(1)}, u32[]{:S(2)}, u32[]{:S(2)}) collective-permute-start(bf16[32,1920]{1,0:T(8,128)(2,1)S(1)} %get-tuple-element.217), channel_id=1, source_target_pairs={{0,14},{1,15},{2,12},{3,13},{4,10},{5,11},{6,8},{7,9},{8,22},{9,23... | collective-permute-start | bytes 368648 | tf_op jit(solution)/shard_map/ppermute | solution.py:327
  50.7 10.8 %collective-permute-start.14 = (bf16[32,1920]{1,0:T(8,128)(2,1)S(1)}, bf16[32,1920]{1,0:T(8,128)(2,1)S(1)}, u32[]{:S(2)}, u32[]{:S(2)}) collective-permute-start(bf16[32,1920]{1,0:T(8,128)(2,1)S(1)} %get-tuple-element.212.refs_2_), channel_id=1, source_target_pairs={{0,8},{1,9},{2,10},{3,11},{4,12},{5,13},{6,14},{7,15},{8,16},{9,17... | collective-permute-start | bytes 368648 | tf_op jit(solution)/shard_map/ppermute | solution.py:327
  59.2 7.6 %collective-permute-start.17 = (bf16[32,1920]{1,0:T(8,128)(2,1)S(1)}, bf16[32,1920]{1,0:T(8,128)(2,1)S(1)}, u32[]{:S(2)}, u32[]{:S(2)}) collective-permute-start(bf16[32,1920]{1,0:T(8,128)(2,1)S(1)} %get-tuple-element.215), channel_id=1, source_target_pairs={{0,10},{1,11},{2,8},{3,9},{4,14},{5,15},{6,12},{7,13},{8,18},{9,19... | collective-permute-start | bytes 368648 | tf_op jit(solution)/shard_map/ppermute | solution.py:327
  59.2 10.1 %collective-permute-start.18 = (bf16[32,1920]{1,0:T(8,128)(2,1)S(1)}, bf16[32,1920]{1,0:T(8,128)(2,1)S(1)}, u32[]{:S(2)}, u32[]{:S(2)}) collective-permute-start(bf16[32,1920]{1,0:T(8,128)(2,1)S(1)} %get-tuple-element.216), channel_id=1, source_target_pairs={{0,12},{1,13},{2,14},{3,15},{4,8},{5,9},{6,10},{7,11},{8,20},{9,21... | collective-permute-start | bytes 368648 | tf_op jit(solution)/shard_map/ppermute | solution.py:327
  61.5 7.8 %collective-permute-start.23 = (bf16[32,1920]{1,0:T(8,128)(2,1)S(1)}, bf16[32,1920]{1,0:T(8,128)(2,1)S(1)}, u32[]{:S(2)}, u32[]{:S(2)}) collective-permute-start(bf16[32,1920]{1,0:T(8,128)(2,1)S(1)} %collective-permute-done.19.refs_3_), channel_id=1, source_target_pairs={{0,1},{1,0},{2,3},{3,2},{4,5},{5,4},{6,7},{7,6},{8,9},{9,8},{10,11... | collective-permute-start | bytes 368648 | tf_op jit(solution)/shard_map/ppermute | solution.py:327
  61.5 7.8 %collective-permute-start.20 = (bf16[32,1920]{1,0:T(8,128)(2,1)S(1)}, bf16[32,1920]{1,0:T(8,128)(2,1)S(1)}, u32[]{:S(2)}, u32[]{:S(2)}) collective-permute-start(bf16[32,1920]{1,0:T(8,128)(2,1)S(1)} %collective-permute-done.14.refs_0_), channel_id=1, source_target_pairs={{0,1},{1,0},{2,3},{3,2},{4,5},{5,4},{6,7},{7,6},{8,9},{9,8},{10,11... | collective-permute-start | bytes 368648 | tf_op jit(solution)/shard_map/ppermute | solution.py:327
  71.5 8.1 %collective-permute-start.24 = (bf16[32,1920]{1,0:T(8,128)(2,1)S(1)}, bf16[32,1920]{1,0:T(8,128)(2,1)S(1)}, u32[]{:S(2)}, u32[]{:S(2)}) collective-permute-start(bf16[32,1920]{1,0:T(8,128)(2,1)S(1)} %get-tuple-element.219), channel_id=1, source_target_pairs={{0,6},{1,7},{2,4},{3,5},{4,2},{5,3},{6,0},{7,1},{8,14},{9,15},{10,... | collective-permute-start | bytes 368648 | tf_op jit(solution)/shard_map/ppermute | solution.py:327
  72.8 11.8 %collective-permute-start.26 = (bf16[32,1920]{1,0:T(8,128)(2,1)S(1)}, bf16[32,1920]{1,0:T(8,128)(2,1)S(1)}, u32[]{:S(2)}, u32[]{:S(2)}) collective-permute-start(bf16[32,1920]{1,0:T(8,128)(2,1)S(1)} %get-tuple-element.221), channel_id=1, source_target_pairs={{0,2},{1,3},{2,0},{3,1},{4,6},{5,7},{6,4},{7,5},{8,10},{9,11},{10,... | collective-permute-start | bytes 368648 | tf_op jit(solution)/shard_map/ppermute | solution.py:327
  72.8 11.8 %collective-permute-start.27 = (bf16[32,1920]{1,0:T(8,128)(2,1)S(1)}, bf16[32,1920]{1,0:T(8,128)(2,1)S(1)}, u32[]{:S(2)}, u32[]{:S(2)}) collective-permute-start(bf16[32,1920]{1,0:T(8,128)(2,1)S(1)} %get-tuple-element.222), channel_id=1, source_target_pairs={{0,4},{1,5},{2,6},{3,7},{4,0},{5,1},{6,2},{7,3},{8,12},{9,13},{10,... | collective-permute-start | bytes 368648 | tf_op jit(solution)/shard_map/ppermute | solution.py:327
  81.1 9.5 %collective-permute-start.30 = (bf16[32,1920]{1,0:T(8,128)(2,1)S(1)}, bf16[32,1920]{1,0:T(8,128)(2,1)S(1)}, u32[]{:S(2)}, u32[]{:S(2)}) collective-permute-start(bf16[32,1920]{1,0:T(8,128)(2,1)S(1)} %get-tuple-element.225), channel_id=1, source_target_pairs={{0,14},{1,15},{2,12},{3,13},{4,10},{5,11},{6,8},{7,9},{8,22},{9,23... | collective-permute-start | bytes 368648 | tf_op jit(solution)/shard_map/ppermute | solution.py:327
  83.0 11.6 %collective-permute-start.25 = (bf16[32,1920]{1,0:T(8,128)(2,1)S(1)}, bf16[32,1920]{1,0:T(8,128)(2,1)S(1)}, u32[]{:S(2)}, u32[]{:S(2)}) collective-permute-start(bf16[32,1920]{1,0:T(8,128)(2,1)S(1)} %get-tuple-element.220.refs_2_), channel_id=1, source_target_pairs={{0,8},{1,9},{2,10},{3,11},{4,12},{5,13},{6,14},{7,15},{8,16},{9,17... | collective-permute-start | bytes 368648 | tf_op jit(solution)/shard_map/ppermute | solution.py:327
  86.1 8.5 %collective-permute-start.28 = (bf16[32,1920]{1,0:T(8,128)(2,1)S(1)}, bf16[32,1920]{1,0:T(8,128)(2,1)S(1)}, u32[]{:S(2)}, u32[]{:S(2)}) collective-permute-start(bf16[32,1920]{1,0:T(8,128)(2,1)S(1)} %get-tuple-element.223), channel_id=1, source_target_pairs={{0,10},{1,11},{2,8},{3,9},{4,14},{5,15},{6,12},{7,13},{8,18},{9,19... | collective-permute-start | bytes 368648 | tf_op jit(solution)/shard_map/ppermute | solution.py:327
  86.2 10.2 %collective-permute-start.29 = (bf16[32,1920]{1,0:T(8,128)(2,1)S(1)}, bf16[32,1920]{1,0:T(8,128)(2,1)S(1)}, u32[]{:S(2)}, u32[]{:S(2)}) collective-permute-start(bf16[32,1920]{1,0:T(8,128)(2,1)S(1)} %get-tuple-element.224), channel_id=1, source_target_pairs={{0,12},{1,13},{2,14},{3,15},{4,8},{5,9},{6,10},{7,11},{8,20},{9,21... | collective-permute-start | bytes 368648 | tf_op jit(solution)/shard_map/ppermute | solution.py:327
  90.6 5.8 %collective-permute-start.34 = (bf16[32,1920]{1,0:T(8,128)(2,1)S(1)}, bf16[32,1920]{1,0:T(8,128)(2,1)S(1)}, u32[]{:S(2)}, u32[]{:S(2)}) collective-permute-start(bf16[32,1920]{1,0:T(8,128)(2,1)S(1)} %collective-permute-done.30.refs_3_), channel_id=1, source_target_pairs={{0,1},{1,0},{2,3},{3,2},{4,5},{5,4},{6,7},{7,6},{8,9},{9,8},{10,11... | collective-permute-start | bytes 368648 | tf_op jit(solution)/shard_map/ppermute | solution.py:327
  98.6 8.1 %collective-permute-start.35 = (bf16[32,1920]{1,0:T(8,128)(2,1)S(1)}, bf16[32,1920]{1,0:T(8,128)(2,1)S(1)}, u32[]{:S(2)}, u32[]{:S(2)}) collective-permute-start(bf16[32,1920]{1,0:T(8,128)(2,1)S(1)} %get-tuple-element.227), channel_id=1, source_target_pairs={{0,6},{1,7},{2,4},{3,5},{4,2},{5,3},{6,0},{7,1},{8,14},{9,15},{10,... | collective-permute-start | bytes 368648 | tf_op jit(solution)/shard_map/ppermute | solution.py:327
  100.4 13.3 %collective-permute-start.37 = (bf16[32,1920]{1,0:T(8,128)(2,1)S(1)}, bf16[32,1920]{1,0:T(8,128)(2,1)S(1)}, u32[]{:S(2)}, u32[]{:S(2)}) collective-permute-start(bf16[32,1920]{1,0:T(8,128)(2,1)S(1)} %get-tuple-element.236), channel_id=1, source_target_pairs={{0,2},{1,3},{2,0},{3,1},{4,6},{5,7},{6,4},{7,5},{8,10},{9,11},{10,... | collective-permute-start | bytes 368648 | tf_op jit(solution)/shard_map/ppermute | solution.py:327
  100.4 13.3 %collective-permute-start.38 = (bf16[32,1920]{1,0:T(8,128)(2,1)S(1)}, bf16[32,1920]{1,0:T(8,128)(2,1)S(1)}, u32[]{:S(2)}, u32[]{:S(2)}) collective-permute-start(bf16[32,1920]{1,0:T(8,128)(2,1)S(1)} %get-tuple-element.237), channel_id=1, source_target_pairs={{0,4},{1,5},{2,6},{3,7},{4,0},{5,1},{6,2},{7,3},{8,12},{9,13},{10,... | collective-permute-start | bytes 368648 | tf_op jit(solution)/shard_map/ppermute | solution.py:327
  110.4 10.6 %collective-permute-start.41 = (bf16[32,1920]{1,0:T(8,128)(2,1)S(1)}, bf16[32,1920]{1,0:T(8,128)(2,1)S(1)}, u32[]{:S(2)}, u32[]{:S(2)}) collective-permute-start(bf16[32,1920]{1,0:T(8,128)(2,1)S(1)} %get-tuple-element.247), channel_id=1, source_target_pairs={{0,14},{1,15},{2,12},{3,13},{4,10},{5,11},{6,8},{7,9},{8,6},{9,7},... | collective-permute-start | bytes 368648 | tf_op jit(solution)/shard_map/ppermute | solution.py:327
  112.0 9.6 %collective-permute-start.36 = (bf16[32,1920]{1,0:T(8,128)(2,1)S(1)}, bf16[32,1920]{1,0:T(8,128)(2,1)S(1)}, u32[]{:S(2)}, u32[]{:S(2)}) collective-permute-start(bf16[32,1920]{1,0:T(8,128)(2,1)S(1)} %get-tuple-element.235.refs_2_.refs_11_), channel_id=1, source_target_pairs={{0,8},{1,9},{2,10},{3,11},{4,12},{5,13},{6,14},{7,15},{8,0},{9,1},... | collective-permute-start | bytes 368648 | tf_op jit(solution)/shard_map/ppermute | solution.py:327
  117.4 6.1 %collective-permute-start.39 = (bf16[32,1920]{1,0:T(8,128)(2,1)S(1)}, bf16[32,1920]{1,0:T(8,128)(2,1)S(1)}, u32[]{:S(2)}, u32[]{:S(2)}) collective-permute-start(bf16[32,1920]{1,0:T(8,128)(2,1)S(1)} %get-tuple-element.245), channel_id=1, source_target_pairs={{0,10},{1,11},{2,8},{3,9},{4,14},{5,15},{6,12},{7,13},{8,2},{9,3},... | collective-permute-start | bytes 368648 | tf_op jit(solution)/shard_map/ppermute | solution.py:327
  118.1 8.0 %collective-permute-start.40 = (bf16[32,1920]{1,0:T(8,128)(2,1)S(1)}, bf16[32,1920]{1,0:T(8,128)(2,1)S(1)}, u32[]{:S(2)}, u32[]{:S(2)}) collective-permute-start(bf16[32,1920]{1,0:T(8,128)(2,1)S(1)} %get-tuple-element.246), channel_id=1, source_target_pairs={{0,12},{1,13},{2,14},{3,15},{4,8},{5,9},{6,10},{7,11},{8,4},{9,5},... | collective-permute-start | bytes 368648 | tf_op jit(solution)/shard_map/ppermute | solution.py:327
  121.1 5.0 %collective-permute-start.45 = (bf16[32,1920]{1,0:T(8,128)(2,1)S(1)}, bf16[32,1920]{1,0:T(8,128)(2,1)S(1)}, u32[]{:S(2)}, u32[]{:S(2)}) collective-permute-start(bf16[32,1920]{1,0:T(8,128)(2,1)S(1)} %collective-permute-done.41.refs_3_), channel_id=1, source_target_pairs={{0,1},{1,0},{2,3},{3,2},{4,5},{5,4},{6,7},{7,6},{8,9},{9,8},{10,11... | collective-permute-start | bytes 368648 | tf_op jit(solution)/shard_map/ppermute | solution.py:327
  121.5 4.5 %collective-permute-start.42 = (bf16[32,1920]{1,0:T(8,128)(2,1)S(1)}, bf16[32,1920]{1,0:T(8,128)(2,1)S(1)}, u32[]{:S(2)}, u32[]{:S(2)}) collective-permute-start(bf16[32,1920]{1,0:T(8,128)(2,1)S(1)} %collective-permute-done.36.refs_0_), channel_id=1, source_target_pairs={{0,1},{1,0},{2,3},{3,2},{4,5},{5,4},{6,7},{7,6},{8,9},{9,8},{10,11... | collective-permute-start | bytes 368648 | tf_op jit(solution)/shard_map/ppermute | solution.py:327
  128.3 8.1 %collective-permute-start.46 = (bf16[32,1920]{1,0:T(8,128)(2,1)S(1)}, bf16[32,1920]{1,0:T(8,128)(2,1)S(1)}, u32[]{:S(2)}, u32[]{:S(2)}) collective-permute-start(bf16[32,1920]{1,0:T(8,128)(2,1)S(1)} %get-tuple-element.249), channel_id=1, source_target_pairs={{0,6},{1,7},{2,4},{3,5},{4,2},{5,3},{6,0},{7,1},{8,14},{9,15},{10,... | collective-permute-start | bytes 368648 | tf_op jit(solution)/shard_map/ppermute | solution.py:327
  129.1 15.7 %collective-permute-start.48 = (bf16[32,1920]{1,0:T(8,128)(2,1)S(1)}, bf16[32,1920]{1,0:T(8,128)(2,1)S(1)}, u32[]{:S(2)}, u32[]{:S(2)}) collective-permute-start(bf16[32,1920]{1,0:T(8,128)(2,1)S(1)} %get-tuple-element.261), channel_id=1, source_target_pairs={{0,2},{1,3},{2,0},{3,1},{4,6},{5,7},{6,4},{7,5},{8,10},{9,11},{10,... | collective-permute-start | bytes 368648 | tf_op jit(solution)/shard_map/ppermute | solution.py:327
  130.1 14.8 %collective-permute-start.49 = (bf16[32,1920]{1,0:T(8,128)(2,1)S(1)}, bf16[32,1920]{1,0:T(8,128)(2,1)S(1)}, u32[]{:S(2)}, u32[]{:S(2)}) collective-permute-start(bf16[32,1920]{1,0:T(8,128)(2,1)S(1)} %get-tuple-element.262), channel_id=1, source_target_pairs={{0,4},{1,5},{2,6},{3,7},{4,0},{5,1},{6,2},{7,3},{8,12},{9,13},{10,... | collective-permute-start | bytes 368648 | tf_op jit(solution)/shard_map/ppermute | solution.py:327
  140.8 12.2 %collective-permute-start.52 = (bf16[32,1920]{1,0:T(8,128)(2,1)S(1)}, bf16[32,1920]{1,0:T(8,128)(2,1)S(1)}, u32[]{:S(2)}, u32[]{:S(2)}) collective-permute-start(bf16[32,1920]{1,0:T(8,128)(2,1)S(1)} %get-tuple-element.275), channel_id=1, source_target_pairs={{0,30},{1,31},{2,28},{3,29},{4,26},{5,27},{6,24},{7,25},{8,6},{9,7... | collective-permute-start | bytes 368648 | tf_op jit(solution)/shard_map/ppermute | solution.py:327
  149.2 6.7 %collective-permute-start.50 = (bf16[32,1920]{1,0:T(8,128)(2,1)S(1)}, bf16[32,1920]{1,0:T(8,128)(2,1)S(1)}, u32[]{:S(2)}, u32[]{:S(2)}) collective-permute-start(bf16[32,1920]{1,0:T(8,128)(2,1)S(1)} %get-tuple-element.273), channel_id=1, source_target_pairs={{0,26},{1,27},{2,24},{3,25},{4,30},{5,31},{6,28},{7,29},{8,2},{9,3... | collective-permute-start | bytes 368648 | tf_op jit(solution)/shard_map/ppermute | solution.py:327
  150.5 7.9 %collective-permute-start.51 = (bf16[32,1920]{1,0:T(8,128)(2,1)S(1)}, bf16[32,1920]{1,0:T(8,128)(2,1)S(1)}, u32[]{:S(2)}, u32[]{:S(2)}) collective-permute-start(bf16[32,1920]{1,0:T(8,128)(2,1)S(1)} %get-tuple-element.274), channel_id=1, source_target_pairs={{0,28},{1,29},{2,30},{3,31},{4,24},{5,25},{6,26},{7,27},{8,4},{9,5... | collective-permute-start | bytes 368648 | tf_op jit(solution)/shard_map/ppermute | solution.py:327
  151.4 8.7 %collective-permute-start.47 = (bf16[32,1920]{1,0:T(8,128)(2,1)S(1)}, bf16[32,1920]{1,0:T(8,128)(2,1)S(1)}, u32[]{:S(2)}, u32[]{:S(2)}) collective-permute-start(bf16[32,1920]{1,0:T(8,128)(2,1)S(1)} %get-tuple-element.260.refs_2_.refs_14_), channel_id=1, source_target_pairs={{0,24},{1,25},{2,26},{3,27},{4,28},{5,29},{6,30},{7,31},{8,0},{9,1... | collective-permute-start | bytes 368648 | tf_op jit(solution)/shard_map/ppermute | solution.py:327
  152.9 7.1 %collective-permute-start.56 = (bf16[32,1920]{1,0:T(8,128)(2,1)S(1)}, bf16[32,1920]{1,0:T(8,128)(2,1)S(1)}, u32[]{:S(2)}, u32[]{:S(2)}) collective-permute-start(bf16[32,1920]{1,0:T(8,128)(2,1)S(1)} %collective-permute-done.52.refs_3_), channel_id=1, source_target_pairs={{0,1},{1,0},{2,3},{3,2},{4,5},{5,4},{6,7},{7,6},{8,9},{9,8},{10,11... | collective-permute-start | bytes 368648 | tf_op jit(solution)/shard_map/ppermute | solution.py:327
  162.2 8.1 %collective-permute-start.57 = (bf16[32,1920]{1,0:T(8,128)(2,1)S(1)}, bf16[32,1920]{1,0:T(8,128)(2,1)S(1)}, u32[]{:S(2)}, u32[]{:S(2)}) collective-permute-start(bf16[32,1920]{1,0:T(8,128)(2,1)S(1)} %get-tuple-element.277), channel_id=1, source_target_pairs={{0,6},{1,7},{2,4},{3,5},{4,2},{5,3},{6,0},{7,1},{8,14},{9,15},{10,... | collective-permute-start | bytes 368648 | tf_op jit(solution)/shard_map/ppermute | solution.py:327
  163.5 11.8 %collective-permute-start.59 = (bf16[32,1920]{1,0:T(8,128)(2,1)S(1)}, bf16[32,1920]{1,0:T(8,128)(2,1)S(1)}, u32[]{:S(2)}, u32[]{:S(2)}) collective-permute-start(bf16[32,1920]{1,0:T(8,128)(2,1)S(1)} %get-tuple-element.284), channel_id=1, source_target_pairs={{0,2},{1,3},{2,0},{3,1},{4,6},{5,7},{6,4},{7,5},{8,10},{9,11},{10,... | collective-permute-start | bytes 368648 | tf_op jit(solution)/shard_map/ppermute | solution.py:327
  163.5 11.8 %collective-permute-start.60 = (bf16[32,1920]{1,0:T(8,128)(2,1)S(1)}, bf16[32,1920]{1,0:T(8,128)(2,1)S(1)}, u32[]{:S(2)}, u32[]{:S(2)}) collective-permute-start(bf16[32,1920]{1,0:T(8,128)(2,1)S(1)} %get-tuple-element.285), channel_id=1, source_target_pairs={{0,4},{1,5},{2,6},{3,7},{4,0},{5,1},{6,2},{7,3},{8,12},{9,13},{10,... | collective-permute-start | bytes 368648 | tf_op jit(solution)/shard_map/ppermute | solution.py:327
  172.5 9.9 %collective-permute-start.63 = (bf16[32,1920]{1,0:T(8,128)(2,1)S(1)}, bf16[32,1920]{1,0:T(8,128)(2,1)S(1)}, u32[]{:S(2)}, u32[]{:S(2)}) collective-permute-start(bf16[32,1920]{1,0:T(8,128)(2,1)S(1)} %get-tuple-element.293), channel_id=1, source_target_pairs={{0,30},{1,31},{2,28},{3,29},{4,26},{5,27},{6,24},{7,25},{8,6},{9,7... | collective-permute-start | bytes 368648 | tf_op jit(solution)/shard_map/ppermute | solution.py:327
  174.8 10.3 %collective-permute-start.58 = (bf16[32,1920]{1,0:T(8,128)(2,1)S(1)}, bf16[32,1920]{1,0:T(8,128)(2,1)S(1)}, u32[]{:S(2)}, u32[]{:S(2)}) collective-permute-start(bf16[32,1920]{1,0:T(8,128)(2,1)S(1)} %get-tuple-element.283.refs_12_), channel_id=1, source_target_pairs={{0,24},{1,25},{2,26},{3,27},{4,28},{5,29},{6,30},{7,31},{8,0},{9,1... | collective-permute-start | bytes 368648 | tf_op jit(solution)/shard_map/ppermute | solution.py:327
  177.5 7.6 %collective-permute-start.61 = (bf16[32,1920]{1,0:T(8,128)(2,1)S(1)}, bf16[32,1920]{1,0:T(8,128)(2,1)S(1)}, u32[]{:S(2)}, u32[]{:S(2)}) collective-permute-start(bf16[32,1920]{1,0:T(8,128)(2,1)S(1)} %get-tuple-element.291), channel_id=1, source_target_pairs={{0,26},{1,27},{2,24},{3,25},{4,30},{5,31},{6,28},{7,29},{8,2},{9,3... | collective-permute-start | bytes 368648 | tf_op jit(solution)/shard_map/ppermute | solution.py:327
  180.1 6.7 %collective-permute-start.62 = (bf16[32,1920]{1,0:T(8,128)(2,1)S(1)}, bf16[32,1920]{1,0:T(8,128)(2,1)S(1)}, u32[]{:S(2)}, u32[]{:S(2)}) collective-permute-start(bf16[32,1920]{1,0:T(8,128)(2,1)S(1)} %get-tuple-element.292), channel_id=1, source_target_pairs={{0,28},{1,29},{2,30},{3,31},{4,24},{5,25},{6,26},{7,27},{8,4},{9,5... | collective-permute-start | bytes 368648 | tf_op jit(solution)/shard_map/ppermute | solution.py:327
  189.0 7.9 %collective-permute-start.68 = (bf16[32,1920]{1,0:T(8,128)(2,1)S(1)}, bf16[32,1920]{1,0:T(8,128)(2,1)S(1)}, u32[]{:S(2)}, u32[]{:S(2)}) collective-permute-start(bf16[32,1920]{1,0:T(8,128)(2,1)S(1)} %get-tuple-element.295), channel_id=1, source_target_pairs={{0,6},{1,7},{2,4},{3,5},{4,2},{5,3},{6,0},{7,1},{8,14},{9,15},{10,... | collective-permute-start | bytes 368648 | tf_op jit(solution)/shard_map/ppermute | solution.py:327
  193.1 13.1 %collective-permute-start.70 = (bf16[32,1920]{1,0:T(8,128)(2,1)S(1)}, bf16[32,1920]{1,0:T(8,128)(2,1)S(1)}, u32[]{:S(2)}, u32[]{:S(2)}) collective-permute-start(bf16[32,1920]{1,0:T(8,128)(2,1)S(1)} %get-tuple-element.336), channel_id=1, source_target_pairs={{0,2},{1,3},{2,0},{3,1},{4,6},{5,7},{6,4},{7,5},{8,10},{9,11},{10,... | collective-permute-start | bytes 368648 | tf_op jit(solution)/shard_map/ppermute | solution.py:327
  194.1 12.2 %collective-permute-start.71 = (bf16[32,1920]{1,0:T(8,128)(2,1)S(1)}, bf16[32,1920]{1,0:T(8,128)(2,1)S(1)}, u32[]{:S(2)}, u32[]{:S(2)}) collective-permute-start(bf16[32,1920]{1,0:T(8,128)(2,1)S(1)} %get-tuple-element.337), channel_id=1, source_target_pairs={{0,4},{1,5},{2,6},{3,7},{4,0},{5,1},{6,2},{7,3},{8,12},{9,13},{10,... | collective-permute-start | bytes 368648 | tf_op jit(solution)/shard_map/ppermute | solution.py:327
  199.1 13.9 %collective-permute-start.74 = (bf16[32,1920]{1,0:T(8,128)(2,1)S(1)}, bf16[32,1920]{1,0:T(8,128)(2,1)S(1)}, u32[]{:S(2)}, u32[]{:S(2)}) collective-permute-start(bf16[32,1920]{1,0:T(8,128)(2,1)S(1)} %get-tuple-element.345), channel_id=1, source_target_pairs={{0,30},{1,31},{2,28},{3,29},{4,26},{5,27},{6,24},{7,25},{8,6},{9,7... | collective-permute-start | bytes 368648 | tf_op jit(solution)/shard_map/ppermute | solution.py:327
  205.9 7.0 %collective-permute-start.69 = (bf16[32,1920]{1,0:T(8,128)(2,1)S(1)}, bf16[32,1920]{1,0:T(8,128)(2,1)S(1)}, u32[]{:S(2)}, u32[]{:S(2)}) collective-permute-start(bf16[32,1920]{1,0:T(8,128)(2,1)S(1)} %get-tuple-element.335.refs_12_), channel_id=1, source_target_pairs={{0,24},{1,25},{2,26},{3,27},{4,28},{5,29},{6,30},{7,31},{8,0},{9,1... | collective-permute-start | bytes 368648 | tf_op jit(solution)/shard_map/ppermute | solution.py:327
  208.4 7.0 %collective-permute-start.72 = (bf16[32,1920]{1,0:T(8,128)(2,1)S(1)}, bf16[32,1920]{1,0:T(8,128)(2,1)S(1)}, u32[]{:S(2)}, u32[]{:S(2)}) collective-permute-start(bf16[32,1920]{1,0:T(8,128)(2,1)S(1)} %get-tuple-element.343), channel_id=1, source_target_pairs={{0,26},{1,27},{2,24},{3,25},{4,30},{5,31},{6,28},{7,29},{8,2},{9,3... | collective-permute-start | bytes 368648 | tf_op jit(solution)/shard_map/ppermute | solution.py:327
  210.3 8.1 %collective-permute-start.73 = (bf16[32,1920]{1,0:T(8,128)(2,1)S(1)}, bf16[32,1920]{1,0:T(8,128)(2,1)S(1)}, u32[]{:S(2)}, u32[]{:S(2)}) collective-permute-start(bf16[32,1920]{1,0:T(8,128)(2,1)S(1)} %get-tuple-element.344), channel_id=1, source_target_pairs={{0,28},{1,29},{2,30},{3,31},{4,24},{5,25},{6,26},{7,27},{8,4},{9,5... | collective-permute-start | bytes 368648 | tf_op jit(solution)/shard_map/ppermute | solution.py:327
  212.9 5.4 %collective-permute-start.78 = (bf16[32,1920]{1,0:T(8,128)(2,1)S(1)}, bf16[32,1920]{1,0:T(8,128)(2,1)S(1)}, u32[]{:S(2)}, u32[]{:S(2)}) collective-permute-start(bf16[32,1920]{1,0:T(8,128)(2,1)S(1)} %collective-permute-done.74.refs_3_), channel_id=1, source_target_pairs={{0,1},{1,0},{2,3},{3,2},{4,5},{5,4},{6,7},{7,6},{8,9},{9,8},{10,11... | collective-permute-start | bytes 368648 | tf_op jit(solution)/shard_map/ppermute | solution.py:327
  212.9 5.4 %collective-permute-start.75 = (bf16[32,1920]{1,0:T(8,128)(2,1)S(1)}, bf16[32,1920]{1,0:T(8,128)(2,1)S(1)}, u32[]{:S(2)}, u32[]{:S(2)}) collective-permute-start(bf16[32,1920]{1,0:T(8,128)(2,1)S(1)} %collective-permute-done.69.refs_0_), channel_id=1, source_target_pairs={{0,1},{1,0},{2,3},{3,2},{4,5},{5,4},{6,7},{7,6},{8,9},{9,8},{10,11... | collective-permute-start | bytes 368648 | tf_op jit(solution)/shard_map/ppermute | solution.py:327
  220.5 11.6 %collective-permute-start.79 = (bf16[32,1920]{1,0:T(8,128)(2,1)S(1)}, bf16[32,1920]{1,0:T(8,128)(2,1)S(1)}, u32[]{:S(2)}, u32[]{:S(2)}) collective-permute-start(bf16[32,1920]{1,0:T(8,128)(2,1)S(1)} %get-tuple-element.347), channel_id=1, source_target_pairs={{0,6},{1,7},{2,4},{3,5},{4,2},{5,3},{6,0},{7,1},{8,14},{9,15},{10,... | collective-permute-start | bytes 368648 | tf_op jit(solution)/shard_map/ppermute | solution.py:327
  222.3 10.9 %collective-permute-start.80 = (bf16[32,1920]{1,0:T(8,128)(2,1)S(1)}, bf16[32,1920]{1,0:T(8,128)(2,1)S(1)}, u32[]{:S(2)}, u32[]{:S(2)}) collective-permute-start(bf16[32,1920]{1,0:T(8,128)(2,1)S(1)} %get-tuple-element.384), channel_id=1, source_target_pairs={{0,2},{1,3},{2,0},{3,1},{4,6},{5,7},{6,4},{7,5},{8,10},{9,11},{10,... | collective-permute-start | bytes 368648 | tf_op jit(solution)/shard_map/ppermute | solution.py:327
  222.3 10.9 %collective-permute-start.81 = (bf16[32,1920]{1,0:T(8,128)(2,1)S(1)}, bf16[32,1920]{1,0:T(8,128)(2,1)S(1)}, u32[]{:S(2)}, u32[]{:S(2)}) collective-permute-start(bf16[32,1920]{1,0:T(8,128)(2,1)S(1)} %get-tuple-element.385), channel_id=1, source_target_pairs={{0,4},{1,5},{2,6},{3,7},{4,0},{5,1},{6,2},{7,3},{8,12},{9,13},{10,... | collective-permute-start | bytes 368648 | tf_op jit(solution)/shard_map/ppermute | solution.py:327
  (22 other events, 62.1 us)

commit v3 on v2

--- a/solution.py
+++ b/solution.py
@@ -70,9 +70,10 @@
     return jax.nn.sigmoid(jnp.sum(normed.astype(f32) * column, axis=-1, keepdims=True))
 
 
-def forward_kernel(count, chained, gain_ref, column_ref, in_ref, out_ref, *refs):
+def forward_kernel(count, chained, passes, gain_ref, column_ref, in_ref, out_ref, *refs):
     arrived, refs = refs[:count], refs[count + chained :]
-    sent, refs = refs[:count], refs[count:]
+    if passes:
+        sent, refs = refs[:count], refs[count:]
     hidden_ref, joined_ref, produced_ref, inverse_ref, gate_ref, normed_ref, activated_ref = refs
     inner = out_ref.shape[0]
     hidden = joined_rows(arrived, in_ref.shape[0])
@@ -83,8 +84,9 @@
     gate_part = joined[:, :inner]
     activated = (gate_part * jax.nn.sigmoid(gate_part) * joined[:, inner:]).astype(bf16)
     produced = jnp.dot(activated, out_ref[...], preferred_element_type=f32).astype(bf16)
-    output = (hidden.astype(f32) + share * produced.astype(f32)).astype(bf16)
-    split_rows(sent, output)
+    if passes:
+        output = (hidden.astype(f32) + share * produced.astype(f32)).astype(bf16)
+        split_rows(sent, output)
     hidden_ref[...] = hidden
     joined_ref[...] = joined
     produced_ref[...] = produced
@@ -407,12 +409,14 @@
         name="fetch",
     )(own_in, own_out)
 
-    def forward(arrived, earlier):
+    def forward(step, arrived, earlier):
         many = len(arrived)
+        passes = step <= last
+        sent = many if passes else 0
         form = lambda length, dtype: jax.ShapeDtypeStruct((many * size, length), dtype)
         out = pl.pallas_call(
-            functools.partial(forward_kernel, many, len(earlier)),
-            out_shape=[piece] * many
+            functools.partial(forward_kernel, many, len(earlier), passes),
+            out_shape=[piece] * sent
             + [
                 form(width, bf16),
                 form(double, f32),
@@ -423,11 +427,11 @@
                 form(inner, bf16),
             ],
             in_specs=[VMEM] * (4 + many) + [ANY] * len(earlier),
-            out_specs=[VMEM] * (many + 7),
+            out_specs=[VMEM] * (sent + 7),
             compiler_params=params,
             name="forward",
         )(gain_row, column, own_in, own_out, *arrived, *earlier)
-        return out[:many], out[many:]
+        return out[:sent], out[sent:]
 
     def record(step, grads, saved, kept):
         sources = sources_of(step, saved)
@@ -531,7 +535,7 @@
             here = [arrived[k] for k in part]
             passed = None
             if step < last + micros:
-                passed, saved = forward(here, earlier)
+                passed, saved = forward(step, here, earlier)
                 forwards[index].append(saved)
             if step >= last:
                 entered = None

time: 239 us -> 238 us (level)
  starting transfers between devices: 99.8 us -> 94.5 us
  waiting for transfers between devices: 73.5 us -> 78.6 us
    ppermute x82, starting transfers between devices: 99.8 us -> 94.5 us  [permuted(): return lax.ppermute(block, ('pipe', 'expert'), route)]
    ppermute x82, waiting for transfers between devices: 73.5 us -> 78.6 us  [permuted(): return lax.ppermute(block, ('pipe', 'expert'), route)]
  transfers between devices with their start and end apart: 82 -> 82, of which waited for: 32 -> 35; matrix products, arithmetic and copies ran while one was open for 0% -> 0% of each run, Pallas kernels for 19% -> 19%
where the time goes in v3:
time: 238 us; the launch traced here: 237 us
  starting transfers between devices  94.5 us (40%)
  waiting for transfers between devices  78.6 us (33%)
  Pallas kernels  57.3 us (24%)
  local copies, waits for them, and re-layouts  3.8 us (2%)
    ppermute x82, starting transfers between devices, permuted(): return lax.ppermute(block, ('pipe', 'expert'), route)  94.5 us
    ppermute x82, waiting for transfers between devices, permuted(): return lax.ppermute(block, ('pipe', 'expert'), route)  78.6 us
    pallas_call x10, Pallas kernels, backward(): pl.pallas_call(functools.partial(backward_kernel, plan), out_shape=[piece...  19.6 us
    pallas_call x10, Pallas kernels, forward(): pl.pallas_call(functools.partial(forward_kernel, many, len(earlier), pass...  14.9 us
    pallas_call x8, Pallas kernels, record(): pl.pallas_call(functools.partial(record_kernel, (layers, micros, len(sour...  7.1 us
    pallas_call x7, Pallas kernels, resort(): pl.pallas_call(functools.partial(resort_kernel, (len(arrived), count, wid...  6.05 us
  transfers between devices with their start and end apart: 82, of which 35 were waited for; matrix products, arithmetic and copies ran while one was open for 0% of the time, Pallas kernels for 19%

profile of v3, /device:TPU:0, one launch (start us, length us, event | category | flops | bytes accessed | tf_op | source)
XLA Modules:
  0.0 237.4 jit_solution(15318127424425266096)
XLA Ops:
  2.6 2.2 copy-done
  4.8 1.6 copy-done.2
  6.9 1.6 prepare.1
  8.4 5.1 %collective-permute-start.2 = (bf16[32,1920]{1,0:T(8,128)(2,1)S(1)}, bf16[32,1920]{1,0:T(8,128)(2,1)S(1)}, u32[]{:S(2)}, u32[]{:S(2)}) collective-permute-start(bf16[32,1920]{1,0:T(8,128)(2,1)S(1)} %get-tuple-element.202), channel_id=1, source_target_pairs={{0,6},{1,7},{2,4},{3,5},{4,2},{5,3},{6,0},{7,1},{8,14},{9,15},{10,... | collective-permute-start | bytes 368648 | tf_op jit(solution)/shard_map/ppermute | solution.py:329
  14.9 2.8 %collective-permute-done.2.refs_1_.refs_3_ = bf16[32,1920]{1,0:T(8,128)(2,1)S(1)} collective-permute-done((bf16[32,1920]{1,0:T(8,128)(2,1)S(1)}, bf16[32,1920]{1,0:T(8,128)(2,1)S(1)}, u32[]{:S(2)}, u32[]{:S(2)}) %collective-permute-start.2) | collective-permute-done | bytes 122912 | tf_op jit(solution)/shard_map/ppermute | solution.py:329
  17.7 1.5 forward.10
  19.3 4.8 %collective-permute-start.8 = (bf16[32,1920]{1,0:T(8,128)(2,1)S(1)}, bf16[32,1920]{1,0:T(8,128)(2,1)S(1)}, u32[]{:S(2)}, u32[]{:S(2)}) collective-permute-start(bf16[32,1920]{1,0:T(8,128)(2,1)S(1)} %get-tuple-element.208), channel_id=1, source_target_pairs={{0,14},{1,15},{2,12},{3,13},{4,10},{5,11},{6,8},{7,9},{8,22},{9,23... | collective-permute-start | bytes 368648 | tf_op jit(solution)/shard_map/ppermute | solution.py:329
  25.6 2.1 collective-permute-done.5.refs_1_.refs_3_
  29.2 3.3 %collective-permute-start.7 = (bf16[32,1920]{1,0:T(8,128)(2,1)S(1)}, bf16[32,1920]{1,0:T(8,128)(2,1)S(1)}, u32[]{:S(2)}, u32[]{:S(2)}) collective-permute-start(bf16[32,1920]{1,0:T(8,128)(2,1)S(1)} %get-tuple-element.207), channel_id=1, source_target_pairs={{0,12},{1,13},{2,14},{3,15},{4,8},{5,9},{6,10},{7,11},{8,20},{9,21... | collective-permute-start | bytes 368648 | tf_op jit(solution)/shard_map/ppermute | solution.py:329
  33.1 4.2 %collective-permute-done.6.refs_1_ = bf16[32,1920]{1,0:T(8,128)(2,1)S(1)} collective-permute-done((bf16[32,1920]{1,0:T(8,128)(2,1)S(1)}, bf16[32,1920]{1,0:T(8,128)(2,1)S(1)}, u32[]{:S(2)}, u32[]{:S(2)}) %collective-permute-start.6) | collective-permute-done | bytes 122912 | tf_op jit(solution)/shard_map/ppermute | solution.py:329
  39.6 1.9 collective-permute-start.13
  42.1 1.9 collective-permute-start.16
  44.1 3.7 %collective-permute-done.13.refs_1_.refs_3_ = bf16[32,1920]{1,0:T(8,128)(2,1)S(1)} collective-permute-done((bf16[32,1920]{1,0:T(8,128)(2,1)S(1)}, bf16[32,1920]{1,0:T(8,128)(2,1)S(1)}, u32[]{:S(2)}, u32[]{:S(2)}) %collective-permute-start.13) | collective-permute-done | bytes 122912 | tf_op jit(solution)/shard_map/ppermute | solution.py:329
  50.7 2.0 collective-permute-start.14
  52.7 5.0 %collective-permute-done.16.refs_1_.refs_3_ = bf16[32,1920]{1,0:T(8,128)(2,1)S(1)} collective-permute-done((bf16[32,1920]{1,0:T(8,128)(2,1)S(1)}, bf16[32,1920]{1,0:T(8,128)(2,1)S(1)}, u32[]{:S(2)}, u32[]{:S(2)}) %collective-permute-start.16) | collective-permute-done | bytes 122912 | tf_op jit(solution)/shard_map/ppermute | solution.py:329
  59.2 2.2 collective-permute-start.18
  62.0 4.8 %collective-permute-done.17.refs_1_ = bf16[32,1920]{1,0:T(8,128)(2,1)S(1)} collective-permute-done((bf16[32,1920]{1,0:T(8,128)(2,1)S(1)}, bf16[32,1920]{1,0:T(8,128)(2,1)S(1)}, u32[]{:S(2)}, u32[]{:S(2)}) %collective-permute-start.17) | collective-permute-done | bytes 122912 | tf_op jit(solution)/shard_map/ppermute | solution.py:329
  66.7 2.6 %collective-permute-done.18.refs_2_ = bf16[32,1920]{1,0:T(8,128)(2,1)S(1)} collective-permute-done((bf16[32,1920]{1,0:T(8,128)(2,1)S(1)}, bf16[32,1920]{1,0:T(8,128)(2,1)S(1)}, u32[]{:S(2)}, u32[]{:S(2)}) %collective-permute-start.18) | collective-permute-done | bytes 122912 | tf_op jit(solution)/shard_map/ppermute | solution.py:329
  72.8 3.1 %collective-permute-start.27 = (bf16[32,1920]{1,0:T(8,128)(2,1)S(1)}, bf16[32,1920]{1,0:T(8,128)(2,1)S(1)}, u32[]{:S(2)}, u32[]{:S(2)}) collective-permute-start(bf16[32,1920]{1,0:T(8,128)(2,1)S(1)} %get-tuple-element.222), channel_id=1, source_target_pairs={{0,4},{1,5},{2,6},{3,7},{4,0},{5,1},{6,2},{7,3},{8,12},{9,13},{10,... | collective-permute-start | bytes 368648 | tf_op jit(solution)/shard_map/ppermute | solution.py:329
  76.0 3.7 %collective-permute-done.24.refs_1_ = bf16[32,1920]{1,0:T(8,128)(2,1)S(1)} collective-permute-done((bf16[32,1920]{1,0:T(8,128)(2,1)S(1)}, bf16[32,1920]{1,0:T(8,128)(2,1)S(1)}, u32[]{:S(2)}, u32[]{:S(2)}) %collective-permute-start.24) | collective-permute-done | bytes 122912 | tf_op jit(solution)/shard_map/ppermute | solution.py:329
  81.1 1.8 collective-permute-start.30
  83.0 1.6 collective-permute-start.25
  84.6 1.5 forward.15
  86.2 4.4 %collective-permute-start.29 = (bf16[32,1920]{1,0:T(8,128)(2,1)S(1)}, bf16[32,1920]{1,0:T(8,128)(2,1)S(1)}, u32[]{:S(2)}, u32[]{:S(2)}) collective-permute-start(bf16[32,1920]{1,0:T(8,128)(2,1)S(1)} %get-tuple-element.224), channel_id=1, source_target_pairs={{0,12},{1,13},{2,14},{3,15},{4,8},{5,9},{6,10},{7,11},{8,20},{9,21... | collective-permute-start | bytes 368648 | tf_op jit(solution)/shard_map/ppermute | solution.py:329
  90.6 3.9 %collective-permute-done.25.refs_0_ = bf16[32,1920]{1,0:T(8,128)(2,1)S(1)} collective-permute-done((bf16[32,1920]{1,0:T(8,128)(2,1)S(1)}, bf16[32,1920]{1,0:T(8,128)(2,1)S(1)}, u32[]{:S(2)}, u32[]{:S(2)}) %collective-permute-start.25) | collective-permute-done | bytes 122912 | tf_op jit(solution)/shard_map/ppermute | solution.py:329
  98.6 1.8 collective-permute-start.35
  100.4 2.7 %collective-permute-start.38 = (bf16[32,1920]{1,0:T(8,128)(2,1)S(1)}, bf16[32,1920]{1,0:T(8,128)(2,1)S(1)}, u32[]{:S(2)}, u32[]{:S(2)}) collective-permute-start(bf16[32,1920]{1,0:T(8,128)(2,1)S(1)} %get-tuple-element.237), channel_id=1, source_target_pairs={{0,4},{1,5},{2,6},{3,7},{4,0},{5,1},{6,2},{7,3},{8,12},{9,13},{10,... | collective-permute-start | bytes 368648 | tf_op jit(solution)/shard_map/ppermute | solution.py:329
  103.1 2.9 %turn.1 = (bf16[1024,2048]{1,0:T(8,128)(2,1)S(1)}, bf16[2048,512]{1,0:T(8,128)(2,1)S(1)}) custom-call(bf16[2048,1024]{1,0:T(8,128)(2,1)S(1)} %get-tuple-element.196.in_ref, bf16[512,2048]{1,0:T(8,128)(2,1)S(1)} %get-tuple-element.197.out_ref), custom_call_target="tpu_custom_call" | custom-call | tf_op jit(solution)/shard_map/turn/pallas_call | solution.py:470
  106.7 1.5 forward.16
  108.2 2.2 backward.10
  110.4 1.5 collective-permute-start.41
  112.0 1.7 collective-permute-start.36
  115.2 2.2 backward.11
  118.1 3.0 %collective-permute-start.40 = (bf16[32,1920]{1,0:T(8,128)(2,1)S(1)}, bf16[32,1920]{1,0:T(8,128)(2,1)S(1)}, u32[]{:S(2)}, u32[]{:S(2)}) collective-permute-start(bf16[32,1920]{1,0:T(8,128)(2,1)S(1)} %get-tuple-element.246), channel_id=1, source_target_pairs={{0,12},{1,13},{2,14},{3,15},{4,8},{5,9},{6,10},{7,11},{8,4},{9,5},... | collective-permute-start | bytes 368648 | tf_op jit(solution)/shard_map/ppermute | solution.py:329
  121.6 1.9 collective-permute-done.39.refs_1_
  123.5 2.6 %collective-permute-done.40.refs_2_ = bf16[32,1920]{1,0:T(8,128)(2,1)S(1)} collective-permute-done((bf16[32,1920]{1,0:T(8,128)(2,1)S(1)}, bf16[32,1920]{1,0:T(8,128)(2,1)S(1)}, u32[]{:S(2)}, u32[]{:S(2)}) %collective-permute-start.40) | collective-permute-done | bytes 122912 | tf_op jit(solution)/shard_map/ppermute | solution.py:329
  130.1 2.6 %collective-permute-start.49 = (bf16[32,1920]{1,0:T(8,128)(2,1)S(1)}, bf16[32,1920]{1,0:T(8,128)(2,1)S(1)}, u32[]{:S(2)}, u32[]{:S(2)}) collective-permute-start(bf16[32,1920]{1,0:T(8,128)(2,1)S(1)} %get-tuple-element.262), channel_id=1, source_target_pairs={{0,4},{1,5},{2,6},{3,7},{4,0},{5,1},{6,2},{7,3},{8,12},{9,13},{10,... | collective-permute-start | bytes 368648 | tf_op jit(solution)/shard_map/ppermute | solution.py:329
  132.7 3.7 %collective-permute-done.46.refs_1_ = bf16[32,1920]{1,0:T(8,128)(2,1)S(1)} collective-permute-done((bf16[32,1920]{1,0:T(8,128)(2,1)S(1)}, bf16[32,1920]{1,0:T(8,128)(2,1)S(1)}, u32[]{:S(2)}, u32[]{:S(2)}) %collective-permute-start.46) | collective-permute-done | bytes 122912 | tf_op jit(solution)/shard_map/ppermute | solution.py:329
  137.8 2.2 backward.12
  140.0 4.1 %collective-permute-start.52 = (bf16[32,1920]{1,0:T(8,128)(2,1)S(1)}, bf16[32,1920]{1,0:T(8,128)(2,1)S(1)}, u32[]{:S(2)}, u32[]{:S(2)}) collective-permute-start(bf16[32,1920]{1,0:T(8,128)(2,1)S(1)} %get-tuple-element.275), channel_id=1, source_target_pairs={{0,30},{1,31},{2,28},{3,29},{4,26},{5,27},{6,24},{7,25},{8,6},{9,7... | collective-permute-start | bytes 368648 | tf_op jit(solution)/shard_map/ppermute | solution.py:329
  145.6 2.2 backward.13
  149.1 2.9 %collective-permute-start.51 = (bf16[32,1920]{1,0:T(8,128)(2,1)S(1)}, bf16[32,1920]{1,0:T(8,128)(2,1)S(1)}, u32[]{:S(2)}, u32[]{:S(2)}) collective-permute-start(bf16[32,1920]{1,0:T(8,128)(2,1)S(1)} %get-tuple-element.274), channel_id=1, source_target_pairs={{0,28},{1,29},{2,30},{3,31},{4,24},{5,25},{6,26},{7,27},{8,4},{9,5... | collective-permute-start | bytes 368648 | tf_op jit(solution)/shard_map/ppermute | solution.py:329
  152.1 2.3 collective-permute-done.50.refs_1_
  154.4 2.5 %collective-permute-done.51.refs_2_ = bf16[32,1920]{1,0:T(8,128)(2,1)S(1)} collective-permute-done((bf16[32,1920]{1,0:T(8,128)(2,1)S(1)}, bf16[32,1920]{1,0:T(8,128)(2,1)S(1)}, u32[]{:S(2)}, u32[]{:S(2)}) %collective-permute-start.51) | collective-permute-done | bytes 122912 | tf_op jit(solution)/shard_map/ppermute | solution.py:329
  156.9 2.0 collective-permute-done.47.refs_0_
  162.1 3.5 %collective-permute-start.60 = (bf16[32,1920]{1,0:T(8,128)(2,1)S(1)}, bf16[32,1920]{1,0:T(8,128)(2,1)S(1)}, u32[]{:S(2)}, u32[]{:S(2)}) collective-permute-start(bf16[32,1920]{1,0:T(8,128)(2,1)S(1)} %get-tuple-element.285), channel_id=1, source_target_pairs={{0,4},{1,5},{2,6},{3,7},{4,0},{5,1},{6,2},{7,3},{8,12},{9,13},{10,... | collective-permute-start | bytes 368648 | tf_op jit(solution)/shard_map/ppermute | solution.py:329
  165.6 3.7 %collective-permute-done.57.refs_1_ = bf16[32,1920]{1,0:T(8,128)(2,1)S(1)} collective-permute-done((bf16[32,1920]{1,0:T(8,128)(2,1)S(1)}, bf16[32,1920]{1,0:T(8,128)(2,1)S(1)}, u32[]{:S(2)}, u32[]{:S(2)}) %collective-permute-start.57) | collective-permute-done | bytes 122912 | tf_op jit(solution)/shard_map/ppermute | solution.py:329
  169.3 2.2 backward.14
  171.4 2.3 collective-permute-start.63
  173.7 2.2 collective-permute-start.58
  176.0 2.2 backward.15
  179.3 2.1 collective-permute-start.62
  181.9 3.7 %collective-permute-done.61.refs_1_ = bf16[32,1920]{1,0:T(8,128)(2,1)S(1)} collective-permute-done((bf16[32,1920]{1,0:T(8,128)(2,1)S(1)}, bf16[32,1920]{1,0:T(8,128)(2,1)S(1)}, u32[]{:S(2)}, u32[]{:S(2)}) %collective-permute-start.61) | collective-permute-done | bytes 122912 | tf_op jit(solution)/shard_map/ppermute | solution.py:329
  185.6 1.7 collective-permute-done.62.refs_2_
  189.5 1.5 collective-permute-start.68
  192.2 1.7 collective-permute-start.71
  193.9 3.6 %collective-permute-done.68.refs_1_ = bf16[32,1920]{1,0:T(8,128)(2,1)S(1)} collective-permute-done((bf16[32,1920]{1,0:T(8,128)(2,1)S(1)}, bf16[32,1920]{1,0:T(8,128)(2,1)S(1)}, u32[]{:S(2)}, u32[]{:S(2)}) %collective-permute-start.68) | collective-permute-done | bytes 122912 | tf_op jit(solution)/shard_map/ppermute | solution.py:329
  197.5 2.2 backward.16
  199.7 4.2 %collective-permute-start.74 = (bf16[32,1920]{1,0:T(8,128)(2,1)S(1)}, bf16[32,1920]{1,0:T(8,128)(2,1)S(1)}, u32[]{:S(2)}, u32[]{:S(2)}) collective-permute-start(bf16[32,1920]{1,0:T(8,128)(2,1)S(1)} %get-tuple-element.345), channel_id=1, source_target_pairs={{0,30},{1,31},{2,28},{3,29},{4,26},{5,27},{6,24},{7,25},{8,6},{9,7... | collective-permute-start | bytes 368648 | tf_op jit(solution)/shard_map/ppermute | solution.py:329
  205.3 2.2 backward.17
  207.5 2.4 %collective-permute-start.73 = (bf16[32,1920]{1,0:T(8,128)(2,1)S(1)}, bf16[32,1920]{1,0:T(8,128)(2,1)S(1)}, u32[]{:S(2)}, u32[]{:S(2)}) collective-permute-start(bf16[32,1920]{1,0:T(8,128)(2,1)S(1)} %get-tuple-element.344), channel_id=1, source_target_pairs={{0,28},{1,29},{2,30},{3,31},{4,24},{5,25},{6,26},{7,27},{8,4},{9,5... | collective-permute-start | bytes 368648 | tf_op jit(solution)/shard_map/ppermute | solution.py:329
  210.5 4.7 %collective-permute-done.72.refs_1_ = bf16[32,1920]{1,0:T(8,128)(2,1)S(1)} collective-permute-done((bf16[32,1920]{1,0:T(8,128)(2,1)S(1)}, bf16[32,1920]{1,0:T(8,128)(2,1)S(1)}, u32[]{:S(2)}, u32[]{:S(2)}) %collective-permute-start.72) | collective-permute-done | bytes 122912 | tf_op jit(solution)/shard_map/ppermute | solution.py:329
  220.3 3.0 %collective-permute-start.81 = (bf16[32,1920]{1,0:T(8,128)(2,1)S(1)}, bf16[32,1920]{1,0:T(8,128)(2,1)S(1)}, u32[]{:S(2)}, u32[]{:S(2)}) collective-permute-start(bf16[32,1920]{1,0:T(8,128)(2,1)S(1)} %get-tuple-element.385), channel_id=1, source_target_pairs={{0,4},{1,5},{2,6},{3,7},{4,0},{5,1},{6,2},{7,3},{8,12},{9,13},{10,... | collective-permute-start | bytes 368648 | tf_op jit(solution)/shard_map/ppermute | solution.py:329
  232.8 4.7 %grads.1 = (bf16[2048,1024]{1,0:T(8,128)(2,1)}, bf16[512,2048]{1,0:T(8,128)(2,1)}) custom-call(s32[3]{0:T(128)S(1)} %get-tuple-element.398.place_ref, bf16[3,64,2048]{2,1,0:T(8,128)(2,1)S(1)} %get-tuple-element.331.refs_0_, bf16[3,64,1024]{2,1,0:T(8,128)(2,1)S(1)} %get-tuple-element.332.refs_1_, bf16[3,64,512]{2,1,0:T(8,128)(2,1)S(1)} %get-tuple-element.333.refs_2_, ...), custom_call_target="tpu_custom_call" | custom-call | tf_op jit(solution)/shard_map/grads/pallas_call | solution.py:584
  (151 shorter events, 60.9 us)
Async XLA Ops:
  1.8 5.0 %collective-permute-start.1 = (bf16[2,80,2048]{2,1,0:T(8,128)(2,1)S(1)}, bf16[2,80,2048]{2,1,0:T(8,128)(2,1)S(1)}, u32[]{:S(2)}, u32[]{:S(2)}) collective-permute-start(bf16[2,80,2048]{2,1,0:T(8,128)(2,1)S(1)} %broadcast_select_fusion.refs_2_), channel_id=1, source_target_pairs={{0,1},{1,0},{2,3},{3,2},{4,5},{5,4},{6,7},{7,6},{8,9},{9,8},{10,11... | collective-permute-start | bytes 1966088 | tf_op jit(solution)/shard_map/ppermute | solution.py:329
  8.4 9.3 %collective-permute-start.2 = (bf16[32,1920]{1,0:T(8,128)(2,1)S(1)}, bf16[32,1920]{1,0:T(8,128)(2,1)S(1)}, u32[]{:S(2)}, u32[]{:S(2)}) collective-permute-start(bf16[32,1920]{1,0:T(8,128)(2,1)S(1)} %get-tuple-element.202), channel_id=1, source_target_pairs={{0,6},{1,7},{2,4},{3,5},{4,2},{5,3},{6,0},{7,1},{8,14},{9,15},{10,... | collective-permute-start | bytes 368648 | tf_op jit(solution)/shard_map/ppermute | solution.py:329
  13.5 12.0 %collective-permute-start.4 = (bf16[32,1920]{1,0:T(8,128)(2,1)S(1)}, bf16[32,1920]{1,0:T(8,128)(2,1)S(1)}, u32[]{:S(2)}, u32[]{:S(2)}) collective-permute-start(bf16[32,1920]{1,0:T(8,128)(2,1)S(1)} %get-tuple-element.204), channel_id=1, source_target_pairs={{0,2},{1,3},{2,0},{3,1},{4,6},{5,7},{6,4},{7,5},{8,10},{9,11},{10,... | collective-permute-start | bytes 368648 | tf_op jit(solution)/shard_map/ppermute | solution.py:329
  13.5 14.1 %collective-permute-start.5 = (bf16[32,1920]{1,0:T(8,128)(2,1)S(1)}, bf16[32,1920]{1,0:T(8,128)(2,1)S(1)}, u32[]{:S(2)}, u32[]{:S(2)}) collective-permute-start(bf16[32,1920]{1,0:T(8,128)(2,1)S(1)} %get-tuple-element.205), channel_id=1, source_target_pairs={{0,4},{1,5},{2,6},{3,7},{4,0},{5,1},{6,2},{7,3},{8,12},{9,13},{10,... | collective-permute-start | bytes 368648 | tf_op jit(solution)/shard_map/ppermute | solution.py:329
  19.3 13.3 %collective-permute-start.8 = (bf16[32,1920]{1,0:T(8,128)(2,1)S(1)}, bf16[32,1920]{1,0:T(8,128)(2,1)S(1)}, u32[]{:S(2)}, u32[]{:S(2)}) collective-permute-start(bf16[32,1920]{1,0:T(8,128)(2,1)S(1)} %get-tuple-element.208), channel_id=1, source_target_pairs={{0,14},{1,15},{2,12},{3,13},{4,10},{5,11},{6,8},{7,9},{8,22},{9,23... | collective-permute-start | bytes 368648 | tf_op jit(solution)/shard_map/ppermute | solution.py:329
  24.1 8.5 %collective-permute-start.3 = (bf16[32,1920]{1,0:T(8,128)(2,1)S(1)}, bf16[32,1920]{1,0:T(8,128)(2,1)S(1)}, u32[]{:S(2)}, u32[]{:S(2)}) collective-permute-start(bf16[32,1920]{1,0:T(8,128)(2,1)S(1)} %get-tuple-element.203.refs_2_), channel_id=1, source_target_pairs={{0,8},{1,9},{2,10},{3,11},{4,12},{5,13},{6,14},{7,15},{8,16},{9,17... | collective-permute-start | bytes 368648 | tf_op jit(solution)/shard_map/ppermute | solution.py:329
  29.2 8.0 %collective-permute-start.6 = (bf16[32,1920]{1,0:T(8,128)(2,1)S(1)}, bf16[32,1920]{1,0:T(8,128)(2,1)S(1)}, u32[]{:S(2)}, u32[]{:S(2)}) collective-permute-start(bf16[32,1920]{1,0:T(8,128)(2,1)S(1)} %get-tuple-element.206), channel_id=1, source_target_pairs={{0,10},{1,11},{2,8},{3,9},{4,14},{5,15},{6,12},{7,13},{8,18},{9,19... | collective-permute-start | bytes 368648 | tf_op jit(solution)/shard_map/ppermute | solution.py:329
  29.2 8.0 %collective-permute-start.7 = (bf16[32,1920]{1,0:T(8,128)(2,1)S(1)}, bf16[32,1920]{1,0:T(8,128)(2,1)S(1)}, u32[]{:S(2)}, u32[]{:S(2)}) collective-permute-start(bf16[32,1920]{1,0:T(8,128)(2,1)S(1)} %get-tuple-element.207), channel_id=1, source_target_pairs={{0,12},{1,13},{2,14},{3,15},{4,8},{5,9},{6,10},{7,11},{8,20},{9,21... | collective-permute-start | bytes 368648 | tf_op jit(solution)/shard_map/ppermute | solution.py:329
  32.5 5.2 %collective-permute-start.12 = (bf16[32,1920]{1,0:T(8,128)(2,1)S(1)}, bf16[32,1920]{1,0:T(8,128)(2,1)S(1)}, u32[]{:S(2)}, u32[]{:S(2)}) collective-permute-start(bf16[32,1920]{1,0:T(8,128)(2,1)S(1)} %collective-permute-done.8.refs_3_), channel_id=1, source_target_pairs={{0,1},{1,0},{2,3},{3,2},{4,5},{5,4},{6,7},{7,6},{8,9},{9,8},{10,11... | collective-permute-start | bytes 368648 | tf_op jit(solution)/shard_map/ppermute | solution.py:329
  32.5 5.2 %collective-permute-start.9 = (bf16[32,1920]{1,0:T(8,128)(2,1)S(1)}, bf16[32,1920]{1,0:T(8,128)(2,1)S(1)}, u32[]{:S(2)}, u32[]{:S(2)}) collective-permute-start(bf16[32,1920]{1,0:T(8,128)(2,1)S(1)} %collective-permute-done.3.refs_0_), channel_id=1, source_target_pairs={{0,1},{1,0},{2,3},{3,2},{4,5},{5,4},{6,7},{7,6},{8,9},{9,8},{10,11... | collective-permute-start | bytes 368648 | tf_op jit(solution)/shard_map/ppermute | solution.py:329
  39.6 8.1 %collective-permute-start.13 = (bf16[32,1920]{1,0:T(8,128)(2,1)S(1)}, bf16[32,1920]{1,0:T(8,128)(2,1)S(1)}, u32[]{:S(2)}, u32[]{:S(2)}) collective-permute-start(bf16[32,1920]{1,0:T(8,128)(2,1)S(1)} %get-tuple-element.211), channel_id=1, source_target_pairs={{0,6},{1,7},{2,4},{3,5},{4,2},{5,3},{6,0},{7,1},{8,14},{9,15},{10,... | collective-permute-start | bytes 368648 | tf_op jit(solution)/shard_map/ppermute | solution.py:329
  41.5 11.2 %collective-permute-start.15 = (bf16[32,1920]{1,0:T(8,128)(2,1)S(1)}, bf16[32,1920]{1,0:T(8,128)(2,1)S(1)}, u32[]{:S(2)}, u32[]{:S(2)}) collective-permute-start(bf16[32,1920]{1,0:T(8,128)(2,1)S(1)} %get-tuple-element.213), channel_id=1, source_target_pairs={{0,2},{1,3},{2,0},{3,1},{4,6},{5,7},{6,4},{7,5},{8,10},{9,11},{10,... | collective-permute-start | bytes 368648 | tf_op jit(solution)/shard_map/ppermute | solution.py:329
  42.1 15.6 %collective-permute-start.16 = (bf16[32,1920]{1,0:T(8,128)(2,1)S(1)}, bf16[32,1920]{1,0:T(8,128)(2,1)S(1)}, u32[]{:S(2)}, u32[]{:S(2)}) collective-permute-start(bf16[32,1920]{1,0:T(8,128)(2,1)S(1)} %get-tuple-element.214), channel_id=1, source_target_pairs={{0,4},{1,5},{2,6},{3,7},{4,0},{5,1},{6,2},{7,3},{8,12},{9,13},{10,... | collective-permute-start | bytes 368648 | tf_op jit(solution)/shard_map/ppermute | solution.py:329
  49.2 12.2 %collective-permute-start.19 = (bf16[32,1920]{1,0:T(8,128)(2,1)S(1)}, bf16[32,1920]{1,0:T(8,128)(2,1)S(1)}, u32[]{:S(2)}, u32[]{:S(2)}) collective-permute-start(bf16[32,1920]{1,0:T(8,128)(2,1)S(1)} %get-tuple-element.217), channel_id=1, source_target_pairs={{0,14},{1,15},{2,12},{3,13},{4,10},{5,11},{6,8},{7,9},{8,22},{9,23... | collective-permute-start | bytes 368648 | tf_op jit(solution)/shard_map/ppermute | solution.py:329
  50.7 10.8 %collective-permute-start.14 = (bf16[32,1920]{1,0:T(8,128)(2,1)S(1)}, bf16[32,1920]{1,0:T(8,128)(2,1)S(1)}, u32[]{:S(2)}, u32[]{:S(2)}) collective-permute-start(bf16[32,1920]{1,0:T(8,128)(2,1)S(1)} %get-tuple-element.212.refs_2_), channel_id=1, source_target_pairs={{0,8},{1,9},{2,10},{3,11},{4,12},{5,13},{6,14},{7,15},{8,16},{9,17... | collective-permute-start | bytes 368648 | tf_op jit(solution)/shard_map/ppermute | solution.py:329
  59.2 7.6 %collective-permute-start.17 = (bf16[32,1920]{1,0:T(8,128)(2,1)S(1)}, bf16[32,1920]{1,0:T(8,128)(2,1)S(1)}, u32[]{:S(2)}, u32[]{:S(2)}) collective-permute-start(bf16[32,1920]{1,0:T(8,128)(2,1)S(1)} %get-tuple-element.215), channel_id=1, source_target_pairs={{0,10},{1,11},{2,8},{3,9},{4,14},{5,15},{6,12},{7,13},{8,18},{9,19... | collective-permute-start | bytes 368648 | tf_op jit(solution)/shard_map/ppermute | solution.py:329
  59.2 10.1 %collective-permute-start.18 = (bf16[32,1920]{1,0:T(8,128)(2,1)S(1)}, bf16[32,1920]{1,0:T(8,128)(2,1)S(1)}, u32[]{:S(2)}, u32[]{:S(2)}) collective-permute-start(bf16[32,1920]{1,0:T(8,128)(2,1)S(1)} %get-tuple-element.216), channel_id=1, source_target_pairs={{0,12},{1,13},{2,14},{3,15},{4,8},{5,9},{6,10},{7,11},{8,20},{9,21... | collective-permute-start | bytes 368648 | tf_op jit(solution)/shard_map/ppermute | solution.py:329
  61.5 7.8 %collective-permute-start.23 = (bf16[32,1920]{1,0:T(8,128)(2,1)S(1)}, bf16[32,1920]{1,0:T(8,128)(2,1)S(1)}, u32[]{:S(2)}, u32[]{:S(2)}) collective-permute-start(bf16[32,1920]{1,0:T(8,128)(2,1)S(1)} %collective-permute-done.19.refs_3_), channel_id=1, source_target_pairs={{0,1},{1,0},{2,3},{3,2},{4,5},{5,4},{6,7},{7,6},{8,9},{9,8},{10,11... | collective-permute-start | bytes 368648 | tf_op jit(solution)/shard_map/ppermute | solution.py:329
  61.5 7.8 %collective-permute-start.20 = (bf16[32,1920]{1,0:T(8,128)(2,1)S(1)}, bf16[32,1920]{1,0:T(8,128)(2,1)S(1)}, u32[]{:S(2)}, u32[]{:S(2)}) collective-permute-start(bf16[32,1920]{1,0:T(8,128)(2,1)S(1)} %collective-permute-done.14.refs_0_), channel_id=1, source_target_pairs={{0,1},{1,0},{2,3},{3,2},{4,5},{5,4},{6,7},{7,6},{8,9},{9,8},{10,11... | collective-permute-start | bytes 368648 | tf_op jit(solution)/shard_map/ppermute | solution.py:329
  71.5 8.1 %collective-permute-start.24 = (bf16[32,1920]{1,0:T(8,128)(2,1)S(1)}, bf16[32,1920]{1,0:T(8,128)(2,1)S(1)}, u32[]{:S(2)}, u32[]{:S(2)}) collective-permute-start(bf16[32,1920]{1,0:T(8,128)(2,1)S(1)} %get-tuple-element.219), channel_id=1, source_target_pairs={{0,6},{1,7},{2,4},{3,5},{4,2},{5,3},{6,0},{7,1},{8,14},{9,15},{10,... | collective-permute-start | bytes 368648 | tf_op jit(solution)/shard_map/ppermute | solution.py:329
  72.8 11.8 %collective-permute-start.26 = (bf16[32,1920]{1,0:T(8,128)(2,1)S(1)}, bf16[32,1920]{1,0:T(8,128)(2,1)S(1)}, u32[]{:S(2)}, u32[]{:S(2)}) collective-permute-start(bf16[32,1920]{1,0:T(8,128)(2,1)S(1)} %get-tuple-element.221), channel_id=1, source_target_pairs={{0,2},{1,3},{2,0},{3,1},{4,6},{5,7},{6,4},{7,5},{8,10},{9,11},{10,... | collective-permute-start | bytes 368648 | tf_op jit(solution)/shard_map/ppermute | solution.py:329
  72.8 11.8 %collective-permute-start.27 = (bf16[32,1920]{1,0:T(8,128)(2,1)S(1)}, bf16[32,1920]{1,0:T(8,128)(2,1)S(1)}, u32[]{:S(2)}, u32[]{:S(2)}) collective-permute-start(bf16[32,1920]{1,0:T(8,128)(2,1)S(1)} %get-tuple-element.222), channel_id=1, source_target_pairs={{0,4},{1,5},{2,6},{3,7},{4,0},{5,1},{6,2},{7,3},{8,12},{9,13},{10,... | collective-permute-start | bytes 368648 | tf_op jit(solution)/shard_map/ppermute | solution.py:329
  81.1 9.5 %collective-permute-start.30 = (bf16[32,1920]{1,0:T(8,128)(2,1)S(1)}, bf16[32,1920]{1,0:T(8,128)(2,1)S(1)}, u32[]{:S(2)}, u32[]{:S(2)}) collective-permute-start(bf16[32,1920]{1,0:T(8,128)(2,1)S(1)} %get-tuple-element.225), channel_id=1, source_target_pairs={{0,14},{1,15},{2,12},{3,13},{4,10},{5,11},{6,8},{7,9},{8,22},{9,23... | collective-permute-start | bytes 368648 | tf_op jit(solution)/shard_map/ppermute | solution.py:329
  83.0 11.6 %collective-permute-start.25 = (bf16[32,1920]{1,0:T(8,128)(2,1)S(1)}, bf16[32,1920]{1,0:T(8,128)(2,1)S(1)}, u32[]{:S(2)}, u32[]{:S(2)}) collective-permute-start(bf16[32,1920]{1,0:T(8,128)(2,1)S(1)} %get-tuple-element.220.refs_2_), channel_id=1, source_target_pairs={{0,8},{1,9},{2,10},{3,11},{4,12},{5,13},{6,14},{7,15},{8,16},{9,17... | collective-permute-start | bytes 368648 | tf_op jit(solution)/shard_map/ppermute | solution.py:329
  86.1 8.5 %collective-permute-start.28 = (bf16[32,1920]{1,0:T(8,128)(2,1)S(1)}, bf16[32,1920]{1,0:T(8,128)(2,1)S(1)}, u32[]{:S(2)}, u32[]{:S(2)}) collective-permute-start(bf16[32,1920]{1,0:T(8,128)(2,1)S(1)} %get-tuple-element.223), channel_id=1, source_target_pairs={{0,10},{1,11},{2,8},{3,9},{4,14},{5,15},{6,12},{7,13},{8,18},{9,19... | collective-permute-start | bytes 368648 | tf_op jit(solution)/shard_map/ppermute | solution.py:329
  86.2 10.2 %collective-permute-start.29 = (bf16[32,1920]{1,0:T(8,128)(2,1)S(1)}, bf16[32,1920]{1,0:T(8,128)(2,1)S(1)}, u32[]{:S(2)}, u32[]{:S(2)}) collective-permute-start(bf16[32,1920]{1,0:T(8,128)(2,1)S(1)} %get-tuple-element.224), channel_id=1, source_target_pairs={{0,12},{1,13},{2,14},{3,15},{4,8},{5,9},{6,10},{7,11},{8,20},{9,21... | collective-permute-start | bytes 368648 | tf_op jit(solution)/shard_map/ppermute | solution.py:329
  90.6 5.8 %collective-permute-start.34 = (bf16[32,1920]{1,0:T(8,128)(2,1)S(1)}, bf16[32,1920]{1,0:T(8,128)(2,1)S(1)}, u32[]{:S(2)}, u32[]{:S(2)}) collective-permute-start(bf16[32,1920]{1,0:T(8,128)(2,1)S(1)} %collective-permute-done.30.refs_3_), channel_id=1, source_target_pairs={{0,1},{1,0},{2,3},{3,2},{4,5},{5,4},{6,7},{7,6},{8,9},{9,8},{10,11... | collective-permute-start | bytes 368648 | tf_op jit(solution)/shard_map/ppermute | solution.py:329
  98.6 8.1 %collective-permute-start.35 = (bf16[32,1920]{1,0:T(8,128)(2,1)S(1)}, bf16[32,1920]{1,0:T(8,128)(2,1)S(1)}, u32[]{:S(2)}, u32[]{:S(2)}) collective-permute-start(bf16[32,1920]{1,0:T(8,128)(2,1)S(1)} %get-tuple-element.227), channel_id=1, source_target_pairs={{0,6},{1,7},{2,4},{3,5},{4,2},{5,3},{6,0},{7,1},{8,14},{9,15},{10,... | collective-permute-start | bytes 368648 | tf_op jit(solution)/shard_map/ppermute | solution.py:329
  100.4 13.3 %collective-permute-start.37 = (bf16[32,1920]{1,0:T(8,128)(2,1)S(1)}, bf16[32,1920]{1,0:T(8,128)(2,1)S(1)}, u32[]{:S(2)}, u32[]{:S(2)}) collective-permute-start(bf16[32,1920]{1,0:T(8,128)(2,1)S(1)} %get-tuple-element.236), channel_id=1, source_target_pairs={{0,2},{1,3},{2,0},{3,1},{4,6},{5,7},{6,4},{7,5},{8,10},{9,11},{10,... | collective-permute-start | bytes 368648 | tf_op jit(solution)/shard_map/ppermute | solution.py:329
  100.4 13.3 %collective-permute-start.38 = (bf16[32,1920]{1,0:T(8,128)(2,1)S(1)}, bf16[32,1920]{1,0:T(8,128)(2,1)S(1)}, u32[]{:S(2)}, u32[]{:S(2)}) collective-permute-start(bf16[32,1920]{1,0:T(8,128)(2,1)S(1)} %get-tuple-element.237), channel_id=1, source_target_pairs={{0,4},{1,5},{2,6},{3,7},{4,0},{5,1},{6,2},{7,3},{8,12},{9,13},{10,... | collective-permute-start | bytes 368648 | tf_op jit(solution)/shard_map/ppermute | solution.py:329
  110.4 10.6 %collective-permute-start.41 = (bf16[32,1920]{1,0:T(8,128)(2,1)S(1)}, bf16[32,1920]{1,0:T(8,128)(2,1)S(1)}, u32[]{:S(2)}, u32[]{:S(2)}) collective-permute-start(bf16[32,1920]{1,0:T(8,128)(2,1)S(1)} %get-tuple-element.247), channel_id=1, source_target_pairs={{0,14},{1,15},{2,12},{3,13},{4,10},{5,11},{6,8},{7,9},{8,6},{9,7},... | collective-permute-start | bytes 368648 | tf_op jit(solution)/shard_map/ppermute | solution.py:329
  112.0 9.6 %collective-permute-start.36 = (bf16[32,1920]{1,0:T(8,128)(2,1)S(1)}, bf16[32,1920]{1,0:T(8,128)(2,1)S(1)}, u32[]{:S(2)}, u32[]{:S(2)}) collective-permute-start(bf16[32,1920]{1,0:T(8,128)(2,1)S(1)} %get-tuple-element.235.refs_2_.refs_11_), channel_id=1, source_target_pairs={{0,8},{1,9},{2,10},{3,11},{4,12},{5,13},{6,14},{7,15},{8,0},{9,1},... | collective-permute-start | bytes 368648 | tf_op jit(solution)/shard_map/ppermute | solution.py:329
  117.4 6.1 %collective-permute-start.39 = (bf16[32,1920]{1,0:T(8,128)(2,1)S(1)}, bf16[32,1920]{1,0:T(8,128)(2,1)S(1)}, u32[]{:S(2)}, u32[]{:S(2)}) collective-permute-start(bf16[32,1920]{1,0:T(8,128)(2,1)S(1)} %get-tuple-element.245), channel_id=1, source_target_pairs={{0,10},{1,11},{2,8},{3,9},{4,14},{5,15},{6,12},{7,13},{8,2},{9,3},... | collective-permute-start | bytes 368648 | tf_op jit(solution)/shard_map/ppermute | solution.py:329
  118.1 8.0 %collective-permute-start.40 = (bf16[32,1920]{1,0:T(8,128)(2,1)S(1)}, bf16[32,1920]{1,0:T(8,128)(2,1)S(1)}, u32[]{:S(2)}, u32[]{:S(2)}) collective-permute-start(bf16[32,1920]{1,0:T(8,128)(2,1)S(1)} %get-tuple-element.246), channel_id=1, source_target_pairs={{0,12},{1,13},{2,14},{3,15},{4,8},{5,9},{6,10},{7,11},{8,4},{9,5},... | collective-permute-start | bytes 368648 | tf_op jit(solution)/shard_map/ppermute | solution.py:329
  121.1 5.0 %collective-permute-start.45 = (bf16[32,1920]{1,0:T(8,128)(2,1)S(1)}, bf16[32,1920]{1,0:T(8,128)(2,1)S(1)}, u32[]{:S(2)}, u32[]{:S(2)}) collective-permute-start(bf16[32,1920]{1,0:T(8,128)(2,1)S(1)} %collective-permute-done.41.refs_3_), channel_id=1, source_target_pairs={{0,1},{1,0},{2,3},{3,2},{4,5},{5,4},{6,7},{7,6},{8,9},{9,8},{10,11... | collective-permute-start | bytes 368648 | tf_op jit(solution)/shard_map/ppermute | solution.py:329
  128.3 8.1 %collective-permute-start.46 = (bf16[32,1920]{1,0:T(8,128)(2,1)S(1)}, bf16[32,1920]{1,0:T(8,128)(2,1)S(1)}, u32[]{:S(2)}, u32[]{:S(2)}) collective-permute-start(bf16[32,1920]{1,0:T(8,128)(2,1)S(1)} %get-tuple-element.249), channel_id=1, source_target_pairs={{0,6},{1,7},{2,4},{3,5},{4,2},{5,3},{6,0},{7,1},{8,14},{9,15},{10,... | collective-permute-start | bytes 368648 | tf_op jit(solution)/shard_map/ppermute | solution.py:329
  129.1 15.0 %collective-permute-start.48 = (bf16[32,1920]{1,0:T(8,128)(2,1)S(1)}, bf16[32,1920]{1,0:T(8,128)(2,1)S(1)}, u32[]{:S(2)}, u32[]{:S(2)}) collective-permute-start(bf16[32,1920]{1,0:T(8,128)(2,1)S(1)} %get-tuple-element.261), channel_id=1, source_target_pairs={{0,2},{1,3},{2,0},{3,1},{4,6},{5,7},{6,4},{7,5},{8,10},{9,11},{10,... | collective-permute-start | bytes 368648 | tf_op jit(solution)/shard_map/ppermute | solution.py:329
  130.1 14.1 %collective-permute-start.49 = (bf16[32,1920]{1,0:T(8,128)(2,1)S(1)}, bf16[32,1920]{1,0:T(8,128)(2,1)S(1)}, u32[]{:S(2)}, u32[]{:S(2)}) collective-permute-start(bf16[32,1920]{1,0:T(8,128)(2,1)S(1)} %get-tuple-element.262), channel_id=1, source_target_pairs={{0,4},{1,5},{2,6},{3,7},{4,0},{5,1},{6,2},{7,3},{8,12},{9,13},{10,... | collective-permute-start | bytes 368648 | tf_op jit(solution)/shard_map/ppermute | solution.py:329
  140.0 12.0 %collective-permute-start.52 = (bf16[32,1920]{1,0:T(8,128)(2,1)S(1)}, bf16[32,1920]{1,0:T(8,128)(2,1)S(1)}, u32[]{:S(2)}, u32[]{:S(2)}) collective-permute-start(bf16[32,1920]{1,0:T(8,128)(2,1)S(1)} %get-tuple-element.275), channel_id=1, source_target_pairs={{0,30},{1,31},{2,28},{3,29},{4,26},{5,27},{6,24},{7,25},{8,6},{9,7... | collective-permute-start | bytes 368648 | tf_op jit(solution)/shard_map/ppermute | solution.py:329
  147.8 6.6 %collective-permute-start.50 = (bf16[32,1920]{1,0:T(8,128)(2,1)S(1)}, bf16[32,1920]{1,0:T(8,128)(2,1)S(1)}, u32[]{:S(2)}, u32[]{:S(2)}) collective-permute-start(bf16[32,1920]{1,0:T(8,128)(2,1)S(1)} %get-tuple-element.273), channel_id=1, source_target_pairs={{0,26},{1,27},{2,24},{3,25},{4,30},{5,31},{6,28},{7,29},{8,2},{9,3... | collective-permute-start | bytes 368648 | tf_op jit(solution)/shard_map/ppermute | solution.py:329
  149.1 7.8 %collective-permute-start.51 = (bf16[32,1920]{1,0:T(8,128)(2,1)S(1)}, bf16[32,1920]{1,0:T(8,128)(2,1)S(1)}, u32[]{:S(2)}, u32[]{:S(2)}) collective-permute-start(bf16[32,1920]{1,0:T(8,128)(2,1)S(1)} %get-tuple-element.274), channel_id=1, source_target_pairs={{0,28},{1,29},{2,30},{3,31},{4,24},{5,25},{6,26},{7,27},{8,4},{9,5... | collective-permute-start | bytes 368648 | tf_op jit(solution)/shard_map/ppermute | solution.py:329
  152.0 6.9 %collective-permute-start.47 = (bf16[32,1920]{1,0:T(8,128)(2,1)S(1)}, bf16[32,1920]{1,0:T(8,128)(2,1)S(1)}, u32[]{:S(2)}, u32[]{:S(2)}) collective-permute-start(bf16[32,1920]{1,0:T(8,128)(2,1)S(1)} %get-tuple-element.260.refs_2_.refs_14_), channel_id=1, source_target_pairs={{0,24},{1,25},{2,26},{3,27},{4,28},{5,29},{6,30},{7,31},{8,0},{9,1... | collective-permute-start | bytes 368648 | tf_op jit(solution)/shard_map/ppermute | solution.py:329
  152.1 6.9 %collective-permute-start.56 = (bf16[32,1920]{1,0:T(8,128)(2,1)S(1)}, bf16[32,1920]{1,0:T(8,128)(2,1)S(1)}, u32[]{:S(2)}, u32[]{:S(2)}) collective-permute-start(bf16[32,1920]{1,0:T(8,128)(2,1)S(1)} %collective-permute-done.52.refs_3_), channel_id=1, source_target_pairs={{0,1},{1,0},{2,3},{3,2},{4,5},{5,4},{6,7},{7,6},{8,9},{9,8},{10,11... | collective-permute-start | bytes 368648 | tf_op jit(solution)/shard_map/ppermute | solution.py:329
  161.1 8.1 %collective-permute-start.57 = (bf16[32,1920]{1,0:T(8,128)(2,1)S(1)}, bf16[32,1920]{1,0:T(8,128)(2,1)S(1)}, u32[]{:S(2)}, u32[]{:S(2)}) collective-permute-start(bf16[32,1920]{1,0:T(8,128)(2,1)S(1)} %get-tuple-element.277), channel_id=1, source_target_pairs={{0,6},{1,7},{2,4},{3,5},{4,2},{5,3},{6,0},{7,1},{8,14},{9,15},{10,... | collective-permute-start | bytes 368648 | tf_op jit(solution)/shard_map/ppermute | solution.py:329
  162.1 13.9 %collective-permute-start.59 = (bf16[32,1920]{1,0:T(8,128)(2,1)S(1)}, bf16[32,1920]{1,0:T(8,128)(2,1)S(1)}, u32[]{:S(2)}, u32[]{:S(2)}) collective-permute-start(bf16[32,1920]{1,0:T(8,128)(2,1)S(1)} %get-tuple-element.284), channel_id=1, source_target_pairs={{0,2},{1,3},{2,0},{3,1},{4,6},{5,7},{6,4},{7,5},{8,10},{9,11},{10,... | collective-permute-start | bytes 368648 | tf_op jit(solution)/shard_map/ppermute | solution.py:329
  162.1 13.9 %collective-permute-start.60 = (bf16[32,1920]{1,0:T(8,128)(2,1)S(1)}, bf16[32,1920]{1,0:T(8,128)(2,1)S(1)}, u32[]{:S(2)}, u32[]{:S(2)}) collective-permute-start(bf16[32,1920]{1,0:T(8,128)(2,1)S(1)} %get-tuple-element.285), channel_id=1, source_target_pairs={{0,4},{1,5},{2,6},{3,7},{4,0},{5,1},{6,2},{7,3},{8,12},{9,13},{10,... | collective-permute-start | bytes 368648 | tf_op jit(solution)/shard_map/ppermute | solution.py:329
  171.4 9.9 %collective-permute-start.63 = (bf16[32,1920]{1,0:T(8,128)(2,1)S(1)}, bf16[32,1920]{1,0:T(8,128)(2,1)S(1)}, u32[]{:S(2)}, u32[]{:S(2)}) collective-permute-start(bf16[32,1920]{1,0:T(8,128)(2,1)S(1)} %get-tuple-element.293), channel_id=1, source_target_pairs={{0,30},{1,31},{2,28},{3,29},{4,26},{5,27},{6,24},{7,25},{8,6},{9,7... | collective-permute-start | bytes 368648 | tf_op jit(solution)/shard_map/ppermute | solution.py:329
  173.7 7.7 %collective-permute-start.58 = (bf16[32,1920]{1,0:T(8,128)(2,1)S(1)}, bf16[32,1920]{1,0:T(8,128)(2,1)S(1)}, u32[]{:S(2)}, u32[]{:S(2)}) collective-permute-start(bf16[32,1920]{1,0:T(8,128)(2,1)S(1)} %get-tuple-element.283.refs_12_), channel_id=1, source_target_pairs={{0,24},{1,25},{2,26},{3,27},{4,28},{5,29},{6,30},{7,31},{8,0},{9,1... | collective-permute-start | bytes 368648 | tf_op jit(solution)/shard_map/ppermute | solution.py:329
  178.1 7.4 %collective-permute-start.61 = (bf16[32,1920]{1,0:T(8,128)(2,1)S(1)}, bf16[32,1920]{1,0:T(8,128)(2,1)S(1)}, u32[]{:S(2)}, u32[]{:S(2)}) collective-permute-start(bf16[32,1920]{1,0:T(8,128)(2,1)S(1)} %get-tuple-element.291), channel_id=1, source_target_pairs={{0,26},{1,27},{2,24},{3,25},{4,30},{5,31},{6,28},{7,29},{8,2},{9,3... | collective-permute-start | bytes 368648 | tf_op jit(solution)/shard_map/ppermute | solution.py:329
  179.3 8.0 %collective-permute-start.62 = (bf16[32,1920]{1,0:T(8,128)(2,1)S(1)}, bf16[32,1920]{1,0:T(8,128)(2,1)S(1)}, u32[]{:S(2)}, u32[]{:S(2)}) collective-permute-start(bf16[32,1920]{1,0:T(8,128)(2,1)S(1)} %get-tuple-element.292), channel_id=1, source_target_pairs={{0,28},{1,29},{2,30},{3,31},{4,24},{5,25},{6,26},{7,27},{8,4},{9,5... | collective-permute-start | bytes 368648 | tf_op jit(solution)/shard_map/ppermute | solution.py:329
  181.4 5.9 %collective-permute-start.67 = (bf16[32,1920]{1,0:T(8,128)(2,1)S(1)}, bf16[32,1920]{1,0:T(8,128)(2,1)S(1)}, u32[]{:S(2)}, u32[]{:S(2)}) collective-permute-start(bf16[32,1920]{1,0:T(8,128)(2,1)S(1)} %collective-permute-done.63.refs_3_), channel_id=1, source_target_pairs={{0,1},{1,0},{2,3},{3,2},{4,5},{5,4},{6,7},{7,6},{8,9},{9,8},{10,11... | collective-permute-start | bytes 368648 | tf_op jit(solution)/shard_map/ppermute | solution.py:329
  181.5 5.8 %collective-permute-start.64 = (bf16[32,1920]{1,0:T(8,128)(2,1)S(1)}, bf16[32,1920]{1,0:T(8,128)(2,1)S(1)}, u32[]{:S(2)}, u32[]{:S(2)}) collective-permute-start(bf16[32,1920]{1,0:T(8,128)(2,1)S(1)} %collective-permute-done.58.refs_0_), channel_id=1, source_target_pairs={{0,1},{1,0},{2,3},{3,2},{4,5},{5,4},{6,7},{7,6},{8,9},{9,8},{10,11... | collective-permute-start | bytes 368648 | tf_op jit(solution)/shard_map/ppermute | solution.py:329
  189.5 8.1 %collective-permute-start.68 = (bf16[32,1920]{1,0:T(8,128)(2,1)S(1)}, bf16[32,1920]{1,0:T(8,128)(2,1)S(1)}, u32[]{:S(2)}, u32[]{:S(2)}) collective-permute-start(bf16[32,1920]{1,0:T(8,128)(2,1)S(1)} %get-tuple-element.295), channel_id=1, source_target_pairs={{0,6},{1,7},{2,4},{3,5},{4,2},{5,3},{6,0},{7,1},{8,14},{9,15},{10,... | collective-permute-start | bytes 368648 | tf_op jit(solution)/shard_map/ppermute | solution.py:329
  191.0 14.2 %collective-permute-start.70 = (bf16[32,1920]{1,0:T(8,128)(2,1)S(1)}, bf16[32,1920]{1,0:T(8,128)(2,1)S(1)}, u32[]{:S(2)}, u32[]{:S(2)}) collective-permute-start(bf16[32,1920]{1,0:T(8,128)(2,1)S(1)} %get-tuple-element.336), channel_id=1, source_target_pairs={{0,2},{1,3},{2,0},{3,1},{4,6},{5,7},{6,4},{7,5},{8,10},{9,11},{10,... | collective-permute-start | bytes 368648 | tf_op jit(solution)/shard_map/ppermute | solution.py:329
  192.2 13.0 %collective-permute-start.71 = (bf16[32,1920]{1,0:T(8,128)(2,1)S(1)}, bf16[32,1920]{1,0:T(8,128)(2,1)S(1)}, u32[]{:S(2)}, u32[]{:S(2)}) collective-permute-start(bf16[32,1920]{1,0:T(8,128)(2,1)S(1)} %get-tuple-element.337), channel_id=1, source_target_pairs={{0,4},{1,5},{2,6},{3,7},{4,0},{5,1},{6,2},{7,3},{8,12},{9,13},{10,... | collective-permute-start | bytes 368648 | tf_op jit(solution)/shard_map/ppermute | solution.py:329
  199.7 10.2 %collective-permute-start.74 = (bf16[32,1920]{1,0:T(8,128)(2,1)S(1)}, bf16[32,1920]{1,0:T(8,128)(2,1)S(1)}, u32[]{:S(2)}, u32[]{:S(2)}) collective-permute-start(bf16[32,1920]{1,0:T(8,128)(2,1)S(1)} %get-tuple-element.345), channel_id=1, source_target_pairs={{0,30},{1,31},{2,28},{3,29},{4,26},{5,27},{6,24},{7,25},{8,6},{9,7... | collective-permute-start | bytes 368648 | tf_op jit(solution)/shard_map/ppermute | solution.py:329
  203.9 6.4 %collective-permute-start.69 = (bf16[32,1920]{1,0:T(8,128)(2,1)S(1)}, bf16[32,1920]{1,0:T(8,128)(2,1)S(1)}, u32[]{:S(2)}, u32[]{:S(2)}) collective-permute-start(bf16[32,1920]{1,0:T(8,128)(2,1)S(1)} %get-tuple-element.335.refs_12_), channel_id=1, source_target_pairs={{0,24},{1,25},{2,26},{3,27},{4,28},{5,29},{6,30},{7,31},{8,0},{9,1... | collective-permute-start | bytes 368648 | tf_op jit(solution)/shard_map/ppermute | solution.py:329
  207.4 7.7 %collective-permute-start.72 = (bf16[32,1920]{1,0:T(8,128)(2,1)S(1)}, bf16[32,1920]{1,0:T(8,128)(2,1)S(1)}, u32[]{:S(2)}, u32[]{:S(2)}) collective-permute-start(bf16[32,1920]{1,0:T(8,128)(2,1)S(1)} %get-tuple-element.343), channel_id=1, source_target_pairs={{0,26},{1,27},{2,24},{3,25},{4,30},{5,31},{6,28},{7,29},{8,2},{9,3... | collective-permute-start | bytes 368648 | tf_op jit(solution)/shard_map/ppermute | solution.py:329
  207.5 9.1 %collective-permute-start.73 = (bf16[32,1920]{1,0:T(8,128)(2,1)S(1)}, bf16[32,1920]{1,0:T(8,128)(2,1)S(1)}, u32[]{:S(2)}, u32[]{:S(2)}) collective-permute-start(bf16[32,1920]{1,0:T(8,128)(2,1)S(1)} %get-tuple-element.344), channel_id=1, source_target_pairs={{0,28},{1,29},{2,30},{3,31},{4,24},{5,25},{6,26},{7,27},{8,4},{9,5... | collective-permute-start | bytes 368648 | tf_op jit(solution)/shard_map/ppermute | solution.py:329
  210.0 6.7 %collective-permute-start.78 = (bf16[32,1920]{1,0:T(8,128)(2,1)S(1)}, bf16[32,1920]{1,0:T(8,128)(2,1)S(1)}, u32[]{:S(2)}, u32[]{:S(2)}) collective-permute-start(bf16[32,1920]{1,0:T(8,128)(2,1)S(1)} %collective-permute-done.74.refs_3_), channel_id=1, source_target_pairs={{0,1},{1,0},{2,3},{3,2},{4,5},{5,4},{6,7},{7,6},{8,9},{9,8},{10,11... | collective-permute-start | bytes 368648 | tf_op jit(solution)/shard_map/ppermute | solution.py:329
  210.3 6.3 %collective-permute-start.75 = (bf16[32,1920]{1,0:T(8,128)(2,1)S(1)}, bf16[32,1920]{1,0:T(8,128)(2,1)S(1)}, u32[]{:S(2)}, u32[]{:S(2)}) collective-permute-start(bf16[32,1920]{1,0:T(8,128)(2,1)S(1)} %collective-permute-done.69.refs_0_), channel_id=1, source_target_pairs={{0,1},{1,0},{2,3},{3,2},{4,5},{5,4},{6,7},{7,6},{8,9},{9,8},{10,11... | collective-permute-start | bytes 368648 | tf_op jit(solution)/shard_map/ppermute | solution.py:329
  218.8 11.6 %collective-permute-start.79 = (bf16[32,1920]{1,0:T(8,128)(2,1)S(1)}, bf16[32,1920]{1,0:T(8,128)(2,1)S(1)}, u32[]{:S(2)}, u32[]{:S(2)}) collective-permute-start(bf16[32,1920]{1,0:T(8,128)(2,1)S(1)} %get-tuple-element.347), channel_id=1, source_target_pairs={{0,6},{1,7},{2,4},{3,5},{4,2},{5,3},{6,0},{7,1},{8,14},{9,15},{10,... | collective-permute-start | bytes 368648 | tf_op jit(solution)/shard_map/ppermute | solution.py:329
  220.3 11.2 %collective-permute-start.80 = (bf16[32,1920]{1,0:T(8,128)(2,1)S(1)}, bf16[32,1920]{1,0:T(8,128)(2,1)S(1)}, u32[]{:S(2)}, u32[]{:S(2)}) collective-permute-start(bf16[32,1920]{1,0:T(8,128)(2,1)S(1)} %get-tuple-element.384), channel_id=1, source_target_pairs={{0,2},{1,3},{2,0},{3,1},{4,6},{5,7},{6,4},{7,5},{8,10},{9,11},{10,... | collective-permute-start | bytes 368648 | tf_op jit(solution)/shard_map/ppermute | solution.py:329
  220.3 11.4 %collective-permute-start.81 = (bf16[32,1920]{1,0:T(8,128)(2,1)S(1)}, bf16[32,1920]{1,0:T(8,128)(2,1)S(1)}, u32[]{:S(2)}, u32[]{:S(2)}) collective-permute-start(bf16[32,1920]{1,0:T(8,128)(2,1)S(1)} %get-tuple-element.385), channel_id=1, source_target_pairs={{0,4},{1,5},{2,6},{3,7},{4,0},{5,1},{6,2},{7,3},{8,12},{9,13},{10,... | collective-permute-start | bytes 368648 | tf_op jit(solution)/shard_map/ppermute | solution.py:329
  (22 other events, 64.4 us)

commit v4 on v3

--- a/solution.py
+++ b/solution.py
@@ -175,12 +175,16 @@
 
 
 def resort_kernel(plan, place_ref, order_ref, *refs):
-    arrivals, count, width, entry, last = plan
+    arrivals, count, width, micros, entry, last = plan
     arrived = refs[:arrivals]
     rest = refs[arrivals:]
     sent = rest[-count:]
+    forward_micro = place_ref[2] - place_ref[0]
+    backward_micro = jnp.clip(forward_micro - 2 * (last - place_ref[0]), 0, micros - 1)
+    is_forward = (forward_micro >= 0) & (forward_micro < micros)
+    which = jnp.where(is_forward, forward_micro, micros + backward_micro)
     value = jnp.dot(
-        order_ref[0], joined_rows(arrived, width), preferred_element_type=f32
+        order_ref[which], joined_rows(arrived, width), preferred_element_type=f32
     ).astype(bf16)
     if entry:
         layer = place_ref[0]
@@ -371,27 +375,14 @@
     )(places[0], *both_ids, *both_entering)
 
     def resort(step, arrived):
-        def which(ref):
-            forward_micro = ref[2] - ref[0]
-            backward_micro = jnp.clip(forward_micro - 2 * (last - ref[0]), 0, micros - 1)
-            is_forward = (forward_micro >= 0) & (forward_micro < micros)
-            return jnp.where(is_forward, forward_micro, micros + backward_micro)
-
         entry = step < micros
-        whole = lambda shape: pl.BlockSpec(shape, lambda i, ref: (0,) * len(shape))
         ins = list(arrived) + ([start[step - 1]] if entry else [])
+        plan = (len(arrived), count, width, micros, entry, last)
         return pl.pallas_call(
-            functools.partial(resort_kernel, (len(arrived), count, width, entry, last)),
+            functools.partial(resort_kernel, plan),
             out_shape=[piece] * count,
-            grid_spec=pltpu.PrefetchScalarGridSpec(
-                num_scalar_prefetch=1,
-                grid=(1,),
-                in_specs=[
-                    pl.BlockSpec((1, rows, homes * rows), lambda i, ref: (which(ref), 0, 0))
-                ]
-                + [whole(value.shape) for value in ins],
-                out_specs=[whole((size, short))] * count,
-            ),
+            in_specs=[SMEM] + [VMEM] * (1 + len(ins)),
+            out_specs=[VMEM] * count,
             compiler_params=params,
             name="resort",
         )(places[step], order, *ins)

time: 238 us -> 238 us (level)
  no operation moved by 1% of the time
where the time goes in v4:
time: 238 us; the launch traced here: 237 us
  starting transfers between devices  94.5 us (40%)
  waiting for transfers between devices  78.6 us (33%)
  Pallas kernels  57.3 us (24%)
  local copies, waits for them, and re-layouts  3.8 us (2%)
    ppermute x82, starting transfers between devices, permuted(): return lax.ppermute(block, ('pipe', 'expert'), route)  94.5 us
    ppermute x82, waiting for transfers between devices, permuted(): return lax.ppermute(block, ('pipe', 'expert'), route)  78.6 us
    pallas_call x10, Pallas kernels, backward(): pl.pallas_call(functools.partial(backward_kernel, plan), out_shape=[piece...  19.6 us
    pallas_call x10, Pallas kernels, forward(): pl.pallas_call(functools.partial(forward_kernel, many, len(earlier), pass...  14.9 us
    pallas_call x8, Pallas kernels, record(): pl.pallas_call(functools.partial(record_kernel, (layers, micros, len(sour...  7.1 us
    pallas_call x7, Pallas kernels, resort(): pl.pallas_call(functools.partial(resort_kernel, plan), out_shape=[piece]...  6.07 us
  transfers between devices with their start and end apart: 82, of which 35 were waited for; matrix products, arithmetic and copies ran while one was open for 0% of the time, Pallas kernels for 19%

profile of v4, /device:TPU:0, one launch (start us, length us, event | category | flops | bytes accessed | tf_op | source)
XLA Modules:
  0.0 237.4 jit_solution(6840267937613627329)
XLA Ops:
  2.6 2.2 copy-done
  4.8 1.6 copy-done.2
  6.9 1.6 prepare.1
  8.4 5.1 %collective-permute-start.2 = (bf16[32,1920]{1,0:T(8,128)(2,1)S(1)}, bf16[32,1920]{1,0:T(8,128)(2,1)S(1)}, u32[]{:S(2)}, u32[]{:S(2)}) collective-permute-start(bf16[32,1920]{1,0:T(8,128)(2,1)S(1)} %get-tuple-element.202), channel_id=1, source_target_pairs={{0,6},{1,7},{2,4},{3,5},{4,2},{5,3},{6,0},{7,1},{8,14},{9,15},{10,... | collective-permute-start | bytes 368648 | tf_op jit(solution)/shard_map/ppermute | solution.py:333
  14.9 2.8 %collective-permute-done.2.refs_1_.refs_3_ = bf16[32,1920]{1,0:T(8,128)(2,1)S(1)} collective-permute-done((bf16[32,1920]{1,0:T(8,128)(2,1)S(1)}, bf16[32,1920]{1,0:T(8,128)(2,1)S(1)}, u32[]{:S(2)}, u32[]{:S(2)}) %collective-permute-start.2) | collective-permute-done | bytes 122912 | tf_op jit(solution)/shard_map/ppermute | solution.py:333
  17.7 1.5 forward.10
  19.3 4.8 %collective-permute-start.8 = (bf16[32,1920]{1,0:T(8,128)(2,1)S(1)}, bf16[32,1920]{1,0:T(8,128)(2,1)S(1)}, u32[]{:S(2)}, u32[]{:S(2)}) collective-permute-start(bf16[32,1920]{1,0:T(8,128)(2,1)S(1)} %get-tuple-element.208), channel_id=1, source_target_pairs={{0,14},{1,15},{2,12},{3,13},{4,10},{5,11},{6,8},{7,9},{8,22},{9,23... | collective-permute-start | bytes 368648 | tf_op jit(solution)/shard_map/ppermute | solution.py:333
  25.6 2.1 collective-permute-done.5.refs_1_.refs_3_
  29.2 3.3 %collective-permute-start.7 = (bf16[32,1920]{1,0:T(8,128)(2,1)S(1)}, bf16[32,1920]{1,0:T(8,128)(2,1)S(1)}, u32[]{:S(2)}, u32[]{:S(2)}) collective-permute-start(bf16[32,1920]{1,0:T(8,128)(2,1)S(1)} %get-tuple-element.207), channel_id=1, source_target_pairs={{0,12},{1,13},{2,14},{3,15},{4,8},{5,9},{6,10},{7,11},{8,20},{9,21... | collective-permute-start | bytes 368648 | tf_op jit(solution)/shard_map/ppermute | solution.py:333
  33.1 4.2 %collective-permute-done.6.refs_1_ = bf16[32,1920]{1,0:T(8,128)(2,1)S(1)} collective-permute-done((bf16[32,1920]{1,0:T(8,128)(2,1)S(1)}, bf16[32,1920]{1,0:T(8,128)(2,1)S(1)}, u32[]{:S(2)}, u32[]{:S(2)}) %collective-permute-start.6) | collective-permute-done | bytes 122912 | tf_op jit(solution)/shard_map/ppermute | solution.py:333
  39.6 1.9 collective-permute-start.13
  42.1 1.9 collective-permute-start.16
  44.1 3.7 %collective-permute-done.13.refs_1_.refs_3_ = bf16[32,1920]{1,0:T(8,128)(2,1)S(1)} collective-permute-done((bf16[32,1920]{1,0:T(8,128)(2,1)S(1)}, bf16[32,1920]{1,0:T(8,128)(2,1)S(1)}, u32[]{:S(2)}, u32[]{:S(2)}) %collective-permute-start.13) | collective-permute-done | bytes 122912 | tf_op jit(solution)/shard_map/ppermute | solution.py:333
  50.7 2.0 collective-permute-start.14
  52.7 5.0 %collective-permute-done.16.refs_1_.refs_3_ = bf16[32,1920]{1,0:T(8,128)(2,1)S(1)} collective-permute-done((bf16[32,1920]{1,0:T(8,128)(2,1)S(1)}, bf16[32,1920]{1,0:T(8,128)(2,1)S(1)}, u32[]{:S(2)}, u32[]{:S(2)}) %collective-permute-start.16) | collective-permute-done | bytes 122912 | tf_op jit(solution)/shard_map/ppermute | solution.py:333
  59.2 2.2 collective-permute-start.18
  62.0 4.8 %collective-permute-done.17.refs_1_ = bf16[32,1920]{1,0:T(8,128)(2,1)S(1)} collective-permute-done((bf16[32,1920]{1,0:T(8,128)(2,1)S(1)}, bf16[32,1920]{1,0:T(8,128)(2,1)S(1)}, u32[]{:S(2)}, u32[]{:S(2)}) %collective-permute-start.17) | collective-permute-done | bytes 122912 | tf_op jit(solution)/shard_map/ppermute | solution.py:333
  66.8 2.5 %collective-permute-done.18.refs_2_ = bf16[32,1920]{1,0:T(8,128)(2,1)S(1)} collective-permute-done((bf16[32,1920]{1,0:T(8,128)(2,1)S(1)}, bf16[32,1920]{1,0:T(8,128)(2,1)S(1)}, u32[]{:S(2)}, u32[]{:S(2)}) %collective-permute-start.18) | collective-permute-done | bytes 122912 | tf_op jit(solution)/shard_map/ppermute | solution.py:333
  72.9 3.1 %collective-permute-start.27 = (bf16[32,1920]{1,0:T(8,128)(2,1)S(1)}, bf16[32,1920]{1,0:T(8,128)(2,1)S(1)}, u32[]{:S(2)}, u32[]{:S(2)}) collective-permute-start(bf16[32,1920]{1,0:T(8,128)(2,1)S(1)} %get-tuple-element.222), channel_id=1, source_target_pairs={{0,4},{1,5},{2,6},{3,7},{4,0},{5,1},{6,2},{7,3},{8,12},{9,13},{10,... | collective-permute-start | bytes 368648 | tf_op jit(solution)/shard_map/ppermute | solution.py:333
  76.0 3.7 %collective-permute-done.24.refs_1_ = bf16[32,1920]{1,0:T(8,128)(2,1)S(1)} collective-permute-done((bf16[32,1920]{1,0:T(8,128)(2,1)S(1)}, bf16[32,1920]{1,0:T(8,128)(2,1)S(1)}, u32[]{:S(2)}, u32[]{:S(2)}) %collective-permute-start.24) | collective-permute-done | bytes 122912 | tf_op jit(solution)/shard_map/ppermute | solution.py:333
  81.2 1.8 collective-permute-start.30
  83.0 1.6 collective-permute-start.25
  84.6 1.5 forward.15
  86.2 4.4 %collective-permute-start.29 = (bf16[32,1920]{1,0:T(8,128)(2,1)S(1)}, bf16[32,1920]{1,0:T(8,128)(2,1)S(1)}, u32[]{:S(2)}, u32[]{:S(2)}) collective-permute-start(bf16[32,1920]{1,0:T(8,128)(2,1)S(1)} %get-tuple-element.224), channel_id=1, source_target_pairs={{0,12},{1,13},{2,14},{3,15},{4,8},{5,9},{6,10},{7,11},{8,20},{9,21... | collective-permute-start | bytes 368648 | tf_op jit(solution)/shard_map/ppermute | solution.py:333
  90.6 3.9 %collective-permute-done.25.refs_0_ = bf16[32,1920]{1,0:T(8,128)(2,1)S(1)} collective-permute-done((bf16[32,1920]{1,0:T(8,128)(2,1)S(1)}, bf16[32,1920]{1,0:T(8,128)(2,1)S(1)}, u32[]{:S(2)}, u32[]{:S(2)}) %collective-permute-start.25) | collective-permute-done | bytes 122912 | tf_op jit(solution)/shard_map/ppermute | solution.py:333
  98.6 1.8 collective-permute-start.35
  100.4 2.7 %collective-permute-start.38 = (bf16[32,1920]{1,0:T(8,128)(2,1)S(1)}, bf16[32,1920]{1,0:T(8,128)(2,1)S(1)}, u32[]{:S(2)}, u32[]{:S(2)}) collective-permute-start(bf16[32,1920]{1,0:T(8,128)(2,1)S(1)} %get-tuple-element.237), channel_id=1, source_target_pairs={{0,4},{1,5},{2,6},{3,7},{4,0},{5,1},{6,2},{7,3},{8,12},{9,13},{10,... | collective-permute-start | bytes 368648 | tf_op jit(solution)/shard_map/ppermute | solution.py:333
  103.1 2.9 %turn.1 = (bf16[1024,2048]{1,0:T(8,128)(2,1)S(1)}, bf16[2048,512]{1,0:T(8,128)(2,1)S(1)}) custom-call(bf16[2048,1024]{1,0:T(8,128)(2,1)S(1)} %get-tuple-element.196.in_ref, bf16[512,2048]{1,0:T(8,128)(2,1)S(1)} %get-tuple-element.197.out_ref), custom_call_target="tpu_custom_call" | custom-call | tf_op jit(solution)/shard_map/turn/pallas_call | solution.py:461
  106.7 1.5 forward.16
  108.2 2.2 backward.10
  110.4 1.5 collective-permute-start.41
  112.0 1.7 collective-permute-start.36
  115.2 2.2 backward.11
  118.1 3.0 %collective-permute-start.40 = (bf16[32,1920]{1,0:T(8,128)(2,1)S(1)}, bf16[32,1920]{1,0:T(8,128)(2,1)S(1)}, u32[]{:S(2)}, u32[]{:S(2)}) collective-permute-start(bf16[32,1920]{1,0:T(8,128)(2,1)S(1)} %get-tuple-element.246), channel_id=1, source_target_pairs={{0,12},{1,13},{2,14},{3,15},{4,8},{5,9},{6,10},{7,11},{8,4},{9,5},... | collective-permute-start | bytes 368648 | tf_op jit(solution)/shard_map/ppermute | solution.py:333
  121.6 1.9 collective-permute-done.39.refs_1_
  123.5 2.6 %collective-permute-done.40.refs_2_ = bf16[32,1920]{1,0:T(8,128)(2,1)S(1)} collective-permute-done((bf16[32,1920]{1,0:T(8,128)(2,1)S(1)}, bf16[32,1920]{1,0:T(8,128)(2,1)S(1)}, u32[]{:S(2)}, u32[]{:S(2)}) %collective-permute-start.40) | collective-permute-done | bytes 122912 | tf_op jit(solution)/shard_map/ppermute | solution.py:333
  130.1 2.6 %collective-permute-start.49 = (bf16[32,1920]{1,0:T(8,128)(2,1)S(1)}, bf16[32,1920]{1,0:T(8,128)(2,1)S(1)}, u32[]{:S(2)}, u32[]{:S(2)}) collective-permute-start(bf16[32,1920]{1,0:T(8,128)(2,1)S(1)} %get-tuple-element.262), channel_id=1, source_target_pairs={{0,4},{1,5},{2,6},{3,7},{4,0},{5,1},{6,2},{7,3},{8,12},{9,13},{10,... | collective-permute-start | bytes 368648 | tf_op jit(solution)/shard_map/ppermute | solution.py:333
  132.7 3.7 %collective-permute-done.46.refs_1_ = bf16[32,1920]{1,0:T(8,128)(2,1)S(1)} collective-permute-done((bf16[32,1920]{1,0:T(8,128)(2,1)S(1)}, bf16[32,1920]{1,0:T(8,128)(2,1)S(1)}, u32[]{:S(2)}, u32[]{:S(2)}) %collective-permute-start.46) | collective-permute-done | bytes 122912 | tf_op jit(solution)/shard_map/ppermute | solution.py:333
  137.8 2.2 backward.12
  140.0 4.1 %collective-permute-start.52 = (bf16[32,1920]{1,0:T(8,128)(2,1)S(1)}, bf16[32,1920]{1,0:T(8,128)(2,1)S(1)}, u32[]{:S(2)}, u32[]{:S(2)}) collective-permute-start(bf16[32,1920]{1,0:T(8,128)(2,1)S(1)} %get-tuple-element.275), channel_id=1, source_target_pairs={{0,30},{1,31},{2,28},{3,29},{4,26},{5,27},{6,24},{7,25},{8,6},{9,7... | collective-permute-start | bytes 368648 | tf_op jit(solution)/shard_map/ppermute | solution.py:333
  145.6 2.2 backward.13
  149.1 2.9 %collective-permute-start.51 = (bf16[32,1920]{1,0:T(8,128)(2,1)S(1)}, bf16[32,1920]{1,0:T(8,128)(2,1)S(1)}, u32[]{:S(2)}, u32[]{:S(2)}) collective-permute-start(bf16[32,1920]{1,0:T(8,128)(2,1)S(1)} %get-tuple-element.274), channel_id=1, source_target_pairs={{0,28},{1,29},{2,30},{3,31},{4,24},{5,25},{6,26},{7,27},{8,4},{9,5... | collective-permute-start | bytes 368648 | tf_op jit(solution)/shard_map/ppermute | solution.py:333
  152.0 2.4 collective-permute-done.50.refs_1_
  154.4 2.5 %collective-permute-done.51.refs_2_ = bf16[32,1920]{1,0:T(8,128)(2,1)S(1)} collective-permute-done((bf16[32,1920]{1,0:T(8,128)(2,1)S(1)}, bf16[32,1920]{1,0:T(8,128)(2,1)S(1)}, u32[]{:S(2)}, u32[]{:S(2)}) %collective-permute-start.51) | collective-permute-done | bytes 122912 | tf_op jit(solution)/shard_map/ppermute | solution.py:333
  156.9 2.0 collective-permute-done.47.refs_0_
  162.1 3.5 %collective-permute-start.60 = (bf16[32,1920]{1,0:T(8,128)(2,1)S(1)}, bf16[32,1920]{1,0:T(8,128)(2,1)S(1)}, u32[]{:S(2)}, u32[]{:S(2)}) collective-permute-start(bf16[32,1920]{1,0:T(8,128)(2,1)S(1)} %get-tuple-element.285), channel_id=1, source_target_pairs={{0,4},{1,5},{2,6},{3,7},{4,0},{5,1},{6,2},{7,3},{8,12},{9,13},{10,... | collective-permute-start | bytes 368648 | tf_op jit(solution)/shard_map/ppermute | solution.py:333
  165.6 3.7 %collective-permute-done.57.refs_1_ = bf16[32,1920]{1,0:T(8,128)(2,1)S(1)} collective-permute-done((bf16[32,1920]{1,0:T(8,128)(2,1)S(1)}, bf16[32,1920]{1,0:T(8,128)(2,1)S(1)}, u32[]{:S(2)}, u32[]{:S(2)}) %collective-permute-start.57) | collective-permute-done | bytes 122912 | tf_op jit(solution)/shard_map/ppermute | solution.py:333
  169.3 2.2 backward.14
  171.4 2.3 collective-permute-start.63
  173.7 2.2 collective-permute-start.58
  175.9 2.2 backward.15
  179.3 2.1 collective-permute-start.62
  181.9 3.6 %collective-permute-done.61.refs_1_ = bf16[32,1920]{1,0:T(8,128)(2,1)S(1)} collective-permute-done((bf16[32,1920]{1,0:T(8,128)(2,1)S(1)}, bf16[32,1920]{1,0:T(8,128)(2,1)S(1)}, u32[]{:S(2)}, u32[]{:S(2)}) %collective-permute-start.61) | collective-permute-done | bytes 122912 | tf_op jit(solution)/shard_map/ppermute | solution.py:333
  185.5 1.8 collective-permute-done.62.refs_2_
  189.5 1.5 collective-permute-start.68
  192.2 1.7 collective-permute-start.71
  193.9 3.6 %collective-permute-done.68.refs_1_ = bf16[32,1920]{1,0:T(8,128)(2,1)S(1)} collective-permute-done((bf16[32,1920]{1,0:T(8,128)(2,1)S(1)}, bf16[32,1920]{1,0:T(8,128)(2,1)S(1)}, u32[]{:S(2)}, u32[]{:S(2)}) %collective-permute-start.68) | collective-permute-done | bytes 122912 | tf_op jit(solution)/shard_map/ppermute | solution.py:333
  197.6 2.2 backward.16
  199.7 4.2 %collective-permute-start.74 = (bf16[32,1920]{1,0:T(8,128)(2,1)S(1)}, bf16[32,1920]{1,0:T(8,128)(2,1)S(1)}, u32[]{:S(2)}, u32[]{:S(2)}) collective-permute-start(bf16[32,1920]{1,0:T(8,128)(2,1)S(1)} %get-tuple-element.345), channel_id=1, source_target_pairs={{0,30},{1,31},{2,28},{3,29},{4,26},{5,27},{6,24},{7,25},{8,6},{9,7... | collective-permute-start | bytes 368648 | tf_op jit(solution)/shard_map/ppermute | solution.py:333
  205.3 2.2 backward.17
  207.5 2.4 %collective-permute-start.73 = (bf16[32,1920]{1,0:T(8,128)(2,1)S(1)}, bf16[32,1920]{1,0:T(8,128)(2,1)S(1)}, u32[]{:S(2)}, u32[]{:S(2)}) collective-permute-start(bf16[32,1920]{1,0:T(8,128)(2,1)S(1)} %get-tuple-element.344), channel_id=1, source_target_pairs={{0,28},{1,29},{2,30},{3,31},{4,24},{5,25},{6,26},{7,27},{8,4},{9,5... | collective-permute-start | bytes 368648 | tf_op jit(solution)/shard_map/ppermute | solution.py:333
  210.5 4.7 %collective-permute-done.72.refs_1_ = bf16[32,1920]{1,0:T(8,128)(2,1)S(1)} collective-permute-done((bf16[32,1920]{1,0:T(8,128)(2,1)S(1)}, bf16[32,1920]{1,0:T(8,128)(2,1)S(1)}, u32[]{:S(2)}, u32[]{:S(2)}) %collective-permute-start.72) | collective-permute-done | bytes 122912 | tf_op jit(solution)/shard_map/ppermute | solution.py:333
  220.3 3.0 %collective-permute-start.81 = (bf16[32,1920]{1,0:T(8,128)(2,1)S(1)}, bf16[32,1920]{1,0:T(8,128)(2,1)S(1)}, u32[]{:S(2)}, u32[]{:S(2)}) collective-permute-start(bf16[32,1920]{1,0:T(8,128)(2,1)S(1)} %get-tuple-element.385), channel_id=1, source_target_pairs={{0,4},{1,5},{2,6},{3,7},{4,0},{5,1},{6,2},{7,3},{8,12},{9,13},{10,... | collective-permute-start | bytes 368648 | tf_op jit(solution)/shard_map/ppermute | solution.py:333
  232.8 4.6 %grads.1 = (bf16[2048,1024]{1,0:T(8,128)(2,1)}, bf16[512,2048]{1,0:T(8,128)(2,1)}) custom-call(s32[3]{0:T(128)S(1)} %get-tuple-element.398.place_ref, bf16[3,64,2048]{2,1,0:T(8,128)(2,1)S(1)} %get-tuple-element.331.refs_0_, bf16[3,64,1024]{2,1,0:T(8,128)(2,1)S(1)} %get-tuple-element.332.refs_1_, bf16[3,64,512]{2,1,0:T(8,128)(2,1)S(1)} %get-tuple-element.333.refs_2_, ...), custom_call_target="tpu_custom_call" | custom-call | tf_op jit(solution)/shard_map/grads/pallas_call | solution.py:575
  (151 shorter events, 60.9 us)
Async XLA Ops:
  1.8 5.0 %collective-permute-start.1 = (bf16[2,80,2048]{2,1,0:T(8,128)(2,1)S(1)}, bf16[2,80,2048]{2,1,0:T(8,128)(2,1)S(1)}, u32[]{:S(2)}, u32[]{:S(2)}) collective-permute-start(bf16[2,80,2048]{2,1,0:T(8,128)(2,1)S(1)} %broadcast_select_fusion.refs_2_), channel_id=1, source_target_pairs={{0,1},{1,0},{2,3},{3,2},{4,5},{5,4},{6,7},{7,6},{8,9},{9,8},{10,11... | collective-permute-start | bytes 1966088 | tf_op jit(solution)/shard_map/ppermute | solution.py:333
  8.4 9.3 %collective-permute-start.2 = (bf16[32,1920]{1,0:T(8,128)(2,1)S(1)}, bf16[32,1920]{1,0:T(8,128)(2,1)S(1)}, u32[]{:S(2)}, u32[]{:S(2)}) collective-permute-start(bf16[32,1920]{1,0:T(8,128)(2,1)S(1)} %get-tuple-element.202), channel_id=1, source_target_pairs={{0,6},{1,7},{2,4},{3,5},{4,2},{5,3},{6,0},{7,1},{8,14},{9,15},{10,... | collective-permute-start | bytes 368648 | tf_op jit(solution)/shard_map/ppermute | solution.py:333
  13.5 12.0 %collective-permute-start.4 = (bf16[32,1920]{1,0:T(8,128)(2,1)S(1)}, bf16[32,1920]{1,0:T(8,128)(2,1)S(1)}, u32[]{:S(2)}, u32[]{:S(2)}) collective-permute-start(bf16[32,1920]{1,0:T(8,128)(2,1)S(1)} %get-tuple-element.204), channel_id=1, source_target_pairs={{0,2},{1,3},{2,0},{3,1},{4,6},{5,7},{6,4},{7,5},{8,10},{9,11},{10,... | collective-permute-start | bytes 368648 | tf_op jit(solution)/shard_map/ppermute | solution.py:333
  13.5 14.1 %collective-permute-start.5 = (bf16[32,1920]{1,0:T(8,128)(2,1)S(1)}, bf16[32,1920]{1,0:T(8,128)(2,1)S(1)}, u32[]{:S(2)}, u32[]{:S(2)}) collective-permute-start(bf16[32,1920]{1,0:T(8,128)(2,1)S(1)} %get-tuple-element.205), channel_id=1, source_target_pairs={{0,4},{1,5},{2,6},{3,7},{4,0},{5,1},{6,2},{7,3},{8,12},{9,13},{10,... | collective-permute-start | bytes 368648 | tf_op jit(solution)/shard_map/ppermute | solution.py:333
  19.3 13.3 %collective-permute-start.8 = (bf16[32,1920]{1,0:T(8,128)(2,1)S(1)}, bf16[32,1920]{1,0:T(8,128)(2,1)S(1)}, u32[]{:S(2)}, u32[]{:S(2)}) collective-permute-start(bf16[32,1920]{1,0:T(8,128)(2,1)S(1)} %get-tuple-element.208), channel_id=1, source_target_pairs={{0,14},{1,15},{2,12},{3,13},{4,10},{5,11},{6,8},{7,9},{8,22},{9,23... | collective-permute-start | bytes 368648 | tf_op jit(solution)/shard_map/ppermute | solution.py:333
  24.1 8.5 %collective-permute-start.3 = (bf16[32,1920]{1,0:T(8,128)(2,1)S(1)}, bf16[32,1920]{1,0:T(8,128)(2,1)S(1)}, u32[]{:S(2)}, u32[]{:S(2)}) collective-permute-start(bf16[32,1920]{1,0:T(8,128)(2,1)S(1)} %get-tuple-element.203.refs_2_), channel_id=1, source_target_pairs={{0,8},{1,9},{2,10},{3,11},{4,12},{5,13},{6,14},{7,15},{8,16},{9,17... | collective-permute-start | bytes 368648 | tf_op jit(solution)/shard_map/ppermute | solution.py:333
  29.2 8.0 %collective-permute-start.6 = (bf16[32,1920]{1,0:T(8,128)(2,1)S(1)}, bf16[32,1920]{1,0:T(8,128)(2,1)S(1)}, u32[]{:S(2)}, u32[]{:S(2)}) collective-permute-start(bf16[32,1920]{1,0:T(8,128)(2,1)S(1)} %get-tuple-element.206), channel_id=1, source_target_pairs={{0,10},{1,11},{2,8},{3,9},{4,14},{5,15},{6,12},{7,13},{8,18},{9,19... | collective-permute-start | bytes 368648 | tf_op jit(solution)/shard_map/ppermute | solution.py:333
  29.2 8.0 %collective-permute-start.7 = (bf16[32,1920]{1,0:T(8,128)(2,1)S(1)}, bf16[32,1920]{1,0:T(8,128)(2,1)S(1)}, u32[]{:S(2)}, u32[]{:S(2)}) collective-permute-start(bf16[32,1920]{1,0:T(8,128)(2,1)S(1)} %get-tuple-element.207), channel_id=1, source_target_pairs={{0,12},{1,13},{2,14},{3,15},{4,8},{5,9},{6,10},{7,11},{8,20},{9,21... | collective-permute-start | bytes 368648 | tf_op jit(solution)/shard_map/ppermute | solution.py:333
  32.5 5.2 %collective-permute-start.12 = (bf16[32,1920]{1,0:T(8,128)(2,1)S(1)}, bf16[32,1920]{1,0:T(8,128)(2,1)S(1)}, u32[]{:S(2)}, u32[]{:S(2)}) collective-permute-start(bf16[32,1920]{1,0:T(8,128)(2,1)S(1)} %collective-permute-done.8.refs_3_), channel_id=1, source_target_pairs={{0,1},{1,0},{2,3},{3,2},{4,5},{5,4},{6,7},{7,6},{8,9},{9,8},{10,11... | collective-permute-start | bytes 368648 | tf_op jit(solution)/shard_map/ppermute | solution.py:333
  32.5 5.2 %collective-permute-start.9 = (bf16[32,1920]{1,0:T(8,128)(2,1)S(1)}, bf16[32,1920]{1,0:T(8,128)(2,1)S(1)}, u32[]{:S(2)}, u32[]{:S(2)}) collective-permute-start(bf16[32,1920]{1,0:T(8,128)(2,1)S(1)} %collective-permute-done.3.refs_0_), channel_id=1, source_target_pairs={{0,1},{1,0},{2,3},{3,2},{4,5},{5,4},{6,7},{7,6},{8,9},{9,8},{10,11... | collective-permute-start | bytes 368648 | tf_op jit(solution)/shard_map/ppermute | solution.py:333
  39.6 8.1 %collective-permute-start.13 = (bf16[32,1920]{1,0:T(8,128)(2,1)S(1)}, bf16[32,1920]{1,0:T(8,128)(2,1)S(1)}, u32[]{:S(2)}, u32[]{:S(2)}) collective-permute-start(bf16[32,1920]{1,0:T(8,128)(2,1)S(1)} %get-tuple-element.211), channel_id=1, source_target_pairs={{0,6},{1,7},{2,4},{3,5},{4,2},{5,3},{6,0},{7,1},{8,14},{9,15},{10,... | collective-permute-start | bytes 368648 | tf_op jit(solution)/shard_map/ppermute | solution.py:333
  41.5 11.2 %collective-permute-start.15 = (bf16[32,1920]{1,0:T(8,128)(2,1)S(1)}, bf16[32,1920]{1,0:T(8,128)(2,1)S(1)}, u32[]{:S(2)}, u32[]{:S(2)}) collective-permute-start(bf16[32,1920]{1,0:T(8,128)(2,1)S(1)} %get-tuple-element.213), channel_id=1, source_target_pairs={{0,2},{1,3},{2,0},{3,1},{4,6},{5,7},{6,4},{7,5},{8,10},{9,11},{10,... | collective-permute-start | bytes 368648 | tf_op jit(solution)/shard_map/ppermute | solution.py:333
  42.1 15.5 %collective-permute-start.16 = (bf16[32,1920]{1,0:T(8,128)(2,1)S(1)}, bf16[32,1920]{1,0:T(8,128)(2,1)S(1)}, u32[]{:S(2)}, u32[]{:S(2)}) collective-permute-start(bf16[32,1920]{1,0:T(8,128)(2,1)S(1)} %get-tuple-element.214), channel_id=1, source_target_pairs={{0,4},{1,5},{2,6},{3,7},{4,0},{5,1},{6,2},{7,3},{8,12},{9,13},{10,... | collective-permute-start | bytes 368648 | tf_op jit(solution)/shard_map/ppermute | solution.py:333
  49.2 12.2 %collective-permute-start.19 = (bf16[32,1920]{1,0:T(8,128)(2,1)S(1)}, bf16[32,1920]{1,0:T(8,128)(2,1)S(1)}, u32[]{:S(2)}, u32[]{:S(2)}) collective-permute-start(bf16[32,1920]{1,0:T(8,128)(2,1)S(1)} %get-tuple-element.217), channel_id=1, source_target_pairs={{0,14},{1,15},{2,12},{3,13},{4,10},{5,11},{6,8},{7,9},{8,22},{9,23... | collective-permute-start | bytes 368648 | tf_op jit(solution)/shard_map/ppermute | solution.py:333
  50.7 10.7 %collective-permute-start.14 = (bf16[32,1920]{1,0:T(8,128)(2,1)S(1)}, bf16[32,1920]{1,0:T(8,128)(2,1)S(1)}, u32[]{:S(2)}, u32[]{:S(2)}) collective-permute-start(bf16[32,1920]{1,0:T(8,128)(2,1)S(1)} %get-tuple-element.212.refs_2_), channel_id=1, source_target_pairs={{0,8},{1,9},{2,10},{3,11},{4,12},{5,13},{6,14},{7,15},{8,16},{9,17... | collective-permute-start | bytes 368648 | tf_op jit(solution)/shard_map/ppermute | solution.py:333
  59.2 7.6 %collective-permute-start.17 = (bf16[32,1920]{1,0:T(8,128)(2,1)S(1)}, bf16[32,1920]{1,0:T(8,128)(2,1)S(1)}, u32[]{:S(2)}, u32[]{:S(2)}) collective-permute-start(bf16[32,1920]{1,0:T(8,128)(2,1)S(1)} %get-tuple-element.215), channel_id=1, source_target_pairs={{0,10},{1,11},{2,8},{3,9},{4,14},{5,15},{6,12},{7,13},{8,18},{9,19... | collective-permute-start | bytes 368648 | tf_op jit(solution)/shard_map/ppermute | solution.py:333
  59.2 10.1 %collective-permute-start.18 = (bf16[32,1920]{1,0:T(8,128)(2,1)S(1)}, bf16[32,1920]{1,0:T(8,128)(2,1)S(1)}, u32[]{:S(2)}, u32[]{:S(2)}) collective-permute-start(bf16[32,1920]{1,0:T(8,128)(2,1)S(1)} %get-tuple-element.216), channel_id=1, source_target_pairs={{0,12},{1,13},{2,14},{3,15},{4,8},{5,9},{6,10},{7,11},{8,20},{9,21... | collective-permute-start | bytes 368648 | tf_op jit(solution)/shard_map/ppermute | solution.py:333
  61.5 7.8 %collective-permute-start.23 = (bf16[32,1920]{1,0:T(8,128)(2,1)S(1)}, bf16[32,1920]{1,0:T(8,128)(2,1)S(1)}, u32[]{:S(2)}, u32[]{:S(2)}) collective-permute-start(bf16[32,1920]{1,0:T(8,128)(2,1)S(1)} %collective-permute-done.19.refs_3_), channel_id=1, source_target_pairs={{0,1},{1,0},{2,3},{3,2},{4,5},{5,4},{6,7},{7,6},{8,9},{9,8},{10,11... | collective-permute-start | bytes 368648 | tf_op jit(solution)/shard_map/ppermute | solution.py:333
  61.5 7.8 %collective-permute-start.20 = (bf16[32,1920]{1,0:T(8,128)(2,1)S(1)}, bf16[32,1920]{1,0:T(8,128)(2,1)S(1)}, u32[]{:S(2)}, u32[]{:S(2)}) collective-permute-start(bf16[32,1920]{1,0:T(8,128)(2,1)S(1)} %collective-permute-done.14.refs_0_), channel_id=1, source_target_pairs={{0,1},{1,0},{2,3},{3,2},{4,5},{5,4},{6,7},{7,6},{8,9},{9,8},{10,11... | collective-permute-start | bytes 368648 | tf_op jit(solution)/shard_map/ppermute | solution.py:333
  71.5 8.1 %collective-permute-start.24 = (bf16[32,1920]{1,0:T(8,128)(2,1)S(1)}, bf16[32,1920]{1,0:T(8,128)(2,1)S(1)}, u32[]{:S(2)}, u32[]{:S(2)}) collective-permute-start(bf16[32,1920]{1,0:T(8,128)(2,1)S(1)} %get-tuple-element.219), channel_id=1, source_target_pairs={{0,6},{1,7},{2,4},{3,5},{4,2},{5,3},{6,0},{7,1},{8,14},{9,15},{10,... | collective-permute-start | bytes 368648 | tf_op jit(solution)/shard_map/ppermute | solution.py:333
  72.9 11.7 %collective-permute-start.26 = (bf16[32,1920]{1,0:T(8,128)(2,1)S(1)}, bf16[32,1920]{1,0:T(8,128)(2,1)S(1)}, u32[]{:S(2)}, u32[]{:S(2)}) collective-permute-start(bf16[32,1920]{1,0:T(8,128)(2,1)S(1)} %get-tuple-element.221), channel_id=1, source_target_pairs={{0,2},{1,3},{2,0},{3,1},{4,6},{5,7},{6,4},{7,5},{8,10},{9,11},{10,... | collective-permute-start | bytes 368648 | tf_op jit(solution)/shard_map/ppermute | solution.py:333
  72.9 11.7 %collective-permute-start.27 = (bf16[32,1920]{1,0:T(8,128)(2,1)S(1)}, bf16[32,1920]{1,0:T(8,128)(2,1)S(1)}, u32[]{:S(2)}, u32[]{:S(2)}) collective-permute-start(bf16[32,1920]{1,0:T(8,128)(2,1)S(1)} %get-tuple-element.222), channel_id=1, source_target_pairs={{0,4},{1,5},{2,6},{3,7},{4,0},{5,1},{6,2},{7,3},{8,12},{9,13},{10,... | collective-permute-start | bytes 368648 | tf_op jit(solution)/shard_map/ppermute | solution.py:333
  81.2 9.5 %collective-permute-start.30 = (bf16[32,1920]{1,0:T(8,128)(2,1)S(1)}, bf16[32,1920]{1,0:T(8,128)(2,1)S(1)}, u32[]{:S(2)}, u32[]{:S(2)}) collective-permute-start(bf16[32,1920]{1,0:T(8,128)(2,1)S(1)} %get-tuple-element.225), channel_id=1, source_target_pairs={{0,14},{1,15},{2,12},{3,13},{4,10},{5,11},{6,8},{7,9},{8,22},{9,23... | collective-permute-start | bytes 368648 | tf_op jit(solution)/shard_map/ppermute | solution.py:333
  83.0 11.6 %collective-permute-start.25 = (bf16[32,1920]{1,0:T(8,128)(2,1)S(1)}, bf16[32,1920]{1,0:T(8,128)(2,1)S(1)}, u32[]{:S(2)}, u32[]{:S(2)}) collective-permute-start(bf16[32,1920]{1,0:T(8,128)(2,1)S(1)} %get-tuple-element.220.refs_2_), channel_id=1, source_target_pairs={{0,8},{1,9},{2,10},{3,11},{4,12},{5,13},{6,14},{7,15},{8,16},{9,17... | collective-permute-start | bytes 368648 | tf_op jit(solution)/shard_map/ppermute | solution.py:333
  86.1 8.5 %collective-permute-start.28 = (bf16[32,1920]{1,0:T(8,128)(2,1)S(1)}, bf16[32,1920]{1,0:T(8,128)(2,1)S(1)}, u32[]{:S(2)}, u32[]{:S(2)}) collective-permute-start(bf16[32,1920]{1,0:T(8,128)(2,1)S(1)} %get-tuple-element.223), channel_id=1, source_target_pairs={{0,10},{1,11},{2,8},{3,9},{4,14},{5,15},{6,12},{7,13},{8,18},{9,19... | collective-permute-start | bytes 368648 | tf_op jit(solution)/shard_map/ppermute | solution.py:333
  86.2 10.2 %collective-permute-start.29 = (bf16[32,1920]{1,0:T(8,128)(2,1)S(1)}, bf16[32,1920]{1,0:T(8,128)(2,1)S(1)}, u32[]{:S(2)}, u32[]{:S(2)}) collective-permute-start(bf16[32,1920]{1,0:T(8,128)(2,1)S(1)} %get-tuple-element.224), channel_id=1, source_target_pairs={{0,12},{1,13},{2,14},{3,15},{4,8},{5,9},{6,10},{7,11},{8,20},{9,21... | collective-permute-start | bytes 368648 | tf_op jit(solution)/shard_map/ppermute | solution.py:333
  90.6 5.8 %collective-permute-start.34 = (bf16[32,1920]{1,0:T(8,128)(2,1)S(1)}, bf16[32,1920]{1,0:T(8,128)(2,1)S(1)}, u32[]{:S(2)}, u32[]{:S(2)}) collective-permute-start(bf16[32,1920]{1,0:T(8,128)(2,1)S(1)} %collective-permute-done.30.refs_3_), channel_id=1, source_target_pairs={{0,1},{1,0},{2,3},{3,2},{4,5},{5,4},{6,7},{7,6},{8,9},{9,8},{10,11... | collective-permute-start | bytes 368648 | tf_op jit(solution)/shard_map/ppermute | solution.py:333
  98.6 8.1 %collective-permute-start.35 = (bf16[32,1920]{1,0:T(8,128)(2,1)S(1)}, bf16[32,1920]{1,0:T(8,128)(2,1)S(1)}, u32[]{:S(2)}, u32[]{:S(2)}) collective-permute-start(bf16[32,1920]{1,0:T(8,128)(2,1)S(1)} %get-tuple-element.227), channel_id=1, source_target_pairs={{0,6},{1,7},{2,4},{3,5},{4,2},{5,3},{6,0},{7,1},{8,14},{9,15},{10,... | collective-permute-start | bytes 368648 | tf_op jit(solution)/shard_map/ppermute | solution.py:333
  100.4 13.3 %collective-permute-start.37 = (bf16[32,1920]{1,0:T(8,128)(2,1)S(1)}, bf16[32,1920]{1,0:T(8,128)(2,1)S(1)}, u32[]{:S(2)}, u32[]{:S(2)}) collective-permute-start(bf16[32,1920]{1,0:T(8,128)(2,1)S(1)} %get-tuple-element.236), channel_id=1, source_target_pairs={{0,2},{1,3},{2,0},{3,1},{4,6},{5,7},{6,4},{7,5},{8,10},{9,11},{10,... | collective-permute-start | bytes 368648 | tf_op jit(solution)/shard_map/ppermute | solution.py:333
  100.4 13.3 %collective-permute-start.38 = (bf16[32,1920]{1,0:T(8,128)(2,1)S(1)}, bf16[32,1920]{1,0:T(8,128)(2,1)S(1)}, u32[]{:S(2)}, u32[]{:S(2)}) collective-permute-start(bf16[32,1920]{1,0:T(8,128)(2,1)S(1)} %get-tuple-element.237), channel_id=1, source_target_pairs={{0,4},{1,5},{2,6},{3,7},{4,0},{5,1},{6,2},{7,3},{8,12},{9,13},{10,... | collective-permute-start | bytes 368648 | tf_op jit(solution)/shard_map/ppermute | solution.py:333
  110.4 10.6 %collective-permute-start.41 = (bf16[32,1920]{1,0:T(8,128)(2,1)S(1)}, bf16[32,1920]{1,0:T(8,128)(2,1)S(1)}, u32[]{:S(2)}, u32[]{:S(2)}) collective-permute-start(bf16[32,1920]{1,0:T(8,128)(2,1)S(1)} %get-tuple-element.247), channel_id=1, source_target_pairs={{0,14},{1,15},{2,12},{3,13},{4,10},{5,11},{6,8},{7,9},{8,6},{9,7},... | collective-permute-start | bytes 368648 | tf_op jit(solution)/shard_map/ppermute | solution.py:333
  112.0 9.6 %collective-permute-start.36 = (bf16[32,1920]{1,0:T(8,128)(2,1)S(1)}, bf16[32,1920]{1,0:T(8,128)(2,1)S(1)}, u32[]{:S(2)}, u32[]{:S(2)}) collective-permute-start(bf16[32,1920]{1,0:T(8,128)(2,1)S(1)} %get-tuple-element.235.refs_2_.refs_11_), channel_id=1, source_target_pairs={{0,8},{1,9},{2,10},{3,11},{4,12},{5,13},{6,14},{7,15},{8,0},{9,1},... | collective-permute-start | bytes 368648 | tf_op jit(solution)/shard_map/ppermute | solution.py:333
  117.4 6.1 %collective-permute-start.39 = (bf16[32,1920]{1,0:T(8,128)(2,1)S(1)}, bf16[32,1920]{1,0:T(8,128)(2,1)S(1)}, u32[]{:S(2)}, u32[]{:S(2)}) collective-permute-start(bf16[32,1920]{1,0:T(8,128)(2,1)S(1)} %get-tuple-element.245), channel_id=1, source_target_pairs={{0,10},{1,11},{2,8},{3,9},{4,14},{5,15},{6,12},{7,13},{8,2},{9,3},... | collective-permute-start | bytes 368648 | tf_op jit(solution)/shard_map/ppermute | solution.py:333
  118.1 8.0 %collective-permute-start.40 = (bf16[32,1920]{1,0:T(8,128)(2,1)S(1)}, bf16[32,1920]{1,0:T(8,128)(2,1)S(1)}, u32[]{:S(2)}, u32[]{:S(2)}) collective-permute-start(bf16[32,1920]{1,0:T(8,128)(2,1)S(1)} %get-tuple-element.246), channel_id=1, source_target_pairs={{0,12},{1,13},{2,14},{3,15},{4,8},{5,9},{6,10},{7,11},{8,4},{9,5},... | collective-permute-start | bytes 368648 | tf_op jit(solution)/shard_map/ppermute | solution.py:333
  121.1 5.0 %collective-permute-start.45 = (bf16[32,1920]{1,0:T(8,128)(2,1)S(1)}, bf16[32,1920]{1,0:T(8,128)(2,1)S(1)}, u32[]{:S(2)}, u32[]{:S(2)}) collective-permute-start(bf16[32,1920]{1,0:T(8,128)(2,1)S(1)} %collective-permute-done.41.refs_3_), channel_id=1, source_target_pairs={{0,1},{1,0},{2,3},{3,2},{4,5},{5,4},{6,7},{7,6},{8,9},{9,8},{10,11... | collective-permute-start | bytes 368648 | tf_op jit(solution)/shard_map/ppermute | solution.py:333
  128.3 8.1 %collective-permute-start.46 = (bf16[32,1920]{1,0:T(8,128)(2,1)S(1)}, bf16[32,1920]{1,0:T(8,128)(2,1)S(1)}, u32[]{:S(2)}, u32[]{:S(2)}) collective-permute-start(bf16[32,1920]{1,0:T(8,128)(2,1)S(1)} %get-tuple-element.249), channel_id=1, source_target_pairs={{0,6},{1,7},{2,4},{3,5},{4,2},{5,3},{6,0},{7,1},{8,14},{9,15},{10,... | collective-permute-start | bytes 368648 | tf_op jit(solution)/shard_map/ppermute | solution.py:333
  129.1 15.0 %collective-permute-start.48 = (bf16[32,1920]{1,0:T(8,128)(2,1)S(1)}, bf16[32,1920]{1,0:T(8,128)(2,1)S(1)}, u32[]{:S(2)}, u32[]{:S(2)}) collective-permute-start(bf16[32,1920]{1,0:T(8,128)(2,1)S(1)} %get-tuple-element.261), channel_id=1, source_target_pairs={{0,2},{1,3},{2,0},{3,1},{4,6},{5,7},{6,4},{7,5},{8,10},{9,11},{10,... | collective-permute-start | bytes 368648 | tf_op jit(solution)/shard_map/ppermute | solution.py:333
  130.1 14.1 %collective-permute-start.49 = (bf16[32,1920]{1,0:T(8,128)(2,1)S(1)}, bf16[32,1920]{1,0:T(8,128)(2,1)S(1)}, u32[]{:S(2)}, u32[]{:S(2)}) collective-permute-start(bf16[32,1920]{1,0:T(8,128)(2,1)S(1)} %get-tuple-element.262), channel_id=1, source_target_pairs={{0,4},{1,5},{2,6},{3,7},{4,0},{5,1},{6,2},{7,3},{8,12},{9,13},{10,... | collective-permute-start | bytes 368648 | tf_op jit(solution)/shard_map/ppermute | solution.py:333
  140.0 12.0 %collective-permute-start.52 = (bf16[32,1920]{1,0:T(8,128)(2,1)S(1)}, bf16[32,1920]{1,0:T(8,128)(2,1)S(1)}, u32[]{:S(2)}, u32[]{:S(2)}) collective-permute-start(bf16[32,1920]{1,0:T(8,128)(2,1)S(1)} %get-tuple-element.275), channel_id=1, source_target_pairs={{0,30},{1,31},{2,28},{3,29},{4,26},{5,27},{6,24},{7,25},{8,6},{9,7... | collective-permute-start | bytes 368648 | tf_op jit(solution)/shard_map/ppermute | solution.py:333
  147.8 6.6 %collective-permute-start.50 = (bf16[32,1920]{1,0:T(8,128)(2,1)S(1)}, bf16[32,1920]{1,0:T(8,128)(2,1)S(1)}, u32[]{:S(2)}, u32[]{:S(2)}) collective-permute-start(bf16[32,1920]{1,0:T(8,128)(2,1)S(1)} %get-tuple-element.273), channel_id=1, source_target_pairs={{0,26},{1,27},{2,24},{3,25},{4,30},{5,31},{6,28},{7,29},{8,2},{9,3... | collective-permute-start | bytes 368648 | tf_op jit(solution)/shard_map/ppermute | solution.py:333
  149.1 7.8 %collective-permute-start.51 = (bf16[32,1920]{1,0:T(8,128)(2,1)S(1)}, bf16[32,1920]{1,0:T(8,128)(2,1)S(1)}, u32[]{:S(2)}, u32[]{:S(2)}) collective-permute-start(bf16[32,1920]{1,0:T(8,128)(2,1)S(1)} %get-tuple-element.274), channel_id=1, source_target_pairs={{0,28},{1,29},{2,30},{3,31},{4,24},{5,25},{6,26},{7,27},{8,4},{9,5... | collective-permute-start | bytes 368648 | tf_op jit(solution)/shard_map/ppermute | solution.py:333
  152.0 6.9 %collective-permute-start.47 = (bf16[32,1920]{1,0:T(8,128)(2,1)S(1)}, bf16[32,1920]{1,0:T(8,128)(2,1)S(1)}, u32[]{:S(2)}, u32[]{:S(2)}) collective-permute-start(bf16[32,1920]{1,0:T(8,128)(2,1)S(1)} %get-tuple-element.260.refs_2_.refs_14_), channel_id=1, source_target_pairs={{0,24},{1,25},{2,26},{3,27},{4,28},{5,29},{6,30},{7,31},{8,0},{9,1... | collective-permute-start | bytes 368648 | tf_op jit(solution)/shard_map/ppermute | solution.py:333
  152.0 6.9 %collective-permute-start.56 = (bf16[32,1920]{1,0:T(8,128)(2,1)S(1)}, bf16[32,1920]{1,0:T(8,128)(2,1)S(1)}, u32[]{:S(2)}, u32[]{:S(2)}) collective-permute-start(bf16[32,1920]{1,0:T(8,128)(2,1)S(1)} %collective-permute-done.52.refs_3_), channel_id=1, source_target_pairs={{0,1},{1,0},{2,3},{3,2},{4,5},{5,4},{6,7},{7,6},{8,9},{9,8},{10,11... | collective-permute-start | bytes 368648 | tf_op jit(solution)/shard_map/ppermute | solution.py:333
  161.1 8.1 %collective-permute-start.57 = (bf16[32,1920]{1,0:T(8,128)(2,1)S(1)}, bf16[32,1920]{1,0:T(8,128)(2,1)S(1)}, u32[]{:S(2)}, u32[]{:S(2)}) collective-permute-start(bf16[32,1920]{1,0:T(8,128)(2,1)S(1)} %get-tuple-element.277), channel_id=1, source_target_pairs={{0,6},{1,7},{2,4},{3,5},{4,2},{5,3},{6,0},{7,1},{8,14},{9,15},{10,... | collective-permute-start | bytes 368648 | tf_op jit(solution)/shard_map/ppermute | solution.py:333
  162.1 13.8 %collective-permute-start.59 = (bf16[32,1920]{1,0:T(8,128)(2,1)S(1)}, bf16[32,1920]{1,0:T(8,128)(2,1)S(1)}, u32[]{:S(2)}, u32[]{:S(2)}) collective-permute-start(bf16[32,1920]{1,0:T(8,128)(2,1)S(1)} %get-tuple-element.284), channel_id=1, source_target_pairs={{0,2},{1,3},{2,0},{3,1},{4,6},{5,7},{6,4},{7,5},{8,10},{9,11},{10,... | collective-permute-start | bytes 368648 | tf_op jit(solution)/shard_map/ppermute | solution.py:333
  162.1 13.8 %collective-permute-start.60 = (bf16[32,1920]{1,0:T(8,128)(2,1)S(1)}, bf16[32,1920]{1,0:T(8,128)(2,1)S(1)}, u32[]{:S(2)}, u32[]{:S(2)}) collective-permute-start(bf16[32,1920]{1,0:T(8,128)(2,1)S(1)} %get-tuple-element.285), channel_id=1, source_target_pairs={{0,4},{1,5},{2,6},{3,7},{4,0},{5,1},{6,2},{7,3},{8,12},{9,13},{10,... | collective-permute-start | bytes 368648 | tf_op jit(solution)/shard_map/ppermute | solution.py:333
  171.4 9.9 %collective-permute-start.63 = (bf16[32,1920]{1,0:T(8,128)(2,1)S(1)}, bf16[32,1920]{1,0:T(8,128)(2,1)S(1)}, u32[]{:S(2)}, u32[]{:S(2)}) collective-permute-start(bf16[32,1920]{1,0:T(8,128)(2,1)S(1)} %get-tuple-element.293), channel_id=1, source_target_pairs={{0,30},{1,31},{2,28},{3,29},{4,26},{5,27},{6,24},{7,25},{8,6},{9,7... | collective-permute-start | bytes 368648 | tf_op jit(solution)/shard_map/ppermute | solution.py:333
  173.7 7.8 %collective-permute-start.58 = (bf16[32,1920]{1,0:T(8,128)(2,1)S(1)}, bf16[32,1920]{1,0:T(8,128)(2,1)S(1)}, u32[]{:S(2)}, u32[]{:S(2)}) collective-permute-start(bf16[32,1920]{1,0:T(8,128)(2,1)S(1)} %get-tuple-element.283.refs_12_), channel_id=1, source_target_pairs={{0,24},{1,25},{2,26},{3,27},{4,28},{5,29},{6,30},{7,31},{8,0},{9,1... | collective-permute-start | bytes 368648 | tf_op jit(solution)/shard_map/ppermute | solution.py:333
  178.1 7.4 %collective-permute-start.61 = (bf16[32,1920]{1,0:T(8,128)(2,1)S(1)}, bf16[32,1920]{1,0:T(8,128)(2,1)S(1)}, u32[]{:S(2)}, u32[]{:S(2)}) collective-permute-start(bf16[32,1920]{1,0:T(8,128)(2,1)S(1)} %get-tuple-element.291), channel_id=1, source_target_pairs={{0,26},{1,27},{2,24},{3,25},{4,30},{5,31},{6,28},{7,29},{8,2},{9,3... | collective-permute-start | bytes 368648 | tf_op jit(solution)/shard_map/ppermute | solution.py:333
  179.3 8.0 %collective-permute-start.62 = (bf16[32,1920]{1,0:T(8,128)(2,1)S(1)}, bf16[32,1920]{1,0:T(8,128)(2,1)S(1)}, u32[]{:S(2)}, u32[]{:S(2)}) collective-permute-start(bf16[32,1920]{1,0:T(8,128)(2,1)S(1)} %get-tuple-element.292), channel_id=1, source_target_pairs={{0,28},{1,29},{2,30},{3,31},{4,24},{5,25},{6,26},{7,27},{8,4},{9,5... | collective-permute-start | bytes 368648 | tf_op jit(solution)/shard_map/ppermute | solution.py:333
  181.4 5.9 %collective-permute-start.67 = (bf16[32,1920]{1,0:T(8,128)(2,1)S(1)}, bf16[32,1920]{1,0:T(8,128)(2,1)S(1)}, u32[]{:S(2)}, u32[]{:S(2)}) collective-permute-start(bf16[32,1920]{1,0:T(8,128)(2,1)S(1)} %collective-permute-done.63.refs_3_), channel_id=1, source_target_pairs={{0,1},{1,0},{2,3},{3,2},{4,5},{5,4},{6,7},{7,6},{8,9},{9,8},{10,11... | collective-permute-start | bytes 368648 | tf_op jit(solution)/shard_map/ppermute | solution.py:333
  181.5 5.8 %collective-permute-start.64 = (bf16[32,1920]{1,0:T(8,128)(2,1)S(1)}, bf16[32,1920]{1,0:T(8,128)(2,1)S(1)}, u32[]{:S(2)}, u32[]{:S(2)}) collective-permute-start(bf16[32,1920]{1,0:T(8,128)(2,1)S(1)} %collective-permute-done.58.refs_0_), channel_id=1, source_target_pairs={{0,1},{1,0},{2,3},{3,2},{4,5},{5,4},{6,7},{7,6},{8,9},{9,8},{10,11... | collective-permute-start | bytes 368648 | tf_op jit(solution)/shard_map/ppermute | solution.py:333
  189.5 8.1 %collective-permute-start.68 = (bf16[32,1920]{1,0:T(8,128)(2,1)S(1)}, bf16[32,1920]{1,0:T(8,128)(2,1)S(1)}, u32[]{:S(2)}, u32[]{:S(2)}) collective-permute-start(bf16[32,1920]{1,0:T(8,128)(2,1)S(1)} %get-tuple-element.295), channel_id=1, source_target_pairs={{0,6},{1,7},{2,4},{3,5},{4,2},{5,3},{6,0},{7,1},{8,14},{9,15},{10,... | collective-permute-start | bytes 368648 | tf_op jit(solution)/shard_map/ppermute | solution.py:333
  191.0 14.2 %collective-permute-start.70 = (bf16[32,1920]{1,0:T(8,128)(2,1)S(1)}, bf16[32,1920]{1,0:T(8,128)(2,1)S(1)}, u32[]{:S(2)}, u32[]{:S(2)}) collective-permute-start(bf16[32,1920]{1,0:T(8,128)(2,1)S(1)} %get-tuple-element.336), channel_id=1, source_target_pairs={{0,2},{1,3},{2,0},{3,1},{4,6},{5,7},{6,4},{7,5},{8,10},{9,11},{10,... | collective-permute-start | bytes 368648 | tf_op jit(solution)/shard_map/ppermute | solution.py:333
  192.2 13.0 %collective-permute-start.71 = (bf16[32,1920]{1,0:T(8,128)(2,1)S(1)}, bf16[32,1920]{1,0:T(8,128)(2,1)S(1)}, u32[]{:S(2)}, u32[]{:S(2)}) collective-permute-start(bf16[32,1920]{1,0:T(8,128)(2,1)S(1)} %get-tuple-element.337), channel_id=1, source_target_pairs={{0,4},{1,5},{2,6},{3,7},{4,0},{5,1},{6,2},{7,3},{8,12},{9,13},{10,... | collective-permute-start | bytes 368648 | tf_op jit(solution)/shard_map/ppermute | solution.py:333
  199.7 10.2 %collective-permute-start.74 = (bf16[32,1920]{1,0:T(8,128)(2,1)S(1)}, bf16[32,1920]{1,0:T(8,128)(2,1)S(1)}, u32[]{:S(2)}, u32[]{:S(2)}) collective-permute-start(bf16[32,1920]{1,0:T(8,128)(2,1)S(1)} %get-tuple-element.345), channel_id=1, source_target_pairs={{0,30},{1,31},{2,28},{3,29},{4,26},{5,27},{6,24},{7,25},{8,6},{9,7... | collective-permute-start | bytes 368648 | tf_op jit(solution)/shard_map/ppermute | solution.py:333
  203.9 6.4 %collective-permute-start.69 = (bf16[32,1920]{1,0:T(8,128)(2,1)S(1)}, bf16[32,1920]{1,0:T(8,128)(2,1)S(1)}, u32[]{:S(2)}, u32[]{:S(2)}) collective-permute-start(bf16[32,1920]{1,0:T(8,128)(2,1)S(1)} %get-tuple-element.335.refs_12_), channel_id=1, source_target_pairs={{0,24},{1,25},{2,26},{3,27},{4,28},{5,29},{6,30},{7,31},{8,0},{9,1... | collective-permute-start | bytes 368648 | tf_op jit(solution)/shard_map/ppermute | solution.py:333
  207.4 7.7 %collective-permute-start.72 = (bf16[32,1920]{1,0:T(8,128)(2,1)S(1)}, bf16[32,1920]{1,0:T(8,128)(2,1)S(1)}, u32[]{:S(2)}, u32[]{:S(2)}) collective-permute-start(bf16[32,1920]{1,0:T(8,128)(2,1)S(1)} %get-tuple-element.343), channel_id=1, source_target_pairs={{0,26},{1,27},{2,24},{3,25},{4,30},{5,31},{6,28},{7,29},{8,2},{9,3... | collective-permute-start | bytes 368648 | tf_op jit(solution)/shard_map/ppermute | solution.py:333
  207.5 9.1 %collective-permute-start.73 = (bf16[32,1920]{1,0:T(8,128)(2,1)S(1)}, bf16[32,1920]{1,0:T(8,128)(2,1)S(1)}, u32[]{:S(2)}, u32[]{:S(2)}) collective-permute-start(bf16[32,1920]{1,0:T(8,128)(2,1)S(1)} %get-tuple-element.344), channel_id=1, source_target_pairs={{0,28},{1,29},{2,30},{3,31},{4,24},{5,25},{6,26},{7,27},{8,4},{9,5... | collective-permute-start | bytes 368648 | tf_op jit(solution)/shard_map/ppermute | solution.py:333
  210.0 6.7 %collective-permute-start.78 = (bf16[32,1920]{1,0:T(8,128)(2,1)S(1)}, bf16[32,1920]{1,0:T(8,128)(2,1)S(1)}, u32[]{:S(2)}, u32[]{:S(2)}) collective-permute-start(bf16[32,1920]{1,0:T(8,128)(2,1)S(1)} %collective-permute-done.74.refs_3_), channel_id=1, source_target_pairs={{0,1},{1,0},{2,3},{3,2},{4,5},{5,4},{6,7},{7,6},{8,9},{9,8},{10,11... | collective-permute-start | bytes 368648 | tf_op jit(solution)/shard_map/ppermute | solution.py:333
  210.3 6.3 %collective-permute-start.75 = (bf16[32,1920]{1,0:T(8,128)(2,1)S(1)}, bf16[32,1920]{1,0:T(8,128)(2,1)S(1)}, u32[]{:S(2)}, u32[]{:S(2)}) collective-permute-start(bf16[32,1920]{1,0:T(8,128)(2,1)S(1)} %collective-permute-done.69.refs_0_), channel_id=1, source_target_pairs={{0,1},{1,0},{2,3},{3,2},{4,5},{5,4},{6,7},{7,6},{8,9},{9,8},{10,11... | collective-permute-start | bytes 368648 | tf_op jit(solution)/shard_map/ppermute | solution.py:333
  218.8 11.6 %collective-permute-start.79 = (bf16[32,1920]{1,0:T(8,128)(2,1)S(1)}, bf16[32,1920]{1,0:T(8,128)(2,1)S(1)}, u32[]{:S(2)}, u32[]{:S(2)}) collective-permute-start(bf16[32,1920]{1,0:T(8,128)(2,1)S(1)} %get-tuple-element.347), channel_id=1, source_target_pairs={{0,6},{1,7},{2,4},{3,5},{4,2},{5,3},{6,0},{7,1},{8,14},{9,15},{10,... | collective-permute-start | bytes 368648 | tf_op jit(solution)/shard_map/ppermute | solution.py:333
  220.3 11.3 %collective-permute-start.80 = (bf16[32,1920]{1,0:T(8,128)(2,1)S(1)}, bf16[32,1920]{1,0:T(8,128)(2,1)S(1)}, u32[]{:S(2)}, u32[]{:S(2)}) collective-permute-start(bf16[32,1920]{1,0:T(8,128)(2,1)S(1)} %get-tuple-element.384), channel_id=1, source_target_pairs={{0,2},{1,3},{2,0},{3,1},{4,6},{5,7},{6,4},{7,5},{8,10},{9,11},{10,... | collective-permute-start | bytes 368648 | tf_op jit(solution)/shard_map/ppermute | solution.py:333
  220.3 11.4 %collective-permute-start.81 = (bf16[32,1920]{1,0:T(8,128)(2,1)S(1)}, bf16[32,1920]{1,0:T(8,128)(2,1)S(1)}, u32[]{:S(2)}, u32[]{:S(2)}) collective-permute-start(bf16[32,1920]{1,0:T(8,128)(2,1)S(1)} %get-tuple-element.385), channel_id=1, source_target_pairs={{0,4},{1,5},{2,6},{3,7},{4,0},{5,1},{6,2},{7,3},{8,12},{9,13},{10,... | collective-permute-start | bytes 368648 | tf_op jit(solution)/shard_map/ppermute | solution.py:333
  (22 other events, 64.5 us)
